TPU v7x, 32 devices: a whole 2x2x4 slice. The times are simulated.
32 devices in a mesh: parts: 2 (over y), inner: 4 (over z), outer: 2 (over x), rep: 2 (over core).
Axes of the slice: x: 2, y: 2, z: 4, core: 2. Of those that a mesh axis runs over, the one named last changes fastest.
Arguments:
- tokens: bfloat16 [512, 1024], P(('parts', 'inner', 'outer'), 'rep'), parts along dimension 0, may hold values from -6 to 6
- teacher: bfloat16 [512, 1024], P(('parts', 'inner', 'outer'), 'rep'), parts along dimension 0, may hold values from -1.5 to 1.5
- expert_ids: int32 [512, 8], P(('parts', 'inner', 'outer')), parts along dimension 0, may hold values from 0 to 7, as said below
- gate_codes: int32 [512, 8], P(('parts', 'inner', 'outer')), parts along dimension 0, may hold values from 49152 to 65535
- gate_up_latent: float32 [8, 2, 384, 1024], P(('inner', 'outer'), None, 'rep'), may hold values from -6 to 6
- down_latent: float32 [8, 384, 1024], P(('inner', 'outer'), 'rep'), may hold values from -6 to 6
Outputs:
- student_out: bfloat16 [512, 1024], P(('parts', 'inner', 'outer'), 'rep'), parts along dimension 0
- new_gate_up: float32 [16, 2, 384, 1024], P(('parts', 'inner', 'outer'), None, 'rep'), parts along dimension 0
- new_down: float32 [16, 384, 1024], P(('parts', 'inner', 'outer'), 'rep'), parts along dimension 0
There are 2 independent parts, one for each index of `parts`. A program takes and returns all parts, laid end to end along the dimension named above; an argument that names none is the same for every part. Nothing has to cross between parts.
Inputs may be any that keep to these rules, and one draw needn't show every extreme that they name: `expert_ids`: each token names 8 different experts. Each aligned block of 32 tokens (the tokens of one device) names any expert at most 32 times, and one expert, the same in every block of a part, exactly 32 times in every block.
All inputs are finite; a program needn't handle non-finite values. Where the computation divides by a largest or mean magnitude, that divisor is 1e-20 or more.
Results may differ from a plain program's by a relative error of at most 0.012.
Values may be sent and summed in bfloat16 or wider, within the bound.
No kernel may reach another device: no remote copies, remote signals or barrier semaphores. Data moves between devices by JAX's collectives and lax.ppermute only.
A program may use at most 64 MiB of HBM per device.

v0:
```python
import math

import jax
import jax.numpy as jnp
from jax import lax
from jax.sharding import PartitionSpec as P

D = 1024
HID = 384


learn_rate = 1.0


def soften(latent, fan_in):
    row_scale = jnp.mean(jnp.abs(latent), axis=-1, keepdims=True) + 1e-06
    normed = latent / row_scale
    lower = jnp.tanh(4.0 * (normed - 0.5))
    upper = jnp.tanh(4.0 * (normed + 0.5))
    fan_root = 1.0 / math.sqrt(fan_in)
    weight = (row_scale * 0.5 * (lower + upper) * fan_root).astype(jnp.bfloat16)
    slope = 2.0 * (2.0 - lower * lower - upper * upper) * fan_root
    return (weight, slope)


def dispatch_rows(outbox):
    return lax.all_to_all(outbox, ("inner", "outer"), split_axis=0, concat_axis=0, tiled=True)


def combine_rows(outbox):
    return lax.all_to_all(outbox, ("inner", "outer"), split_axis=0, concat_axis=0, tiled=True)


def upstream_rows(outbox):
    return lax.all_to_all(outbox, ("inner", "outer"), split_axis=0, concat_axis=0, tiled=True)


def on_device(tokens, teacher, expert_ids, gate_codes, gate_up_latent, down_latent):
    experts = lax.axis_size("inner") * lax.axis_size("outer")
    tok_rows, top_count = expert_ids.shape
    part_width = tokens.shape[1]
    capacity = min(tok_rows, 2 * tok_rows * top_count // experts)
    flat_ids = expert_ids.reshape(-1)
    one_hot = (flat_ids[:, None] == jnp.arange(experts, dtype=jnp.int32)[None, :]).astype(jnp.int32)
    before = jnp.cumsum(one_hot, axis=0) - one_hot
    route_slot = jnp.sum(before * one_hot, axis=1)
    target = flat_ids * capacity + route_slot
    payload = jnp.repeat(tokens, top_count, axis=0)
    outbox = jnp.zeros((experts * capacity, part_width), jnp.bfloat16).at[target].set(payload)
    received = dispatch_rows(outbox)
    expert_rows = lax.all_gather(received, "rep", axis=1, tiled=True)
    gu_weight, gu_slope = soften(gate_up_latent[0], D)
    dn_weight, dn_slope = soften(down_latent[0], HID)
    projected = lax.dot_general(
        gu_weight, expert_rows, (((2,), (1,)), ((), ())), preferred_element_type=jnp.float32
    )
    pre_gate = projected[0]
    pre_up = projected[1]
    sigmoid_gate = jax.nn.sigmoid(pre_gate)
    activated = pre_gate * sigmoid_gate
    hidden = (activated * pre_up).astype(jnp.bfloat16)
    partial_out = lax.dot_general(
        hidden, dn_weight, (((0,), (0,)), ((), ())), preferred_element_type=jnp.float32
    )
    expert_out = lax.psum_scatter(
        partial_out.astype(jnp.bfloat16), "rep", scatter_dimension=1, tiled=True
    )
    returned = combine_rows(expert_out)
    picked = returned[target].reshape(tok_rows, top_count, part_width)
    gating = gate_codes.astype(jnp.float32) / 65536.0
    mixed = jnp.sum(gating[:, :, None] * picked.astype(jnp.float32), axis=1)
    student_out = mixed.astype(jnp.bfloat16)
    residual = mixed - teacher.astype(jnp.float32)
    pair_grad = (
        (gating[:, :, None] * residual[:, None, :]).astype(jnp.bfloat16).reshape(-1, part_width)
    )
    grad_outbox = (
        jnp.zeros((experts * capacity, part_width), jnp.bfloat16).at[target].set(pair_grad)
    )
    grad_part = upstream_rows(grad_outbox)
    out_grad = lax.all_gather(grad_part, "rep", axis=1, tiled=True)
    down_grad = jnp.dot(hidden, out_grad, preferred_element_type=jnp.float32)
    hidden_grad = lax.dot_general(
        dn_weight, out_grad, (((1,), (1,)), ((), ())), preferred_element_type=jnp.float32
    )
    gate_grad = (
        hidden_grad * pre_up * sigmoid_gate * (1.0 + pre_gate * (1.0 - sigmoid_gate))
    ).astype(jnp.bfloat16)
    up_grad = (hidden_grad * activated).astype(jnp.bfloat16)
    weight_grads = lax.dot_general(
        jnp.stack([gate_grad, up_grad]),
        expert_rows,
        (((2,), (0,)), ((), ())),
        preferred_element_type=jnp.float32,
    )
    new_gate_up = gate_up_latent - learn_rate * (gu_slope * weight_grads)[None]
    new_down = down_latent - learn_rate * (dn_slope * down_grad)[None]
    return (student_out, new_gate_up, new_down)


def solution(mesh):
    return jax.shard_map(
        on_device,
        mesh=mesh,
        in_specs=(
            P(("parts", "inner", "outer"), "rep"),
            P(("parts", "inner", "outer"), "rep"),
            P(("parts", "inner", "outer"), None),
            P(("parts", "inner", "outer"), None),
            P(("inner", "outer"), None, "rep", None),
            P(("inner", "outer"), "rep", None),
        ),
        out_specs=(
            P(("parts", "inner", "outer"), "rep"),
            P(("parts", "inner", "outer"), None, "rep", None),
            P(("parts", "inner", "outer"), "rep", None),
        ),
        check_vma=False,
    )
```

profile of v0, /device:TPU:0, one launch (start us, length us, event | category | flops | bytes accessed | tf_op | source)
XLA Modules:
  0.0 85.9 jit_solution(5057384777320037804)
XLA Ops:
  7.2 0.0 copy-start
  7.2 0.0 copy-start.2
  7.2 0.8 broadcast_multiply_fusion
  8.0 0.8 copy.12
  8.7 0.1 eq.29
  8.8 0.1 eq.25
  8.9 0.1 copy.11
  9.0 0.1 mul.182
  9.1 0.6 reduce-window.6
  9.7 0.2 slice_reduce_fusion
  9.9 0.1 fusion.36
  10.0 0.0 copy-done
  10.0 2.2 %scatter_custom_fusion = bf16[256,512]{1,0:T(8,128)(2,1)} fusion(s32[256]{0:T(256)S(1)} %bitcast.118, bf16[32,512]{1,0:T(8,128)(2,1)S(1)} %copy-done, bf16[]{:T(256)} %constant.12.clone.1), kind=kCustom, calls=%fused_computation.31 | custom fusion | bytes 294914 | tf_op jit(solution)/shard_map/scatter | solution.py:49
  12.2 7.3 %all-to-all-start = ((bf16[8,32,512]{2,1,0:T(8,128)(2,1)}), bf16[8,32,512]{2,1,0:T(8,128)(2,1)S(1)}, u32[]{:S(2)}, u32[]{:S(2)}) async-start(bf16[8,32,512]{2,1,0:T(8,128)(2,1)} %bitcast.6), calls=%async_computation | async-start | bytes 524288 | tf_op jit(solution)/shard_map/all_to_all | solution.py:27
  19.5 0.0 copy-start.1
  19.5 0.0 reduce-scatter.2.cloned.1.call-start
  19.5 1.7 %fusion = f32[2,192]{1,0:T(2,128)S(1)} fusion(f32[1,2,192,1024]{3,2,1,0:T(8,128)} %param.10), kind=kLoop, calls=%fused_computation.6 | loop fusion | flops 786048 | bytes 1574400 | tf_op jit(solution)/shard_map/reduce_sum | solution.py:16
  21.3 0.0 copy-done.2
  21.3 0.1 fusion.3
  21.4 7.0 %all-to-all-done = bf16[8,32,512]{2,1,0:T(8,128)(2,1)S(1)} async-done(((bf16[8,32,512]{2,1,0:T(8,128)(2,1)}), bf16[8,32,512]{2,1,0:T(8,128)(2,1)S(1)}, u32[]{:S(2)}, u32[]{:S(2)}) %all-to-all-start) | async-done | bytes 262176 | tf_op jit(solution)/shard_map/all_to_all | solution.py:27
  28.4 2.2 %all_gather.6 = bf16[256,1024]{1,0:T(8,128)(2,1)S(1)} all-gather(bf16[256,512]{1,0:T(8,128)(2,1)S(1)} %bitcast.114), channel_id=1, replica_groups=mesh['parts'=2,'inner'=4,'outer'=2,'rep'=2] {'rep'}, dimensions={1}, use_global_device_ids=true | all-gather | bytes 786432 | tf_op jit(solution)/shard_map/all_gather | solution.py:51
  30.6 0.0 copy-done.1
  30.6 0.7 fusion.4
  31.3 0.0 copy-start.5
  31.3 0.7 copy-done.5
  32.1 0.0 copy-start.4
  32.1 1.4 %convolution_convert_fusion = bf16[256,1024]{1,0:T(8,128)(2,1)} fusion(f32[1,192,1024]{2,1,0:T(8,128)S(1)} %copy-done.2, f32[192]{0:T(256)S(1)} %get-tuple-element.10, f32[192]{0:T(256)S(1)} %get-tuple-element.9, f32[2,192,256]{2,1,0:T(8,128)S(1)} %fusion.4), kind=kOutput, calls=%fused_computation.10 | convolution fusion | flops 102989824 | bytes 1705472 | tf_op jit(solution)/shard_map/dot_general | solution.py:62
  33.5 0.0 reduce-scatter.2.cloned.1.call-update
  33.5 7.1 %reduce-scatter.2.cloned.1.call-done = bf16[256,512]{1,0:T(8,128)(2,1)} async-done(((bf16[256,1024]{1,0:T(8,128)(2,1)}), bf16[256,512]{1,0:T(8,128)(2,1)}) %reduce-scatter.2.cloned.1.call-update) | async-done | bytes 262160 | tf_op jit(solution)/shard_map/reduce_scatter | solution.py:65
  40.6 0.0 copy-start.3
  40.6 5.8 %all-to-all-start.1 = ((bf16[8,32,512]{2,1,0:T(8,128)(2,1)}), bf16[8,32,512]{2,1,0:T(8,128)(2,1)S(1)}, u32[]{:S(2)}, u32[]{:S(2)}) async-start(bf16[8,32,512]{2,1,0:T(8,128)(2,1)} %bitcast.117), calls=%async_computation.2 | async-start | bytes 524288 | tf_op jit(solution)/shard_map/all_to_all | solution.py:31
  46.5 0.0 copy-done.4
  46.5 0.1 copy.10
  46.6 0.1 mul.203
  46.7 9.2 %all-to-all-done.1 = bf16[8,32,512]{2,1,0:T(8,128)(2,1)S(1)} async-done(((bf16[8,32,512]{2,1,0:T(8,128)(2,1)}), bf16[8,32,512]{2,1,0:T(8,128)(2,1)S(1)}, u32[]{:S(2)}, u32[]{:S(2)}) %all-to-all-start.1) | async-done | bytes 262176 | tf_op jit(solution)/shard_map/all_to_all | solution.py:31
  55.9 1.2 %gather_fusion = bf16[256,512]{1,0:T(8,128)(2,1)S(1)} fusion(bf16[256,512]{1,0:T(8,128)(2,1)S(1)} %bitcast.113, s32[1024]{0:T(1024)S(1)} %pad_clamp_fusion), kind=kCustom, calls=%fused_computation | custom fusion | bytes 525312 | tf_op jit(solution)/shard_map/gather | solution.py:69
  57.0 0.2 fusion.5
  57.3 0.0 copy-done.3
  57.3 0.6 convert_subtract_fusion
  57.9 1.6 %scatter_custom_fusion.1 = bf16[256,512]{1,0:T(8,128)(2,1)S(1)} fusion(s32[256]{0:T(256)S(1)} %bitcast.120, f32[32,512]{1,0:T(8,128)S(1)} %get-tuple-element.5, f32[256]{0:T(256)S(1)} %mul.203, bf16[]{:T(256)} %constant.12.clone.1), kind=kCustom, calls=%fused_computation.30 | custom fusion | flops 262144 | bytes 328706 | tf_op jit(solution)/shard_map/scatter | solution.py:78
  59.5 12.4 %all_to_all.36 = bf16[8,32,512]{2,1,0:T(8,128)(2,1)S(1)} all-to-all(bf16[8,32,512]{2,1,0:T(8,128)(2,1)S(1)} %bitcast.116), channel_id=1, replica_groups=mesh['parts'=2,'inner'=4,'outer'=2,'rep'=2] {'inner','outer'}, dimensions={0} | all-to-all | bytes 524288 | tf_op jit(solution)/shard_map/all_to_all | solution.py:35
  71.9 2.2 %all_gather.7 = bf16[256,1024]{1,0:T(8,128)(2,1)S(1)} all-gather(bf16[256,512]{1,0:T(8,128)(2,1)S(1)} %bitcast.115), channel_id=1, replica_groups=mesh['parts'=2,'inner'=4,'outer'=2,'rep'=2] {'rep'}, dimensions={1}, use_global_device_ids=true | all-gather | bytes 786432 | tf_op jit(solution)/shard_map/all_gather | solution.py:81
  74.1 0.0 copy-start.6
  74.1 1.6 %fusion.34 = (bf16[1,192,256]{2,1,0:T(8,128)(2,1)S(1)}, bf16[1,192,256]{2,1,0:T(8,128)(2,1)S(1)}) fusion(f32[2,192,256]{2,1,0:T(8,128)} %copy-done.5, bf16[256,1024]{1,0:T(8,128)(2,1)S(1)} %all_gather.7, f32[1,192,1024]{2,1,0:T(8,128)S(1)} %copy-done.2, f32[192]{0:T(256)S(1)} %get-tuple-element.10, f32[192]{0:T(256)S(1)} %get-tuple-element.9), kind=kOutput, calls=%fused_computation.58 | convolution fusion | flops 103071744 | bytes 1902080 | tf_op jit(solution)/shard_map/dot_general | solution.py:83
  75.6 0.0 copy-done.6
  75.6 1.4 %fusion.2 = f32[1,192,1024]{2,1,0:T(8,128)} fusion(f32[1,192,1024]{2,1,0:T(8,128)S(1)} %copy-done.2, bf16[256,1024]{1,0:T(8,128)(2,1)S(1)} %all_gather.7, f32[192]{0:T(256)S(1)} %get-tuple-element.10, f32[2,192,256]{2,1,0:T(8,128)S(1)} %copy-done.6), kind=kOutput, calls=%fused_computation.13 | convolution fusion | flops 103317504 | bytes 2491136 | tf_op jit(solution)/shard_map/dot_general | solution.py:82
  77.0 2.0 %bitcast_subtract_fusion = f32[1,2,192,1024]{3,2,1,0:T(8,128)} fusion(f32[1,2,192,1024]{3,2,1,0:T(8,128)S(1)} %copy-done.1, f32[2,192]{1,0:T(2,128)S(1)} %get-tuple-element.8, bf16[256,1024]{1,0:T(8,128)(2,1)S(1)} %all_gather.6, bf16[1,192,256]{2,1,0:T(8,128)(2,1)S(1)} %get-tuple-element.4, bf16[1,192,256]{2,1,0:T(8,128)(2,1)S(1)} %get-tuple-element.3), kind=kOutput, calls=%fused_computation.3 | convolution fusion | flops 206143488 | bytes 3868160 | tf_op jit(solution)/shard_map/dot_general | solution.py:90
  (8 shorter events, 0.1 us)
Async XLA Ops:
  7.2 2.9 %copy-start = (bf16[32,512]{1,0:T(8,128)(2,1)S(1)}, bf16[32,512]{1,0:T(8,128)(2,1)}, u32[]{:S(2)}) copy-start(bf16[32,512]{1,0:T(8,128)(2,1)} %param.6) | copy-start | bytes 98308
  7.2 14.1 %copy-start.2 = (f32[1,192,1024]{2,1,0:T(8,128)S(1)}, f32[1,192,1024]{2,1,0:T(8,128)}, u32[]{:S(2)}) copy-start(f32[1,192,1024]{2,1,0:T(8,128)} %param.11) | copy-start | bytes 2359300
  12.2 16.2 %all-to-all-start = ((bf16[8,32,512]{2,1,0:T(8,128)(2,1)}), bf16[8,32,512]{2,1,0:T(8,128)(2,1)S(1)}, u32[]{:S(2)}, u32[]{:S(2)}) async-start(bf16[8,32,512]{2,1,0:T(8,128)(2,1)} %bitcast.6), calls=%async_computation | async-start | bytes 524288 | tf_op jit(solution)/shard_map/all_to_all | solution.py:27
  19.5 11.1 %copy-start.1 = (f32[1,2,192,1024]{3,2,1,0:T(8,128)S(1)}, f32[1,2,192,1024]{3,2,1,0:T(8,128)}, u32[]{:S(2)}) copy-start(f32[1,2,192,1024]{3,2,1,0:T(8,128)} %param.10) | copy-start | bytes 4718596
  19.5 21.1 %reduce-scatter.2.cloned.1.call-start = ((), (), s32[]{:S(2)}) async-start(), calls=%async_computation.4 | async-start | bytes 786432 | tf_op jit(solution)/shard_map/reduce_scatter | solution.py:65
  31.3 0.7 copy-start.5
  32.1 14.4 %copy-start.4 = (s32[32,8]{0,1:T(8,128)S(1)}, s32[32,8]{0,1:T(8,128)}, u32[]{:S(2)}) copy-start(s32[32,8]{0,1:T(8,128)} %param.9) | copy-start | bytes 3076
  40.6 16.6 %copy-start.3 = (bf16[32,512]{1,0:T(8,128)(2,1)S(1)}, bf16[32,512]{1,0:T(8,128)(2,1)}, u32[]{:S(2)}) copy-start(bf16[32,512]{1,0:T(8,128)(2,1)} %param.7) | copy-start | bytes 98308
  40.6 15.3 %all-to-all-start.1 = ((bf16[8,32,512]{2,1,0:T(8,128)(2,1)}), bf16[8,32,512]{2,1,0:T(8,128)(2,1)S(1)}, u32[]{:S(2)}, u32[]{:S(2)}) async-start(bf16[8,32,512]{2,1,0:T(8,128)(2,1)} %bitcast.117), calls=%async_computation.2 | async-start | bytes 524288 | tf_op jit(solution)/shard_map/all_to_all | solution.py:31
  74.1 1.6 %copy-start.6 = (f32[2,192,256]{2,1,0:T(8,128)S(1)}, f32[2,192,256]{2,1,0:T(8,128)}, u32[]{:S(2)}) copy-start(f32[2,192,256]{2,1,0:T(8,128)} %copy-done.5) | copy-start | bytes 1179652
Sparse Core Ops, SparseCore 0:
  33.6 6.9 reduce-scatter.1
where the time goes:
time: 86.4 us; the launch traced here: 85.9 us
  waiting for transfers between devices  23.3 us (27%)
  blocking collectives  16.7 us (19%)
  between operations  14.2 us (16%)
  starting transfers between devices  13.2 us (15%)
  matrix products  7.07 us (8%)
  other arithmetic  5.84 us (7%)
  local copies, waits for them, and re-layouts  5.57 us (6%)
    all_to_all x1, blocking collectives, upstream_rows(): lax.all_to_all(outbox, ('inner', 'outer'), split_axis=0, concat_axis=0, t...  12.4 us
    all_to_all x1, waiting for transfers between devices, combine_rows(): lax.all_to_all(outbox, ('inner', 'outer'), split_axis=0, concat_axis=0, t...  9.22 us
    all_to_all x1, starting transfers between devices, dispatch_rows(): lax.all_to_all(outbox, ('inner', 'outer'), split_axis=0, concat_axis=0, t...  7.28 us
    reduce_scatter x1, waiting for transfers between devices, on_device(): lax.psum_scatter(partial_out.astype(jnp.bfloat16), 'rep', scatter_dimensi...  7.13 us
    all_to_all x1, waiting for transfers between devices, dispatch_rows(): lax.all_to_all(outbox, ('inner', 'outer'), split_axis=0, concat_axis=0, t...  6.97 us
    all_to_all x1, starting transfers between devices, combine_rows(): lax.all_to_all(outbox, ('inner', 'outer'), split_axis=0, concat_axis=0, t...  5.85 us
    all_gather x1, blocking collectives, on_device(): expert_rows = lax.all_gather(received, 'rep', axis=1, tiled=True)  2.17 us
    all_gather x1, blocking collectives, on_device(): out_grad = lax.all_gather(grad_part, 'rep', axis=1, tiled=True)  2.17 us
  transfers between devices with their start and end apart: 3, of which 3 were waited for; matrix products, arithmetic and copies ran while one was open for 2% of the time, Pallas kernels for 0%

commit v1 on v0

--- a/solution.py
+++ b/solution.py
@@ -4,10 +4,6 @@
 import jax.numpy as jnp
 from jax import lax
 from jax.sharding import PartitionSpec as P
-
-D = 1024
-HID = 384
-
 
 learn_rate = 1.0
 
@@ -23,20 +19,112 @@
     return (weight, slope)
 
 
-def dispatch_rows(outbox):
+def shift(x, axis, step):
+    size = lax.axis_size(axis)
+    if step % size == 0:
+        return x
+    return lax.ppermute(x, axis, [(i, (i + step) % size) for i in range(size)])
+
+
+def across(x, axis):
+    return [shift(x, axis, k) for k in range(lax.axis_size(axis))]
+
+
+def other_rep(x):
+    return shift(x, "rep", 1)
+
+
+def dense_step(tokens, teacher, expert_ids, gate_codes, gate_up_latent, down_latent):
+    depth = lax.axis_size("inner")
+    width = lax.axis_size("outer")
+    reps = lax.axis_size("rep")
+    experts = depth * width
+    tok_rows, part_width = tokens.shape
+    rep = lax.axis_index("rep")
+    column_rows = depth * tok_rows
+
+    chosen = expert_ids[:, :, None] == jnp.arange(experts, dtype=jnp.int32)[None, None, :]
+    codes = jnp.sum(jnp.where(chosen, gate_codes[:, :, None], 0), axis=1).T
+
+    def column(x, axis):
+        return jnp.concatenate(across(x, "inner"), axis=axis)
+
+    tok_column = column(tokens, 0)
+    code_column = column(codes, 1)
+    tok_rows_all = jnp.concatenate(across(tok_column, "outer"), axis=0)
+    codes_all = jnp.concatenate(across(code_column, "outer"), axis=1)
+
+    def both_features(x):
+        theirs = other_rep(x)
+        pair = jnp.where(rep == 0, jnp.stack([x, theirs]), jnp.stack([theirs, x]))
+        return jnp.concatenate([pair[0], pair[1]], axis=1)
+
+    expert_rows = both_features(tok_rows_all)
+    mine = lax.axis_index("inner") * width + lax.axis_index("outer")
+    gate = lax.dynamic_slice_in_dim(codes_all, mine, 1, 0).astype(jnp.float32) / 65536.0
+
+    gu_weight, gu_slope = soften(gate_up_latent[0], tokens.shape[1] * reps)
+    dn_weight, dn_slope = soften(down_latent[0], down_latent.shape[1] * reps)
+    projected = lax.dot_general(
+        gu_weight, expert_rows, (((2,), (1,)), ((), ())), preferred_element_type=jnp.float32
+    )
+    pre_gate = projected[0]
+    pre_up = projected[1]
+    sigmoid_gate = jax.nn.sigmoid(pre_gate)
+    activated = pre_gate * sigmoid_gate
+    gated_hidden = (activated * pre_up * gate).astype(jnp.bfloat16)
+
+    dn_keep = lax.dynamic_slice_in_dim(dn_weight, rep * part_width, part_width, 1)
+    dn_send = lax.dynamic_slice_in_dim(dn_weight, (1 - rep) * part_width, part_width, 1)
+
+    def down(weight):
+        return lax.dot_general(
+            gated_hidden, weight, (((0,), (0,)), ((), ())), preferred_element_type=jnp.float32
+        )
+
+    theirs = other_rep(down(dn_send).astype(jnp.bfloat16))
+    partial_out = down(dn_keep) + theirs.astype(jnp.float32)
+    partial_out = partial_out.reshape(width, column_rows, part_width)
+    column_sum = partial_out[0]
+    for j in range(1, width):
+        column_sum = column_sum + shift(partial_out[j].astype(jnp.bfloat16), "outer", -j).astype(
+            jnp.float32
+        )
+    column_sum = column_sum.reshape(depth, tok_rows, part_width)
+    mixed = column_sum[0]
+    for k in range(1, depth):
+        mixed = mixed + shift(column_sum[k].astype(jnp.bfloat16), "inner", -k).astype(jnp.float32)
+    student_out = mixed.astype(jnp.bfloat16)
+    residual = (mixed - teacher.astype(jnp.float32)).astype(jnp.bfloat16)
+
+    res_rows = jnp.concatenate(across(column(residual, 0), "outer"), axis=0)
+    upstream = both_features(res_rows)
+    down_grad = jnp.dot(gated_hidden, upstream, preferred_element_type=jnp.float32)
+    hidden_grad = gate * lax.dot_general(
+        dn_weight, upstream, (((1,), (1,)), ((), ())), preferred_element_type=jnp.float32
+    )
+    gate_grad = (
+        hidden_grad * pre_up * sigmoid_gate * (1.0 + pre_gate * (1.0 - sigmoid_gate))
+    ).astype(jnp.bfloat16)
+    up_grad = (hidden_grad * activated).astype(jnp.bfloat16)
+    weight_grads = lax.dot_general(
+        jnp.stack([gate_grad, up_grad]),
+        expert_rows,
+        (((2,), (0,)), ((), ())),
+        preferred_element_type=jnp.float32,
+    )
+    new_gate_up = gate_up_latent - learn_rate * (gu_slope * weight_grads)[None]
+    new_down = down_latent - learn_rate * (dn_slope * down_grad)[None]
+    return (student_out, new_gate_up, new_down)
+
+
+def exchange(outbox):
     return lax.all_to_all(outbox, ("inner", "outer"), split_axis=0, concat_axis=0, tiled=True)
 
 
-def combine_rows(outbox):
-    return lax.all_to_all(outbox, ("inner", "outer"), split_axis=0, concat_axis=0, tiled=True)
-
-
-def upstream_rows(outbox):
-    return lax.all_to_all(outbox, ("inner", "outer"), split_axis=0, concat_axis=0, tiled=True)
-
-
-def on_device(tokens, teacher, expert_ids, gate_codes, gate_up_latent, down_latent):
+def routed_step(tokens, teacher, expert_ids, gate_codes, gate_up_latent, down_latent):
     experts = lax.axis_size("inner") * lax.axis_size("outer")
+    reps = lax.axis_size("rep")
     tok_rows, top_count = expert_ids.shape
     part_width = tokens.shape[1]
     capacity = min(tok_rows, 2 * tok_rows * top_count // experts)
@@ -47,10 +135,10 @@
     target = flat_ids * capacity + route_slot
     payload = jnp.repeat(tokens, top_count, axis=0)
     outbox = jnp.zeros((experts * capacity, part_width), jnp.bfloat16).at[target].set(payload)
-    received = dispatch_rows(outbox)
+    received = exchange(outbox)
     expert_rows = lax.all_gather(received, "rep", axis=1, tiled=True)
-    gu_weight, gu_slope = soften(gate_up_latent[0], D)
-    dn_weight, dn_slope = soften(down_latent[0], HID)
+    gu_weight, gu_slope = soften(gate_up_latent[0], part_width * reps)
+    dn_weight, dn_slope = soften(down_latent[0], down_latent.shape[1] * reps)
     projected = lax.dot_general(
         gu_weight, expert_rows, (((2,), (1,)), ((), ())), preferred_element_type=jnp.float32
     )
@@ -61,11 +149,14 @@
     hidden = (activated * pre_up).astype(jnp.bfloat16)
     partial_out = lax.dot_general(
         hidden, dn_weight, (((0,), (0,)), ((), ())), preferred_element_type=jnp.float32
-    )
-    expert_out = lax.psum_scatter(
-        partial_out.astype(jnp.bfloat16), "rep", scatter_dimension=1, tiled=True
-    )
-    returned = combine_rows(expert_out)
+    ).astype(jnp.bfloat16)
+    rep = lax.axis_index("rep")
+    keep = lax.dynamic_slice_in_dim(partial_out, rep * part_width, part_width, 1)
+    send = lax.dynamic_slice_in_dim(partial_out, (1 - rep) * part_width, part_width, 1)
+    expert_out = (keep.astype(jnp.float32) + other_rep(send).astype(jnp.float32)).astype(
+        jnp.bfloat16
+    )
+    returned = exchange(expert_out)
     picked = returned[target].reshape(tok_rows, top_count, part_width)
     gating = gate_codes.astype(jnp.float32) / 65536.0
     mixed = jnp.sum(gating[:, :, None] * picked.astype(jnp.float32), axis=1)
@@ -77,7 +168,7 @@
     grad_outbox = (
         jnp.zeros((experts * capacity, part_width), jnp.bfloat16).at[target].set(pair_grad)
     )
-    grad_part = upstream_rows(grad_outbox)
+    grad_part = exchange(grad_outbox)
     out_grad = lax.all_gather(grad_part, "rep", axis=1, tiled=True)
     down_grad = jnp.dot(hidden, out_grad, preferred_element_type=jnp.float32)
     hidden_grad = lax.dot_general(
@@ -96,6 +187,12 @@
     new_gate_up = gate_up_latent - learn_rate * (gu_slope * weight_grads)[None]
     new_down = down_latent - learn_rate * (dn_slope * down_grad)[None]
     return (student_out, new_gate_up, new_down)
+
+
+def on_device(tokens, teacher, expert_ids, gate_codes, gate_up_latent, down_latent):
+    experts = lax.axis_size("inner") * lax.axis_size("outer")
+    step = dense_step if expert_ids.shape[1] == experts else routed_step
+    return step(tokens, teacher, expert_ids, gate_codes, gate_up_latent, down_latent)
 
 
 def solution(mesh):

time: 86.4 us -> 59.7 us (0.69)
  blocking collectives: 16.7 us -> 0 us
  between operations: 14.2 us -> 0.93 us
  starting transfers between devices: 13.2 us -> 26.3 us
  local copies, waits for them, and re-layouts: 5.57 us -> 0.27 us
  other arithmetic: 5.84 us -> 3.85 us
  matrix products: 7.07 us -> 5.92 us
  waiting for transfers between devices: 23.3 us -> 22.2 us
    ppermute x0 -> x19, starting transfers between devices: none -> 26.3 us  [shift(): return lax.ppermute(x, axis, [(i, (i + step) % size) for i in range(size)])]
    ppermute x0 -> x19, waiting for transfers between devices: none -> 22.2 us  [shift(): return lax.ppermute(x, axis, [(i, (i + step) % size) for i in range(size)])]
    all_to_all x2 -> x0, waiting for transfers between devices: 16.2 us -> none  [the longest x1 9.22 us: combine_rows(): lax.all_to_all(outbox, ('inner', 'outer'), split_axis=0, concat_axis=0, t...]
    all_to_all x2 -> x0, starting transfers between devices: 13.1 us -> none  [the longest x1 7.28 us: dispatch_rows(): lax.all_to_all(outbox, ('inner', 'outer'), split_axis=0, concat_axis=0, t...]
    all_to_all x1 -> x0, blocking collectives: 12.4 us -> none  [upstream_rows(): lax.all_to_all(outbox, ('inner', 'outer'), split_axis=0, concat_axis=0, t...]
    reduce_scatter x1 -> x0, waiting for transfers between devices: 7.13 us -> none  [on_device(): lax.psum_scatter(partial_out.astype(jnp.bfloat16), 'rep', scatter_dimensi...]
    all_gather x2 -> x0, blocking collectives: 4.34 us -> none  [the longest x1 2.17 us: on_device(): expert_rows = lax.all_gather(received, 'rep', axis=1, tiled=True)]
    scatter x1 -> x0, local copies, waits for them, and re-layouts: 2.16 us -> none  [on_device(): jnp.zeros((experts * capacity, part_width), jnp.bfloat16).at[target]]
  transfers between devices with their start and end apart: 3 -> 19, of which waited for: 3 -> 13; matrix products, arithmetic and copies ran while one was open for 2% -> 6% of each run, Pallas kernels for 0% -> 0%
where the time goes in v1:
time: 59.7 us; the launch traced here: 59.5 us
  starting transfers between devices  26.3 us (44%)
  waiting for transfers between devices  22.2 us (37%)
  matrix products  5.92 us (10%)
  other arithmetic  3.85 us (6%)
  between operations  0.93 us (2%)
    ppermute x19, starting transfers between devices, shift(): return lax.ppermute(x, axis, [(i, (i + step) % size) for i in range(size)])  26.3 us
    ppermute x19, waiting for transfers between devices, shift(): return lax.ppermute(x, axis, [(i, (i + step) % size) for i in range(size)])  22.2 us
    dot_general x1, matrix products, dense_step(): lax.dot_general(jnp.stack([gate_grad, up_grad]), expert_rows, (((2,), (0,...  2.01 us
    reduce_sum x2, other arithmetic, soften(): row_scale = jnp.mean(jnp.abs(latent), axis=-1, keepdims=True) + 1e-06  1.75 us
    dot_general x2, matrix products, down(): lax.dot_general(gated_hidden, weight, (((0,), (0,)), ((), ())), preferred...  1.45 us
    dot_general x1, matrix products, dense_step(): jnp.dot(gated_hidden, upstream, preferred_element_type=jnp.float32)  1.39 us
  transfers between devices with their start and end apart: 19, of which 13 were waited for; matrix products, arithmetic and copies ran while one was open for 6% of the time, Pallas kernels for 0%

profile of v1, /device:TPU:0, one launch (start us, length us, event | category | flops | bytes accessed | tf_op | source)
XLA Modules:
  0.0 59.5 jit_solution(15557909416153520052)
XLA Ops:
  0.6 0.0 copy-start
  0.6 3.1 %collective-permute-start = (bf16[32,512]{1,0:T(8,128)(2,1)}, bf16[32,512]{1,0:T(8,128)(2,1)S(1)}, u32[]{:S(2)}, u32[]{:S(2)}) collective-permute-start(bf16[32,512]{1,0:T(8,128)(2,1)} %param.6), channel_id=1, source_target_pairs={{0,4},{4,8},{8,12},{12,0},{1,5},{5,9},{9,13},{13,1},{2,6},{6,10},{... | collective-permute-start | bytes 98312 | tf_op jit(solution)/shard_map/ppermute | solution.py:26
  3.7 2.6 %collective-permute-start.1 = (bf16[32,512]{1,0:T(8,128)(2,1)}, bf16[32,512]{1,0:T(8,128)(2,1)S(1)}, u32[]{:S(2)}, u32[]{:S(2)}) collective-permute-start(bf16[32,512]{1,0:T(8,128)(2,1)} %param.6), channel_id=1, source_target_pairs={{0,8},{4,12},{8,0},{12,4},{1,9},{5,13},{9,1},{13,5},{2,10},{6,14},... | collective-permute-start | bytes 98312 | tf_op jit(solution)/shard_map/ppermute | solution.py:26
  6.3 0.7 %select_reduce_fusion = s32[32,8]{0,1:T(8,128)S(1)} fusion(s32[32,8]{0,1:T(8,128)} %param.9, s32[32,8]{0,1:T(8,128)} %param.8), kind=kLoop, calls=%fused_computation.51 | loop fusion | flops 5888 | bytes 3072 | tf_op jit(solution)/shard_map/reduce_sum | solution.py:47
  7.1 0.0 copy-start.6
  7.1 0.1 collective-permute-start.5
  7.2 1.8 %collective-permute-start.6 = (s32[8,32]{1,0:T(8,128)S(1)}, s32[8,32]{1,0:T(8,128)S(1)}, u32[]{:S(2)}, u32[]{:S(2)}) collective-permute-start(s32[8,32]{1,0:T(8,128)S(1)} %bitcast.76), channel_id=1, source_target_pairs={{0,8},{4,12},{8,0},{12,4},{1,9},{5,13},{9,1},{13,5},{2,10},{6,14},... | collective-permute-start | bytes 3080 | tf_op jit(solution)/shard_map/ppermute | solution.py:26
  9.0 1.9 %collective-permute-start.7 = (s32[8,32]{1,0:T(8,128)S(1)}, s32[8,32]{1,0:T(8,128)S(1)}, u32[]{:S(2)}, u32[]{:S(2)}) collective-permute-start(s32[8,32]{1,0:T(8,128)S(1)} %bitcast.77), channel_id=1, source_target_pairs={{0,12},{4,0},{8,4},{12,8},{1,13},{5,1},{9,5},{13,9},{2,14},{6,2},{... | collective-permute-start | bytes 3080 | tf_op jit(solution)/shard_map/ppermute | solution.py:26
  10.9 1.6 %fusion = f32[2,192]{1,0:T(2,128)S(1)} fusion(f32[1,2,192,1024]{3,2,1,0:T(8,128)} %param.10), kind=kLoop, calls=%fused_computation.3 | loop fusion | flops 786048 | bytes 1574400 | tf_op jit(solution)/shard_map/reduce_sum | solution.py:12
  12.6 0.1 fusion.3
  12.7 0.4 multiply_convert_fusion.1
  13.1 0.0 copy-done.6
  13.1 0.0 copy-start.1
  13.1 0.0 collective-permute-done.5
  13.1 0.7 %collective-permute-start.2 = (bf16[32,512]{1,0:T(8,128)(2,1)S(1)}, bf16[32,512]{1,0:T(8,128)(2,1)S(1)}, u32[]{:S(2)}, u32[]{:S(2)}) collective-permute-start(bf16[32,512]{1,0:T(8,128)(2,1)S(1)} %copy-done.6), channel_id=1, source_target_pairs={{0,12},{4,0},{8,4},{12,8},{1,13},{5,1},{9,5},{13,9},{2,14},{6,2},{... | collective-permute-start | bytes 98312 | tf_op jit(solution)/shard_map/ppermute | solution.py:26
  13.8 0.0 collective-permute-done.6
  13.8 0.0 collective-permute-done.7
  13.8 0.1 pad_add_fusion
  13.9 1.6 %collective-permute-start.8 = (s32[8,128]{1,0:T(8,128)S(1)}, s32[8,128]{1,0:T(8,128)S(1)}, u32[]{:S(2)}, u32[]{:S(2)}) collective-permute-start(s32[8,128]{1,0:T(8,128)S(1)} %pad_add_fusion), channel_id=1, source_target_pairs={{0,2},{2,0},{1,3},{3,1},{4,6},{6,4},{5,7},{7,5},{8,10},{10,8},{9,1... | collective-permute-start | bytes 12296 | tf_op jit(solution)/shard_map/ppermute | solution.py:26
  15.5 0.0 collective-permute-done
  15.5 0.0 collective-permute-done.1
  15.5 1.5 %collective-permute-done.2 = bf16[32,512]{1,0:T(8,128)(2,1)S(1)} collective-permute-done((bf16[32,512]{1,0:T(8,128)(2,1)S(1)}, bf16[32,512]{1,0:T(8,128)(2,1)S(1)}, u32[]{:S(2)}, u32[]{:S(2)}) %collective-permute-start.2) | collective-permute-done | bytes 32800 | tf_op jit(solution)/shard_map/ppermute | solution.py:26
  17.1 1.6 %collective-permute-start.3 = (bf16[128,512]{1,0:T(8,128)(2,1)S(1)}, bf16[128,512]{1,0:T(8,128)(2,1)S(1)}, u32[]{:S(2)}, u32[]{:S(2)}) collective-permute-start(bf16[128,512]{1,0:T(8,128)(2,1)S(1)} %pad_maximum_fusion.3), channel_id=1, source_target_pairs={{0,2},{2,0},{1,3},{3,1},{4,6},{6,4},{5,7},{7,5},{8,10},{10,8},{9,1... | collective-permute-start | bytes 393224 | tf_op jit(solution)/shard_map/ppermute | solution.py:26
  18.7 3.5 %collective-permute-done.3 = bf16[128,512]{1,0:T(8,128)(2,1)S(1)} collective-permute-done((bf16[128,512]{1,0:T(8,128)(2,1)S(1)}, bf16[128,512]{1,0:T(8,128)(2,1)S(1)}, u32[]{:S(2)}, u32[]{:S(2)}) %collective-permute-start.3) | collective-permute-done | bytes 131104 | tf_op jit(solution)/shard_map/ppermute | solution.py:26
  22.1 0.1 collective-permute-start.4
  22.2 0.0 collective-permute-done.8
  22.3 0.1 concatenate.31
  22.3 1.4 %collective-permute-done.4 = bf16[256,512]{1,0:T(8,128)(2,1)S(1)} collective-permute-done((bf16[256,512]{1,0:T(8,128)(2,1)S(1)}, bf16[256,512]{1,0:T(8,128)(2,1)S(1)}, u32[]{:S(2)}, u32[]{:S(2)}) %collective-permute-start.4) | collective-permute-done | bytes 262176 | tf_op jit(solution)/shard_map/ppermute | solution.py:26
  23.7 0.1 maximum_select_fusion
  23.9 0.0 copy-start.4
  23.9 0.7 %fusion.4 = f32[2,192,256]{2,1,0:T(8,128)S(1)} fusion(f32[1,2,192,1024]{3,2,1,0:T(8,128)S(1)} %copy-done.1, f32[2,192]{1,0:T(2,128)S(1)} %get-tuple-element.17, f32[2,192]{1,0:T(2,128)S(1)} %get-tuple-element.16, bf16[256,512]{1,0:T(8,128)(2,1)S(1)} %get-tuple-element.12, bf16[256,512]{1,0:T(8,128)(2,1)S(1)} %get-tuple-element.11), kind=kOutput, calls=%fused_computation.18 | convolution fusion | flops 205914112 | bytes 2493440 | tf_op jit(solution)/shard_map/dot_general | solution.py:68
  24.7 0.0 copy-done.4
  24.7 0.1 multiply_convert_fusion.5
  24.7 0.0 copy-start.7
  24.8 0.2 convolution_convert_fusion
  25.0 0.2 collective-permute-start.9
  25.2 1.5 %collective-permute-done.9 = bf16[256,512]{1,0:T(8,128)(2,1)} collective-permute-done((bf16[256,512]{1,0:T(8,128)(2,1)S(1)}, bf16[256,512]{1,0:T(8,128)(2,1)}, u32[]{:S(2)}, u32[]{:S(2)}) %collective-permute-start.9) | collective-permute-done | bytes 262176 | tf_op jit(solution)/shard_map/ppermute | solution.py:26
  26.7 1.2 %convert_add_fusion = f32[256,512]{1,0:T(8,128)S(1)} fusion(bf16[256,512]{1,0:T(8,128)(2,1)} %collective-permute-done.9, bf16[192,256]{1,0:T(8,128)(2,1)S(1)} %multiply_convert_fusion.5, bf16[192,1024]{1,0:T(8,128)(2,1)S(1)} %multiply_convert_fusion.1, s32[]{:T(128)S(6)} %select_n.29), kind=kOutput, calls=%fused_computation.23 | convolution fusion | flops 50593792 | bytes 1081348 | tf_op jit(solution)/shard_map/dot_general | solution.py:81
  28.0 1.6 %collective-permute-start.10 = (bf16[128,512]{1,0:T(8,128)(2,1)S(1)}, bf16[128,512]{1,0:T(8,128)(2,1)S(1)}, u32[]{:S(2)}, u32[]{:S(2)}) collective-permute-start(bf16[128,512]{1,0:T(8,128)(2,1)S(1)} %slice.103), channel_id=1, source_target_pairs={{0,2},{2,0},{1,3},{3,1},{4,6},{6,4},{5,7},{7,5},{8,10},{10,8},{9,1... | collective-permute-start | bytes 393224 | tf_op jit(solution)/shard_map/ppermute | solution.py:26
  29.5 4.1 %collective-permute-done.10 = bf16[128,512]{1,0:T(8,128)(2,1)S(1)} collective-permute-done((bf16[128,512]{1,0:T(8,128)(2,1)S(1)}, bf16[128,512]{1,0:T(8,128)(2,1)S(1)}, u32[]{:S(2)}, u32[]{:S(2)}) %collective-permute-start.10) | collective-permute-done | bytes 131104 | tf_op jit(solution)/shard_map/ppermute | solution.py:26
  33.6 0.6 %collective-permute-start.13 = (bf16[32,512]{1,0:T(8,128)(2,1)S(1)}, bf16[32,512]{1,0:T(8,128)(2,1)S(1)}, u32[]{:S(2)}, u32[]{:S(2)}) collective-permute-start(bf16[32,512]{1,0:T(8,128)(2,1)S(1)} %get-tuple-element.14), channel_id=1, source_target_pairs={{0,4},{4,8},{8,12},{12,0},{1,5},{5,9},{9,13},{13,1},{2,6},{6,10},{... | collective-permute-start | bytes 98312 | tf_op jit(solution)/shard_map/ppermute | solution.py:26
  34.3 2.4 %collective-permute-start.12 = (bf16[32,512]{1,0:T(8,128)(2,1)S(1)}, bf16[32,512]{1,0:T(8,128)(2,1)S(1)}, u32[]{:S(2)}, u32[]{:S(2)}) collective-permute-start(bf16[32,512]{1,0:T(8,128)(2,1)S(1)} %get-tuple-element.15), channel_id=1, source_target_pairs={{0,8},{4,12},{8,0},{12,4},{1,9},{5,13},{9,1},{13,5},{2,10},{6,14},... | collective-permute-start | bytes 98312 | tf_op jit(solution)/shard_map/ppermute | solution.py:26
  36.7 1.9 %collective-permute-start.11 = (bf16[32,512]{1,0:T(8,128)(2,1)S(1)}, bf16[32,512]{1,0:T(8,128)(2,1)S(1)}, u32[]{:S(2)}, u32[]{:S(2)}) collective-permute-start(bf16[32,512]{1,0:T(8,128)(2,1)S(1)} %get-tuple-element.13), channel_id=1, source_target_pairs={{0,12},{4,0},{8,4},{12,8},{1,13},{5,1},{9,5},{13,9},{2,14},{6,2},{... | collective-permute-start | bytes 98312 | tf_op jit(solution)/shard_map/ppermute | solution.py:26
  38.6 0.9 %collective-permute-done.13 = bf16[32,512]{1,0:T(8,128)(2,1)S(1)} collective-permute-done((bf16[32,512]{1,0:T(8,128)(2,1)S(1)}, bf16[32,512]{1,0:T(8,128)(2,1)S(1)}, u32[]{:S(2)}, u32[]{:S(2)}) %collective-permute-start.13) | collective-permute-done | bytes 32800 | tf_op jit(solution)/shard_map/ppermute | solution.py:26
  39.5 0.2 collective-permute-done.12
  39.7 0.9 %collective-permute-done.11 = bf16[32,512]{1,0:T(8,128)(2,1)S(1)} collective-permute-done((bf16[32,512]{1,0:T(8,128)(2,1)S(1)}, bf16[32,512]{1,0:T(8,128)(2,1)S(1)}, u32[]{:S(2)}, u32[]{:S(2)}) %collective-permute-start.11) | collective-permute-done | bytes 32800 | tf_op jit(solution)/shard_map/ppermute | solution.py:26
  40.6 0.0 copy-done.7
  40.6 1.4 %collective-permute-start.14 = (bf16[32,512]{1,0:T(8,128)(2,1)S(1)}, bf16[32,512]{1,0:T(8,128)(2,1)S(1)}, u32[]{:S(2)}, u32[]{:S(2)}) collective-permute-start(bf16[32,512]{1,0:T(8,128)(2,1)S(1)} %get-tuple-element.4), channel_id=1, source_target_pairs={{0,4},{4,8},{8,12},{12,0},{1,5},{5,9},{9,13},{13,1},{2,6},{6,10},{... | collective-permute-start | bytes 98312 | tf_op jit(solution)/shard_map/ppermute | solution.py:26
  42.1 2.9 %collective-permute-start.15 = (bf16[32,512]{1,0:T(8,128)(2,1)S(1)}, bf16[32,512]{1,0:T(8,128)(2,1)S(1)}, u32[]{:S(2)}, u32[]{:S(2)}) collective-permute-start(bf16[32,512]{1,0:T(8,128)(2,1)S(1)} %get-tuple-element.4), channel_id=1, source_target_pairs={{0,8},{4,12},{8,0},{12,4},{1,9},{5,13},{9,1},{13,5},{2,10},{6,14},... | collective-permute-start | bytes 98312 | tf_op jit(solution)/shard_map/ppermute | solution.py:26
  45.0 0.0 collective-permute-start.16
  45.0 1.4 %collective-permute-done.14 = bf16[32,512]{1,0:T(8,128)(2,1)S(1)} collective-permute-done((bf16[32,512]{1,0:T(8,128)(2,1)S(1)}, bf16[32,512]{1,0:T(8,128)(2,1)S(1)}, u32[]{:S(2)}, u32[]{:S(2)}) %collective-permute-start.14) | collective-permute-done | bytes 32800 | tf_op jit(solution)/shard_map/ppermute | solution.py:26
  46.4 0.7 %collective-permute-done.15 = bf16[32,512]{1,0:T(8,128)(2,1)S(1)} collective-permute-done((bf16[32,512]{1,0:T(8,128)(2,1)S(1)}, bf16[32,512]{1,0:T(8,128)(2,1)S(1)}, u32[]{:S(2)}, u32[]{:S(2)}) %collective-permute-start.15) | collective-permute-done | bytes 32800 | tf_op jit(solution)/shard_map/ppermute | solution.py:26
  47.1 1.8 %collective-permute-done.16 = bf16[32,512]{1,0:T(8,128)(2,1)S(1)} collective-permute-done((bf16[32,512]{1,0:T(8,128)(2,1)S(1)}, bf16[32,512]{1,0:T(8,128)(2,1)S(1)}, u32[]{:S(2)}, u32[]{:S(2)}) %collective-permute-start.16) | collective-permute-done | bytes 32800 | tf_op jit(solution)/shard_map/ppermute | solution.py:26
  48.9 1.6 %collective-permute-start.17 = (bf16[128,512]{1,0:T(8,128)(2,1)S(1)}, bf16[128,512]{1,0:T(8,128)(2,1)S(1)}, u32[]{:S(2)}, u32[]{:S(2)}) collective-permute-start(bf16[128,512]{1,0:T(8,128)(2,1)S(1)} %pad_maximum_fusion.4), channel_id=1, source_target_pairs={{0,2},{2,0},{1,3},{3,1},{4,6},{6,4},{5,7},{7,5},{8,10},{10,8},{9,1... | collective-permute-start | bytes 393224 | tf_op jit(solution)/shard_map/ppermute | solution.py:26
  50.5 3.5 %collective-permute-done.17 = bf16[128,512]{1,0:T(8,128)(2,1)S(1)} collective-permute-done((bf16[128,512]{1,0:T(8,128)(2,1)S(1)}, bf16[128,512]{1,0:T(8,128)(2,1)S(1)}, u32[]{:S(2)}, u32[]{:S(2)}) %collective-permute-start.17) | collective-permute-done | bytes 131104 | tf_op jit(solution)/shard_map/ppermute | solution.py:26
  54.0 0.1 collective-permute-start.18
  54.0 0.6 %fusion.18 = bf16[32,512]{1,0:T(8,128)(2,1)} fusion(bf16[32,512]{1,0:T(8,128)(2,1)S(1)} %collective-permute-done.13, bf16[32,512]{1,0:T(8,128)(2,1)S(1)} %collective-permute-done.12, bf16[32,512]{1,0:T(8,128)(2,1)S(1)} %collective-permute-done.11, f32[128,512]{1,0:T(8,128)S(1)} %get-tuple-element.6), kind=kLoop, calls=%fused_computation.68 | loop fusion | flops 114688 | bytes 196608 | tf_op jit(solution)/shard_map/convert_element_type | solution.py:97
  54.7 0.9 %collective-permute-done.18 = bf16[256,512]{1,0:T(8,128)(2,1)S(1)} collective-permute-done((bf16[256,512]{1,0:T(8,128)(2,1)S(1)}, bf16[256,512]{1,0:T(8,128)(2,1)S(1)}, u32[]{:S(2)}, u32[]{:S(2)}) %collective-permute-start.18) | collective-permute-done | bytes 262176 | tf_op jit(solution)/shard_map/ppermute | solution.py:26
  55.6 0.1 maximum_select_fusion.1
  55.7 0.3 fusion.15
  56.1 0.0 copy-start.5
  56.1 1.4 %fusion.2 = f32[1,192,1024]{2,1,0:T(8,128)} fusion(f32[1,192,1024]{2,1,0:T(8,128)S(1)} %copy-done, bf16[192,256]{1,0:T(8,128)(2,1)S(1)} %multiply_convert_fusion.5, f32[192]{0:T(256)S(1)} %get-tuple-element.19, bf16[256,512]{1,0:T(8,128)(2,1)S(1)} %get-tuple-element.10, bf16[256,512]{1,0:T(8,128)(2,1)S(1)} %get-tuple-element.9), kind=kOutput, calls=%fused_computation.9 | convolution fusion | flops 104071168 | bytes 2196224 | tf_op jit(solution)/shard_map/dot_general | solution.py:102
  57.5 0.0 copy-done.3
  57.5 2.0 %bitcast_subtract_fusion = f32[1,2,192,1024]{3,2,1,0:T(8,128)} fusion(f32[1,2,192,1024]{3,2,1,0:T(8,128)S(1)} %copy-done.1, f32[2,192]{1,0:T(2,128)S(1)} %get-tuple-element.17, bf16[256,512]{1,0:T(8,128)(2,1)S(1)} %copy-done.5, bf16[256,512]{1,0:T(8,128)(2,1)S(1)} %copy-done.3, bf16[1,192,256]{2,1,0:T(8,128)(2,1)S(1)} %get-tuple-element.8, ...), kind=kOutput, calls=%fused_computation | convolution fusion | flops 207192064 | bytes 3868160 | tf_op jit(solution)/shard_map/dot_general | solution.py:110
  (26 shorter events, 0.3 us)
Async XLA Ops:
  0.6 11.9 %copy-start = (f32[1,192,1024]{2,1,0:T(8,128)S(1)}, f32[1,192,1024]{2,1,0:T(8,128)}, u32[]{:S(2)}) copy-start(f32[1,192,1024]{2,1,0:T(8,128)} %param.11) | copy-start | bytes 2359300
  0.6 14.9 %collective-permute-start = (bf16[32,512]{1,0:T(8,128)(2,1)}, bf16[32,512]{1,0:T(8,128)(2,1)S(1)}, u32[]{:S(2)}, u32[]{:S(2)}) collective-permute-start(bf16[32,512]{1,0:T(8,128)(2,1)} %param.6), channel_id=1, source_target_pairs={{0,4},{4,8},{8,12},{12,0},{1,5},{5,9},{9,13},{13,1},{2,6},{6,10},{... | collective-permute-start | bytes 98312 | tf_op jit(solution)/shard_map/ppermute | solution.py:26
  3.7 11.8 %collective-permute-start.1 = (bf16[32,512]{1,0:T(8,128)(2,1)}, bf16[32,512]{1,0:T(8,128)(2,1)S(1)}, u32[]{:S(2)}, u32[]{:S(2)}) collective-permute-start(bf16[32,512]{1,0:T(8,128)(2,1)} %param.6), channel_id=1, source_target_pairs={{0,8},{4,12},{8,0},{12,4},{1,9},{5,13},{9,1},{13,5},{2,10},{6,14},... | collective-permute-start | bytes 98312 | tf_op jit(solution)/shard_map/ppermute | solution.py:26
  7.1 6.0 %copy-start.6 = (bf16[32,512]{1,0:T(8,128)(2,1)S(1)}, bf16[32,512]{1,0:T(8,128)(2,1)}, u32[]{:S(2)}) copy-start(bf16[32,512]{1,0:T(8,128)(2,1)} %param.6) | copy-start | bytes 98308
  7.1 6.0 %collective-permute-start.5 = (s32[8,32]{1,0:T(8,128)S(1)}, s32[8,32]{1,0:T(8,128)S(1)}, u32[]{:S(2)}, u32[]{:S(2)}) collective-permute-start(s32[8,32]{1,0:T(8,128)S(1)} %bitcast.75), channel_id=1, source_target_pairs={{0,4},{4,8},{8,12},{12,0},{1,5},{5,9},{9,13},{13,1},{2,6},{6,10},{... | collective-permute-start | bytes 3080 | tf_op jit(solution)/shard_map/ppermute | solution.py:26
  7.2 6.6 %collective-permute-start.6 = (s32[8,32]{1,0:T(8,128)S(1)}, s32[8,32]{1,0:T(8,128)S(1)}, u32[]{:S(2)}, u32[]{:S(2)}) collective-permute-start(s32[8,32]{1,0:T(8,128)S(1)} %bitcast.76), channel_id=1, source_target_pairs={{0,8},{4,12},{8,0},{12,4},{1,9},{5,13},{9,1},{13,5},{2,10},{6,14},... | collective-permute-start | bytes 3080 | tf_op jit(solution)/shard_map/ppermute | solution.py:26
  9.0 4.8 %collective-permute-start.7 = (s32[8,32]{1,0:T(8,128)S(1)}, s32[8,32]{1,0:T(8,128)S(1)}, u32[]{:S(2)}, u32[]{:S(2)}) collective-permute-start(s32[8,32]{1,0:T(8,128)S(1)} %bitcast.77), channel_id=1, source_target_pairs={{0,12},{4,0},{8,4},{12,8},{1,13},{5,1},{9,5},{13,9},{2,14},{6,2},{... | collective-permute-start | bytes 3080 | tf_op jit(solution)/shard_map/ppermute | solution.py:26
  13.1 10.8 %copy-start.1 = (f32[1,2,192,1024]{3,2,1,0:T(8,128)S(1)}, f32[1,2,192,1024]{3,2,1,0:T(8,128)}, u32[]{:S(2)}) copy-start(f32[1,2,192,1024]{3,2,1,0:T(8,128)} %param.10) | copy-start | bytes 4718596
  13.1 4.0 %collective-permute-start.2 = (bf16[32,512]{1,0:T(8,128)(2,1)S(1)}, bf16[32,512]{1,0:T(8,128)(2,1)S(1)}, u32[]{:S(2)}, u32[]{:S(2)}) collective-permute-start(bf16[32,512]{1,0:T(8,128)(2,1)S(1)} %copy-done.6), channel_id=1, source_target_pairs={{0,12},{4,0},{8,4},{12,8},{1,13},{5,1},{9,5},{13,9},{2,14},{6,2},{... | collective-permute-start | bytes 98312 | tf_op jit(solution)/shard_map/ppermute | solution.py:26
  13.9 8.4 %collective-permute-start.8 = (s32[8,128]{1,0:T(8,128)S(1)}, s32[8,128]{1,0:T(8,128)S(1)}, u32[]{:S(2)}, u32[]{:S(2)}) collective-permute-start(s32[8,128]{1,0:T(8,128)S(1)} %pad_add_fusion), channel_id=1, source_target_pairs={{0,2},{2,0},{1,3},{3,1},{4,6},{6,4},{5,7},{7,5},{8,10},{10,8},{9,1... | collective-permute-start | bytes 12296 | tf_op jit(solution)/shard_map/ppermute | solution.py:26
  17.1 5.0 %collective-permute-start.3 = (bf16[128,512]{1,0:T(8,128)(2,1)S(1)}, bf16[128,512]{1,0:T(8,128)(2,1)S(1)}, u32[]{:S(2)}, u32[]{:S(2)}) collective-permute-start(bf16[128,512]{1,0:T(8,128)(2,1)S(1)} %pad_maximum_fusion.3), channel_id=1, source_target_pairs={{0,2},{2,0},{1,3},{3,1},{4,6},{6,4},{5,7},{7,5},{8,10},{10,8},{9,1... | collective-permute-start | bytes 393224 | tf_op jit(solution)/shard_map/ppermute | solution.py:26
  22.1 1.6 %collective-permute-start.4 = (bf16[256,512]{1,0:T(8,128)(2,1)S(1)}, bf16[256,512]{1,0:T(8,128)(2,1)S(1)}, u32[]{:S(2)}, u32[]{:S(2)}) collective-permute-start(bf16[256,512]{1,0:T(8,128)(2,1)S(1)} %constant_dynamic-update-slice_fusion), channel_id=1, source_target_pairs={{0,1},{1,0},{2,3},{3,2},{4,5},{5,4},{6,7},{7,6},{8,9},{9,8},{10,11... | collective-permute-start | bytes 786440 | tf_op jit(solution)/shard_map/ppermute | solution.py:26
  23.9 0.8 %copy-start.2 = (bf16[256,512]{1,0:T(8,128)(2,1)}, bf16[256,512]{1,0:T(8,128)(2,1)S(1)}, u32[]{:S(2)}) copy-start(bf16[256,512]{1,0:T(8,128)(2,1)S(1)} %get-tuple-element.11) | copy-start | bytes 786436
  23.9 0.8 %copy-start.4 = (bf16[256,512]{1,0:T(8,128)(2,1)}, bf16[256,512]{1,0:T(8,128)(2,1)S(1)}, u32[]{:S(2)}) copy-start(bf16[256,512]{1,0:T(8,128)(2,1)S(1)} %get-tuple-element.12) | copy-start | bytes 786436
  24.7 15.9 %copy-start.7 = (bf16[32,512]{1,0:T(8,128)(2,1)S(1)}, bf16[32,512]{1,0:T(8,128)(2,1)}, u32[]{:S(2)}) copy-start(bf16[32,512]{1,0:T(8,128)(2,1)} %param.7) | copy-start | bytes 98308
  25.0 1.7 %collective-permute-start.9 = (bf16[256,512]{1,0:T(8,128)(2,1)S(1)}, bf16[256,512]{1,0:T(8,128)(2,1)}, u32[]{:S(2)}, u32[]{:S(2)}) collective-permute-start(bf16[256,512]{1,0:T(8,128)(2,1)S(1)} %convolution_convert_fusion), channel_id=1, source_target_pairs={{0,1},{1,0},{2,3},{3,2},{4,5},{5,4},{6,7},{7,6},{8,9},{9,8},{10,11... | collective-permute-start | bytes 786440 | tf_op jit(solution)/shard_map/ppermute | solution.py:26
  28.0 5.6 %collective-permute-start.10 = (bf16[128,512]{1,0:T(8,128)(2,1)S(1)}, bf16[128,512]{1,0:T(8,128)(2,1)S(1)}, u32[]{:S(2)}, u32[]{:S(2)}) collective-permute-start(bf16[128,512]{1,0:T(8,128)(2,1)S(1)} %slice.103), channel_id=1, source_target_pairs={{0,2},{2,0},{1,3},{3,1},{4,6},{6,4},{5,7},{7,5},{8,10},{10,8},{9,1... | collective-permute-start | bytes 393224 | tf_op jit(solution)/shard_map/ppermute | solution.py:26
  33.6 5.9 %collective-permute-start.13 = (bf16[32,512]{1,0:T(8,128)(2,1)S(1)}, bf16[32,512]{1,0:T(8,128)(2,1)S(1)}, u32[]{:S(2)}, u32[]{:S(2)}) collective-permute-start(bf16[32,512]{1,0:T(8,128)(2,1)S(1)} %get-tuple-element.14), channel_id=1, source_target_pairs={{0,4},{4,8},{8,12},{12,0},{1,5},{5,9},{9,13},{13,1},{2,6},{6,10},{... | collective-permute-start | bytes 98312 | tf_op jit(solution)/shard_map/ppermute | solution.py:26
  34.3 5.4 %collective-permute-start.12 = (bf16[32,512]{1,0:T(8,128)(2,1)S(1)}, bf16[32,512]{1,0:T(8,128)(2,1)S(1)}, u32[]{:S(2)}, u32[]{:S(2)}) collective-permute-start(bf16[32,512]{1,0:T(8,128)(2,1)S(1)} %get-tuple-element.15), channel_id=1, source_target_pairs={{0,8},{4,12},{8,0},{12,4},{1,9},{5,13},{9,1},{13,5},{2,10},{6,14},... | collective-permute-start | bytes 98312 | tf_op jit(solution)/shard_map/ppermute | solution.py:26
  36.7 3.9 %collective-permute-start.11 = (bf16[32,512]{1,0:T(8,128)(2,1)S(1)}, bf16[32,512]{1,0:T(8,128)(2,1)S(1)}, u32[]{:S(2)}, u32[]{:S(2)}) collective-permute-start(bf16[32,512]{1,0:T(8,128)(2,1)S(1)} %get-tuple-element.13), channel_id=1, source_target_pairs={{0,12},{4,0},{8,4},{12,8},{1,13},{5,1},{9,5},{13,9},{2,14},{6,2},{... | collective-permute-start | bytes 98312 | tf_op jit(solution)/shard_map/ppermute | solution.py:26
  40.6 5.8 %collective-permute-start.14 = (bf16[32,512]{1,0:T(8,128)(2,1)S(1)}, bf16[32,512]{1,0:T(8,128)(2,1)S(1)}, u32[]{:S(2)}, u32[]{:S(2)}) collective-permute-start(bf16[32,512]{1,0:T(8,128)(2,1)S(1)} %get-tuple-element.4), channel_id=1, source_target_pairs={{0,4},{4,8},{8,12},{12,0},{1,5},{5,9},{9,13},{13,1},{2,6},{6,10},{... | collective-permute-start | bytes 98312 | tf_op jit(solution)/shard_map/ppermute | solution.py:26
  42.1 5.0 %collective-permute-start.15 = (bf16[32,512]{1,0:T(8,128)(2,1)S(1)}, bf16[32,512]{1,0:T(8,128)(2,1)S(1)}, u32[]{:S(2)}, u32[]{:S(2)}) collective-permute-start(bf16[32,512]{1,0:T(8,128)(2,1)S(1)} %get-tuple-element.4), channel_id=1, source_target_pairs={{0,8},{4,12},{8,0},{12,4},{1,9},{5,13},{9,1},{13,5},{2,10},{6,14},... | collective-permute-start | bytes 98312 | tf_op jit(solution)/shard_map/ppermute | solution.py:26
  45.0 3.9 %collective-permute-start.16 = (bf16[32,512]{1,0:T(8,128)(2,1)S(1)}, bf16[32,512]{1,0:T(8,128)(2,1)S(1)}, u32[]{:S(2)}, u32[]{:S(2)}) collective-permute-start(bf16[32,512]{1,0:T(8,128)(2,1)S(1)} %get-tuple-element.4), channel_id=1, source_target_pairs={{0,12},{4,0},{8,4},{12,8},{1,13},{5,1},{9,5},{13,9},{2,14},{6,2},{... | collective-permute-start | bytes 98312 | tf_op jit(solution)/shard_map/ppermute | solution.py:26
  48.9 5.0 %collective-permute-start.17 = (bf16[128,512]{1,0:T(8,128)(2,1)S(1)}, bf16[128,512]{1,0:T(8,128)(2,1)S(1)}, u32[]{:S(2)}, u32[]{:S(2)}) collective-permute-start(bf16[128,512]{1,0:T(8,128)(2,1)S(1)} %pad_maximum_fusion.4), channel_id=1, source_target_pairs={{0,2},{2,0},{1,3},{3,1},{4,6},{6,4},{5,7},{7,5},{8,10},{10,8},{9,1... | collective-permute-start | bytes 393224 | tf_op jit(solution)/shard_map/ppermute | solution.py:26
  54.0 1.6 %collective-permute-start.18 = (bf16[256,512]{1,0:T(8,128)(2,1)S(1)}, bf16[256,512]{1,0:T(8,128)(2,1)S(1)}, u32[]{:S(2)}, u32[]{:S(2)}) collective-permute-start(bf16[256,512]{1,0:T(8,128)(2,1)S(1)} %constant_dynamic-update-slice_fusion.5), channel_id=1, source_target_pairs={{0,1},{1,0},{2,3},{3,2},{4,5},{5,4},{6,7},{7,6},{8,9},{9,8},{10,11... | collective-permute-start | bytes 786440 | tf_op jit(solution)/shard_map/ppermute | solution.py:26
  56.0 1.4 %copy-start.3 = (bf16[256,512]{1,0:T(8,128)(2,1)S(1)}, bf16[256,512]{1,0:T(8,128)(2,1)}, u32[]{:S(2)}) copy-start(bf16[256,512]{1,0:T(8,128)(2,1)} %copy-done.2) | copy-start | bytes 786436
  56.1 1.4 %copy-start.5 = (bf16[256,512]{1,0:T(8,128)(2,1)S(1)}, bf16[256,512]{1,0:T(8,128)(2,1)}, u32[]{:S(2)}) copy-start(bf16[256,512]{1,0:T(8,128)(2,1)} %copy-done.4) | copy-start | bytes 786436

commit v2 on v1

--- a/solution.py
+++ b/solution.py
@@ -34,92 +34,103 @@
     return shift(x, "rep", 1)
 
 
+def exchange(outbox):
+    return lax.all_to_all(outbox, ("inner", "outer"), split_axis=0, concat_axis=0, tiled=True)
+
+
 def dense_step(tokens, teacher, expert_ids, gate_codes, gate_up_latent, down_latent):
     depth = lax.axis_size("inner")
     width = lax.axis_size("outer")
     reps = lax.axis_size("rep")
-    experts = depth * width
     tok_rows, part_width = tokens.shape
     rep = lax.axis_index("rep")
-    column_rows = depth * tok_rows
-
-    chosen = expert_ids[:, :, None] == jnp.arange(experts, dtype=jnp.int32)[None, None, :]
-    codes = jnp.sum(jnp.where(chosen, gate_codes[:, :, None], 0), axis=1).T
-
-    def column(x, axis):
-        return jnp.concatenate(across(x, "inner"), axis=axis)
-
-    tok_column = column(tokens, 0)
-    code_column = column(codes, 1)
-    tok_rows_all = jnp.concatenate(across(tok_column, "outer"), axis=0)
-    codes_all = jnp.concatenate(across(code_column, "outer"), axis=1)
+    inner = lax.axis_index("inner")
+    outer = lax.axis_index("outer")
+    f32 = jnp.float32
+    bf16 = jnp.bfloat16
+
+    def code_of(column):
+        expert = (inner + jnp.arange(depth, dtype=jnp.int32)) % depth * width + column
+        chosen = expert_ids[None] == expert[:, None, None]
+        return jnp.sum(jnp.where(chosen, gate_codes[None], 0), axis=2)
+
+    blocks = across(tokens, "inner")
+    tok_groups = [jnp.concatenate(blocks, axis=0)]
+    code_groups = [code_of(outer)]
+    pad_rows = -depth % 8
+    for j in range(1, width):
+        codes = code_of((outer + j) % width)
+        pieces = jnp.concatenate([codes // 256, codes % 256], axis=1).astype(bf16)
+        pieces = jnp.pad(pieces, ((0, pad_rows), (0, part_width - 2 * tok_rows)))
+        arrived = shift(jnp.concatenate([tok_groups[0], pieces], axis=0), "outer", j)
+        tok_groups.append(arrived[: depth * tok_rows])
+        pieces = arrived[depth * tok_rows : depth * tok_rows + depth].astype(f32)
+        code_groups.append(256.0 * pieces[:, :tok_rows] + pieces[:, tok_rows : 2 * tok_rows])
+    gate = jnp.concatenate([c.astype(f32) for c in code_groups], axis=1)[:, :, None] / 65536.0
 
     def both_features(x):
         theirs = other_rep(x)
         pair = jnp.where(rep == 0, jnp.stack([x, theirs]), jnp.stack([theirs, x]))
         return jnp.concatenate([pair[0], pair[1]], axis=1)
 
-    expert_rows = both_features(tok_rows_all)
-    mine = lax.axis_index("inner") * width + lax.axis_index("outer")
-    gate = lax.dynamic_slice_in_dim(codes_all, mine, 1, 0).astype(jnp.float32) / 65536.0
+    expert_rows = jnp.concatenate([both_features(g) for g in tok_groups], axis=0)
 
     gu_weight, gu_slope = soften(gate_up_latent[0], tokens.shape[1] * reps)
     dn_weight, dn_slope = soften(down_latent[0], down_latent.shape[1] * reps)
     projected = lax.dot_general(
-        gu_weight, expert_rows, (((2,), (1,)), ((), ())), preferred_element_type=jnp.float32
+        gu_weight, expert_rows, (((2,), (1,)), ((), ())), preferred_element_type=f32
     )
     pre_gate = projected[0]
     pre_up = projected[1]
     sigmoid_gate = jax.nn.sigmoid(pre_gate)
     activated = pre_gate * sigmoid_gate
-    gated_hidden = (activated * pre_up * gate).astype(jnp.bfloat16)
+    hidden = (activated * pre_up).astype(bf16)
 
     dn_keep = lax.dynamic_slice_in_dim(dn_weight, rep * part_width, part_width, 1)
     dn_send = lax.dynamic_slice_in_dim(dn_weight, (1 - rep) * part_width, part_width, 1)
 
     def down(weight):
-        return lax.dot_general(
-            gated_hidden, weight, (((0,), (0,)), ((), ())), preferred_element_type=jnp.float32
-        )
-
-    theirs = other_rep(down(dn_send).astype(jnp.bfloat16))
-    partial_out = down(dn_keep) + theirs.astype(jnp.float32)
-    partial_out = partial_out.reshape(width, column_rows, part_width)
-    column_sum = partial_out[0]
-    for j in range(1, width):
-        column_sum = column_sum + shift(partial_out[j].astype(jnp.bfloat16), "outer", -j).astype(
-            jnp.float32
-        )
-    column_sum = column_sum.reshape(depth, tok_rows, part_width)
-    mixed = column_sum[0]
-    for k in range(1, depth):
-        mixed = mixed + shift(column_sum[k].astype(jnp.bfloat16), "inner", -k).astype(jnp.float32)
-    student_out = mixed.astype(jnp.bfloat16)
-    residual = (mixed - teacher.astype(jnp.float32)).astype(jnp.bfloat16)
-
-    res_rows = jnp.concatenate(across(column(residual, 0), "outer"), axis=0)
-    upstream = both_features(res_rows)
-    down_grad = jnp.dot(gated_hidden, upstream, preferred_element_type=jnp.float32)
-    hidden_grad = gate * lax.dot_general(
-        dn_weight, upstream, (((1,), (1,)), ((), ())), preferred_element_type=jnp.float32
+        return lax.dot_general(hidden, weight, (((0,), (0,)), ((), ())), preferred_element_type=f32)
+
+    theirs = other_rep(down(dn_send).astype(bf16))
+    expert_out = (down(dn_keep) + theirs.astype(f32)).astype(bf16)
+    expert_out = expert_out.reshape(width, depth, tok_rows, part_width)
+
+    pair_rows = width * tok_rows
+    column_sum = 0.0
+    for k in range(depth):
+        picked = shift(expert_out[:, k].reshape(pair_rows, part_width), "inner", -k)
+        column_sum = column_sum + gate[k] * picked.astype(f32)
+    column_sum = column_sum.reshape(width, tok_rows, part_width)
+    wanted = teacher.astype(f32)
+    sent = jnp.concatenate([(column_sum[0] - wanted)[None], column_sum[1:]], axis=0).astype(bf16)
+    sums = [column_sum[j] for j in range(width)]
+    for step in range(1, width):
+        arrived = shift(sent, "outer", step).astype(f32)
+        sums = [sums[j] + arrived[(j - step) % width] for j in range(width)]
+    student_out = sums[0].astype(bf16)
+    residual = jnp.concatenate([sums[0] - wanted] + sums[1:], axis=0)
+    grads = [shift((gate[k] * residual).astype(bf16), "inner", k) for k in range(depth)]
+    grads = jnp.stack([g.reshape(width, tok_rows, part_width) for g in grads], axis=1)
+    upstream = both_features(grads.reshape(depth * pair_rows, part_width))
+
+    down_grad = jnp.dot(hidden, upstream, preferred_element_type=f32)
+    hidden_grad = lax.dot_general(
+        dn_weight, upstream, (((1,), (1,)), ((), ())), preferred_element_type=f32
     )
     gate_grad = (
         hidden_grad * pre_up * sigmoid_gate * (1.0 + pre_gate * (1.0 - sigmoid_gate))
-    ).astype(jnp.bfloat16)
-    up_grad = (hidden_grad * activated).astype(jnp.bfloat16)
+    ).astype(bf16)
+    up_grad = (hidden_grad * activated).astype(bf16)
     weight_grads = lax.dot_general(
         jnp.stack([gate_grad, up_grad]),
         expert_rows,
         (((2,), (0,)), ((), ())),
-        preferred_element_type=jnp.float32,
+        preferred_element_type=f32,
     )
     new_gate_up = gate_up_latent - learn_rate * (gu_slope * weight_grads)[None]
     new_down = down_latent - learn_rate * (dn_slope * down_grad)[None]
     return (student_out, new_gate_up, new_down)
-
-
-def exchange(outbox):
-    return lax.all_to_all(outbox, ("inner", "outer"), split_axis=0, concat_axis=0, tiled=True)
 
 
 def routed_step(tokens, teacher, expert_ids, gate_codes, gate_up_latent, down_latent):

time: 59.7 us -> 52.2 us (0.87)
  starting transfers between devices: 26.3 us -> 17.6 us
  other arithmetic: 3.85 us -> 5.8 us
  local copies, waits for them, and re-layouts: 0.27 us -> 2.05 us
  waiting for transfers between devices: 22.2 us -> 20.5 us
  matrix products: 5.92 us -> 4.99 us
    ppermute x19 -> x15, starting transfers between devices: 26.3 us -> 17.6 us  [shift(): return lax.ppermute(x, axis, [(i, (i + step) % size) for i in range(size)])]
    ppermute x19 -> x15, waiting for transfers between devices: 22.2 us -> 20.5 us  [shift(): return lax.ppermute(x, axis, [(i, (i + step) % size) for i in range(size)])]
    mul x0 -> x1, local copies, waits for them, and re-layouts: none -> 1.31 us  [dense_step(): column_sum = column_sum + gate[k] * picked.astype(f32)]
    convert_element_type x2 -> x4, other arithmetic: 0.7 us -> 1.66 us  [the longest x1 0.85 us: dense_step(): arrived = shift(sent, 'outer', step).astype(f32)]
    dot_general x3, matrix products: 2.84 us -> 1.89 us  [the longest x1 1.4 us: dense_step(): down_grad = jnp.dot(hidden, upstream, preferred_element_type=f32)]
    concatenate x3 -> x5, other arithmetic: 0.09 us -> 0.88 us  [the longest x1 0.64 us: dense_step(): jnp.concatenate([(column_sum[0] - wanted)[None], column_sum[1:]], axis=0)]
    sub x0 -> x1, other arithmetic: none -> 0.64 us  [dense_step(): residual = jnp.concatenate([sums[0] - wanted] + sums[1:], axis=0)]
    reduce_sum x1, other arithmetic: 0.72 us -> 0.09 us  [code_of(): return jnp.sum(jnp.where(chosen, gate_codes[None], 0), axis=2)]
  transfers between devices with their start and end apart: 19 -> 15, of which waited for: 13 -> 12; matrix products, arithmetic and copies ran while one was open for 6% -> 10% of each run, Pallas kernels for 0% -> 0%
where the time goes in v2:
time: 52.2 us; the launch traced here: 52 us
  waiting for transfers between devices  20.5 us (39%)
  starting transfers between devices  17.6 us (34%)
  other arithmetic  5.8 us (11%)
  matrix products  4.99 us (10%)
  local copies, waits for them, and re-layouts  2.05 us (4%)
  between operations  1.08 us (2%)
    ppermute x15, waiting for transfers between devices, shift(): return lax.ppermute(x, axis, [(i, (i + step) % size) for i in range(size)])  20.5 us
    ppermute x15, starting transfers between devices, shift(): return lax.ppermute(x, axis, [(i, (i + step) % size) for i in range(size)])  17.6 us
    dot_general x1, matrix products, dense_step(): lax.dot_general(jnp.stack([gate_grad, up_grad]), expert_rows, (((2,), (0,...  2.02 us
    reduce_sum x2, other arithmetic, soften(): row_scale = jnp.mean(jnp.abs(latent), axis=-1, keepdims=True) + 1e-06  1.76 us
    dot_general x1, matrix products, dense_step(): down_grad = jnp.dot(hidden, upstream, preferred_element_type=f32)  1.4 us
    mul x1, local copies, waits for them, and re-layouts, dense_step(): column_sum = column_sum + gate[k] * picked.astype(f32)  1.31 us
  transfers between devices with their start and end apart: 15, of which 12 were waited for; matrix products, arithmetic and copies ran while one was open for 10% of the time, Pallas kernels for 0%

profile of v2, /device:TPU:0, one launch (start us, length us, event | category | flops | bytes accessed | tf_op | source)
XLA Modules:
  0.0 52.0 jit_solution(6167390013538533523)
XLA Ops:
  0.7 3.1 %collective-permute-start = (bf16[32,512]{1,0:T(8,128)(2,1)}, bf16[32,512]{1,0:T(8,128)(2,1)S(1)}, u32[]{:S(2)}, u32[]{:S(2)}) collective-permute-start(bf16[32,512]{1,0:T(8,128)(2,1)} %param.6), channel_id=1, source_target_pairs={{0,4},{4,8},{8,12},{12,0},{1,5},{5,9},{9,13},{13,1},{2,6},{6,10},{... | collective-permute-start | bytes 98312 | tf_op jit(solution)/shard_map/ppermute | solution.py:26
  3.8 2.6 %collective-permute-start.1 = (bf16[32,512]{1,0:T(8,128)(2,1)}, bf16[32,512]{1,0:T(8,128)(2,1)S(1)}, u32[]{:S(2)}, u32[]{:S(2)}) collective-permute-start(bf16[32,512]{1,0:T(8,128)(2,1)} %param.6), channel_id=1, source_target_pairs={{0,8},{4,12},{8,0},{12,4},{1,9},{5,13},{9,1},{13,5},{2,10},{6,14},... | collective-permute-start | bytes 98312 | tf_op jit(solution)/shard_map/ppermute | solution.py:26
  6.4 1.3 %collective-permute-start.2 = (bf16[32,512]{1,0:T(8,128)(2,1)}, bf16[32,512]{1,0:T(8,128)(2,1)S(1)}, u32[]{:S(2)}, u32[]{:S(2)}) collective-permute-start(bf16[32,512]{1,0:T(8,128)(2,1)} %param.6), channel_id=1, source_target_pairs={{0,12},{4,0},{8,4},{12,8},{1,13},{5,1},{9,5},{13,9},{2,14},{6,2},{... | collective-permute-start | bytes 98312 | tf_op jit(solution)/shard_map/ppermute | solution.py:26
  7.7 1.6 %fusion = f32[2,192]{1,0:T(2,128)S(1)} fusion(f32[1,2,192,1024]{3,2,1,0:T(8,128)} %param.10), kind=kLoop, calls=%fused_computation.3 | loop fusion | flops 786048 | bytes 1574400 | tf_op jit(solution)/shard_map/reduce_sum | solution.py:12
  9.3 0.0 copy-start.12
  9.4 0.1 select_reduce_fusion.1
  9.5 0.1 fusion.3
  9.7 0.4 multiply_convert_fusion.1
  10.0 0.0 copy-done.9
  10.0 0.0 copy-start.1
  10.1 0.0 collective-permute-done
  10.1 0.0 collective-permute-done.1
  10.1 0.4 collective-permute-done.2
  10.5 0.0 collective-permute-start.4
  10.5 0.1 constant_dynamic-update-slice_fusion
  10.6 1.5 %collective-permute-start.3 = (bf16[136,512]{1,0:T(8,128)(2,1)S(1)}, bf16[136,512]{1,0:T(8,128)(2,1)S(1)}, u32[]{:S(2)}, u32[]{:S(2)}) collective-permute-start(bf16[136,512]{1,0:T(8,128)(2,1)S(1)} %constant_dynamic-update-slice_fusion), channel_id=1, source_target_pairs={{0,2},{2,0},{1,3},{3,1},{4,6},{6,4},{5,7},{7,5},{8,10},{10,8},{9,1... | collective-permute-start | bytes 417800 | tf_op jit(solution)/shard_map/ppermute | solution.py:26
  12.1 0.0 collective-permute-done.4
  12.2 4.5 %collective-permute-done.3 = bf16[136,512]{1,0:T(8,128)(2,1)S(1)} collective-permute-done((bf16[136,512]{1,0:T(8,128)(2,1)S(1)}, bf16[136,512]{1,0:T(8,128)(2,1)S(1)}, u32[]{:S(2)}, u32[]{:S(2)}) %collective-permute-start.3) | collective-permute-done | bytes 139296 | tf_op jit(solution)/shard_map/ppermute | solution.py:26
  16.7 0.1 collective-permute-start.5
  16.8 1.3 %collective-permute-done.5 = bf16[128,512]{1,0:T(8,128)(2,1)S(1)} collective-permute-done((bf16[128,512]{1,0:T(8,128)(2,1)S(1)}, bf16[128,512]{1,0:T(8,128)(2,1)S(1)}, u32[]{:S(2)}, u32[]{:S(2)}) %collective-permute-start.5) | collective-permute-done | bytes 131104 | tf_op jit(solution)/shard_map/ppermute | solution.py:26
  18.1 0.0 copy-start.5
  18.2 0.0 copy-start.7
  18.2 0.7 %fusion.4 = f32[2,192,256]{2,1,0:T(8,128)S(1)} fusion(f32[1,2,192,1024]{3,2,1,0:T(8,128)S(1)} %copy-done.1, f32[2,192]{1,0:T(2,128)S(1)} %get-tuple-element.42, f32[2,192]{1,0:T(2,128)S(1)} %get-tuple-element.41, bf16[128,512]{1,0:T(8,128)(2,1)S(1)} %get-tuple-element.19, bf16[128,512]{1,0:T(8,128)(2,1)S(1)} %get-tuple-element.18, ...), kind=kOutput, calls=%fused_computation.17 | convolution fusion | flops 206962688 | bytes 2493440 | tf_op jit(solution)/shard_map/dot_general | solution.py:80
  18.9 0.0 copy-done.3
  18.9 0.0 copy-done.5
  19.0 0.0 copy-done.7
  19.0 0.0 copy-start.2
  19.0 0.1 multiply_convert_fusion.5
  19.0 0.2 convolution_convert_fusion
  19.3 0.2 collective-permute-start.6
  19.5 0.1 fusion.34
  19.6 0.1 maximum_multiply_fusion
  19.7 1.2 %collective-permute-done.6 = bf16[256,512]{1,0:T(8,128)(2,1)S(1)} collective-permute-done((bf16[256,512]{1,0:T(8,128)(2,1)S(1)}, bf16[256,512]{1,0:T(8,128)(2,1)S(1)}, u32[]{:S(2)}, u32[]{:S(2)}) %collective-permute-start.6) | collective-permute-done | bytes 262176 | tf_op jit(solution)/shard_map/ppermute | solution.py:26
  20.9 0.2 add_convert_fusion
  21.2 0.4 collective-permute-start.9
  21.6 3.3 %collective-permute-start.8 = (bf16[64,512]{1,0:T(8,128)(2,1)S(1)}, bf16[64,512]{1,0:T(8,128)(2,1)S(1)}, u32[]{:S(2)}, u32[]{:S(2)}) collective-permute-start(bf16[64,512]{1,0:T(8,128)(2,1)S(1)} %bitcast.125), channel_id=1, source_target_pairs={{0,8},{4,12},{8,0},{12,4},{1,9},{5,13},{9,1},{13,5},{2,10},{6,14},... | collective-permute-start | bytes 196616 | tf_op jit(solution)/shard_map/ppermute | solution.py:26
  25.0 0.2 collective-permute-start.7
  25.2 0.5 %slice_reduce_fusion = (f32[64]{0:T(128)}, f32[64]{0:T(128)S(1)}, f32[64]{0:T(128)S(1)}, f32[64]{0:T(128)S(1)}, f32[64]{0:T(128)S(1)}) fusion(f32[4,64,1]{1,0,2:T(4,128)S(1)} %maximum_multiply_fusion), kind=kLoop, calls=%fused_computation.117 | loop fusion | bytes 2304 | tf_op jit(solution)/shard_map/slice | solution.py:103
  25.7 2.5 %collective-permute-done.9 = bf16[64,512]{1,0:T(8,128)(2,1)S(1)} collective-permute-done((bf16[64,512]{1,0:T(8,128)(2,1)S(1)}, bf16[64,512]{1,0:T(8,128)(2,1)S(1)}, u32[]{:S(2)}, u32[]{:S(2)}) %collective-permute-start.9) | collective-permute-done | bytes 65568 | tf_op jit(solution)/shard_map/ppermute | solution.py:26
  28.1 1.9 %collective-permute-done.8 = bf16[64,512]{1,0:T(8,128)(2,1)S(1)} collective-permute-done((bf16[64,512]{1,0:T(8,128)(2,1)S(1)}, bf16[64,512]{1,0:T(8,128)(2,1)S(1)}, u32[]{:S(2)}, u32[]{:S(2)}) %collective-permute-start.8) | collective-permute-done | bytes 65568 | tf_op jit(solution)/shard_map/ppermute | solution.py:26
  30.1 0.1 collective-permute-done.7
  30.2 0.1 fusion.17
  30.4 0.0 copy-done.2
  30.4 0.6 %pad_maximum_fusion.5 = bf16[2,32,512]{2,1,0:T(8,128)(2,1)} fusion(bf16[1,32,512]{2,1,0:T(8,128)(2,1)S(1)} %fusion.23, bf16[1,32,512]{2,1,0:T(8,128)(2,1)S(1)} %fusion.24), kind=kLoop, calls=%fused_computation.63 | loop fusion | flops 32768 | bytes 131072 | tf_op jit(solution)/shard_map/concatenate | solution.py:106
  31.0 1.5 %collective-permute-start.10 = (bf16[2,32,512]{2,1,0:T(8,128)(2,1)}, bf16[2,32,512]{2,1,0:T(8,128)(2,1)}, u32[]{:S(2)}, u32[]{:S(2)}) collective-permute-start(bf16[2,32,512]{2,1,0:T(8,128)(2,1)} %pad_maximum_fusion.5), channel_id=1, source_target_pairs={{0,2},{2,0},{1,3},{3,1},{4,6},{6,4},{5,7},{7,5},{8,10},{10,8},{9,1... | collective-permute-start | bytes 196616 | tf_op jit(solution)/shard_map/ppermute | solution.py:26
  32.5 1.3 %mul.242 = f32[2,32]{1,0:T(2,128)} reshape(f32[64]{0:T(128)} %get-tuple-element.34) | data formatting | bytes 512 | tf_op jit(solution)/shard_map/mul | solution.py:103
  33.8 1.8 %collective-permute-done.10 = bf16[2,32,512]{2,1,0:T(8,128)(2,1)} collective-permute-done((bf16[2,32,512]{2,1,0:T(8,128)(2,1)}, bf16[2,32,512]{2,1,0:T(8,128)(2,1)}, u32[]{:S(2)}, u32[]{:S(2)}) %collective-permute-start.10) | collective-permute-done | bytes 65568 | tf_op jit(solution)/shard_map/ppermute | solution.py:26
  35.6 0.8 %convert_element_type.97 = f32[2,32,512]{2,1,0:T(8,128)S(1)} convert(bf16[2,32,512]{2,1,0:T(8,128)(2,1)} %collective-permute-done.10) | non-fusion elementwise | flops 32768 | bytes 196608 | tf_op jit(solution)/shard_map/convert_element_type | solution.py:109
  36.5 0.6 %convert_subtract_fusion = (f32[32,512]{1,0:T(8,128)S(1)}, f32[32,512]{1,0:T(8,128)S(1)}, bf16[32,512]{1,0:T(8,128)(2,1)}) fusion(bf16[32,512]{1,0:T(8,128)(2,1)S(1)} %copy-done.2, f32[2,32,512]{2,1,0:T(8,128)S(1)} %convert_element_type.97, f32[64,512]{1,0:T(8,128)S(1)} %fusion.17), kind=kLoop, calls=%fused_computation.56 | loop fusion | flops 81920 | bytes 458752 | tf_op jit(solution)/shard_map/sub | solution.py:112
  37.1 0.1 pad_maximum_fusion.4
  37.2 2.6 %collective-permute-start.13 = (bf16[64,512]{1,0:T(8,128)(2,1)S(1)}, bf16[64,512]{1,0:T(8,128)(2,1)S(1)}, u32[]{:S(2)}, u32[]{:S(2)}) collective-permute-start(bf16[64,512]{1,0:T(8,128)(2,1)S(1)} %get-tuple-element.25), channel_id=1, source_target_pairs={{0,12},{4,0},{8,4},{12,8},{1,13},{5,1},{9,5},{13,9},{2,14},{6,2},{... | collective-permute-start | bytes 196616 | tf_op jit(solution)/shard_map/ppermute | solution.py:26
  39.8 0.6 %collective-permute-start.12 = (bf16[64,512]{1,0:T(8,128)(2,1)S(1)}, bf16[64,512]{1,0:T(8,128)(2,1)S(1)}, u32[]{:S(2)}, u32[]{:S(2)}) collective-permute-start(bf16[64,512]{1,0:T(8,128)(2,1)S(1)} %get-tuple-element.24), channel_id=1, source_target_pairs={{0,8},{4,12},{8,0},{12,4},{1,9},{5,13},{9,1},{13,5},{2,10},{6,14},... | collective-permute-start | bytes 196616 | tf_op jit(solution)/shard_map/ppermute | solution.py:26
  40.3 0.1 collective-permute-start.11
  40.4 0.7 %multiply_convert_fusion.9 = bf16[2,1,32,512]{3,2,1,0:T(8,128)(2,1)S(1)} fusion(f32[2,1,32,512]{3,2,1,0:T(8,128)S(1)} %bitcast.119, f32[2,32]{1,0:T(2,128)} %mul.242), kind=kLoop, calls=%fused_computation.53 | loop fusion | flops 65536 | bytes 196864 | tf_op jit(solution)/shard_map/convert_element_type | solution.py:113
  41.1 0.5 collective-permute-done.13
  41.7 3.4 %collective-permute-done.12 = bf16[64,512]{1,0:T(8,128)(2,1)S(1)} collective-permute-done((bf16[64,512]{1,0:T(8,128)(2,1)S(1)}, bf16[64,512]{1,0:T(8,128)(2,1)S(1)}, u32[]{:S(2)}, u32[]{:S(2)}) %collective-permute-start.12) | collective-permute-done | bytes 65568 | tf_op jit(solution)/shard_map/ppermute | solution.py:26
  45.0 1.4 %collective-permute-done.11 = bf16[64,512]{1,0:T(8,128)(2,1)S(1)} collective-permute-done((bf16[64,512]{1,0:T(8,128)(2,1)S(1)}, bf16[64,512]{1,0:T(8,128)(2,1)S(1)}, u32[]{:S(2)}, u32[]{:S(2)}) %collective-permute-start.11) | collective-permute-done | bytes 65568 | tf_op jit(solution)/shard_map/ppermute | solution.py:26
  46.5 0.1 collective-permute-start.14
  46.5 1.5 %collective-permute-done.14 = bf16[256,512]{1,0:T(8,128)(2,1)S(1)} collective-permute-done((bf16[256,512]{1,0:T(8,128)(2,1)S(1)}, bf16[256,512]{1,0:T(8,128)(2,1)S(1)}, u32[]{:S(2)}, u32[]{:S(2)}) %collective-permute-start.14) | collective-permute-done | bytes 262176 | tf_op jit(solution)/shard_map/ppermute | solution.py:26
  48.1 0.1 maximum_select_fusion
  48.2 0.3 fusion.19
  48.5 0.0 copy-start.8
  48.6 1.4 %fusion.2 = f32[1,192,1024]{2,1,0:T(8,128)} fusion(f32[1,192,1024]{2,1,0:T(8,128)S(1)} %copy-done, bf16[192,256]{1,0:T(8,128)(2,1)S(1)} %multiply_convert_fusion.5, f32[192]{0:T(256)S(1)} %get-tuple-element.44, bf16[256,512]{1,0:T(8,128)(2,1)S(1)} %get-tuple-element.8, bf16[256,512]{1,0:T(8,128)(2,1)S(1)} %get-tuple-element.7), kind=kOutput, calls=%fused_computation.9 | convolution fusion | flops 104071168 | bytes 2196224 | tf_op jit(solution)/shard_map/dot_general | solution.py:117
  50.0 2.0 %bitcast_subtract_fusion = f32[1,2,192,1024]{3,2,1,0:T(8,128)} fusion(f32[1,2,192,1024]{3,2,1,0:T(8,128)S(1)} %copy-done.1, f32[2,192]{1,0:T(2,128)S(1)} %copy-done.13, bf16[128,512]{1,0:T(8,128)(2,1)S(1)} %copy-done.8, bf16[128,512]{1,0:T(8,128)(2,1)S(1)} %copy-done.6, bf16[128,512]{1,0:T(8,128)(2,1)S(1)} %copy-done.4, ...), kind=kOutput, calls=%fused_computation | convolution fusion | flops 208240640 | bytes 3868160 | tf_op jit(solution)/shard_map/dot_general | solution.py:125
  (37 shorter events, 0.3 us)
Async XLA Ops:
  0.6 8.7 %copy-start.10 = (s32[32,8]{0,1:T(8,128)S(1)}, s32[32,8]{0,1:T(8,128)}, u32[]{:S(2)}) copy-start(s32[32,8]{0,1:T(8,128)} %param.9) | copy-start | bytes 3076
  0.6 8.7 %copy-start.11 = (s32[32,8]{0,1:T(8,128)S(1)}, s32[32,8]{0,1:T(8,128)}, u32[]{:S(2)}) copy-start(s32[32,8]{0,1:T(8,128)} %param.8) | copy-start | bytes 3076
  0.7 8.9 %copy-start = (f32[1,192,1024]{2,1,0:T(8,128)S(1)}, f32[1,192,1024]{2,1,0:T(8,128)}, u32[]{:S(2)}) copy-start(f32[1,192,1024]{2,1,0:T(8,128)} %param.11) | copy-start | bytes 2359300
  0.7 9.4 %collective-permute-start = (bf16[32,512]{1,0:T(8,128)(2,1)}, bf16[32,512]{1,0:T(8,128)(2,1)S(1)}, u32[]{:S(2)}, u32[]{:S(2)}) collective-permute-start(bf16[32,512]{1,0:T(8,128)(2,1)} %param.6), channel_id=1, source_target_pairs={{0,4},{4,8},{8,12},{12,0},{1,5},{5,9},{9,13},{13,1},{2,6},{6,10},{... | collective-permute-start | bytes 98312 | tf_op jit(solution)/shard_map/ppermute | solution.py:26
  3.8 6.3 %collective-permute-start.1 = (bf16[32,512]{1,0:T(8,128)(2,1)}, bf16[32,512]{1,0:T(8,128)(2,1)S(1)}, u32[]{:S(2)}, u32[]{:S(2)}) collective-permute-start(bf16[32,512]{1,0:T(8,128)(2,1)} %param.6), channel_id=1, source_target_pairs={{0,8},{4,12},{8,0},{12,4},{1,9},{5,13},{9,1},{13,5},{2,10},{6,14},... | collective-permute-start | bytes 98312 | tf_op jit(solution)/shard_map/ppermute | solution.py:26
  6.4 4.1 %collective-permute-start.2 = (bf16[32,512]{1,0:T(8,128)(2,1)}, bf16[32,512]{1,0:T(8,128)(2,1)S(1)}, u32[]{:S(2)}, u32[]{:S(2)}) collective-permute-start(bf16[32,512]{1,0:T(8,128)(2,1)} %param.6), channel_id=1, source_target_pairs={{0,12},{4,0},{8,4},{12,8},{1,13},{5,1},{9,5},{13,9},{2,14},{6,2},{... | collective-permute-start | bytes 98312 | tf_op jit(solution)/shard_map/ppermute | solution.py:26
  7.7 2.3 %copy-start.9 = (bf16[32,512]{1,0:T(8,128)(2,1)S(1)}, bf16[32,512]{1,0:T(8,128)(2,1)}, u32[]{:S(2)}) copy-start(bf16[32,512]{1,0:T(8,128)(2,1)} %param.6) | copy-start | bytes 98308
  9.3 8.8 %copy-start.12 = (f32[2,192]{1,0:T(2,128)}, f32[2,192]{1,0:T(2,128)S(1)}, u32[]{:S(2)}) copy-start(f32[2,192]{1,0:T(2,128)S(1)} %get-tuple-element.42) | copy-start | bytes 4612
  10.0 8.2 %copy-start.1 = (f32[1,2,192,1024]{3,2,1,0:T(8,128)S(1)}, f32[1,2,192,1024]{3,2,1,0:T(8,128)}, u32[]{:S(2)}) copy-start(f32[1,2,192,1024]{3,2,1,0:T(8,128)} %param.10) | copy-start | bytes 4718596
  10.5 1.6 %collective-permute-start.4 = (bf16[128,512]{1,0:T(8,128)(2,1)S(1)}, bf16[128,512]{1,0:T(8,128)(2,1)S(1)}, u32[]{:S(2)}, u32[]{:S(2)}) collective-permute-start(bf16[128,512]{1,0:T(8,128)(2,1)S(1)} %get-tuple-element.26), channel_id=1, source_target_pairs={{0,1},{1,0},{2,3},{3,2},{4,5},{5,4},{6,7},{7,6},{8,9},{9,8},{10,11... | collective-permute-start | bytes 393224 | tf_op jit(solution)/shard_map/ppermute | solution.py:26
  10.6 6.1 %collective-permute-start.3 = (bf16[136,512]{1,0:T(8,128)(2,1)S(1)}, bf16[136,512]{1,0:T(8,128)(2,1)S(1)}, u32[]{:S(2)}, u32[]{:S(2)}) collective-permute-start(bf16[136,512]{1,0:T(8,128)(2,1)S(1)} %constant_dynamic-update-slice_fusion), channel_id=1, source_target_pairs={{0,2},{2,0},{1,3},{3,1},{4,6},{6,4},{5,7},{7,5},{8,10},{10,8},{9,1... | collective-permute-start | bytes 417800 | tf_op jit(solution)/shard_map/ppermute | solution.py:26
  12.2 6.8 %copy-start.3 = (bf16[128,512]{1,0:T(8,128)(2,1)}, bf16[128,512]{1,0:T(8,128)(2,1)S(1)}, u32[]{:S(2)}) copy-start(bf16[128,512]{1,0:T(8,128)(2,1)S(1)} %get-tuple-element.17) | copy-start | bytes 393220
  16.7 1.4 %collective-permute-start.5 = (bf16[128,512]{1,0:T(8,128)(2,1)S(1)}, bf16[128,512]{1,0:T(8,128)(2,1)S(1)}, u32[]{:S(2)}, u32[]{:S(2)}) collective-permute-start(bf16[128,512]{1,0:T(8,128)(2,1)S(1)} %get-tuple-element.21), channel_id=1, source_target_pairs={{0,1},{1,0},{2,3},{3,2},{4,5},{5,4},{6,7},{7,6},{8,9},{9,8},{10,11... | collective-permute-start | bytes 393224 | tf_op jit(solution)/shard_map/ppermute | solution.py:26
  18.1 0.8 %copy-start.5 = (bf16[128,512]{1,0:T(8,128)(2,1)}, bf16[128,512]{1,0:T(8,128)(2,1)S(1)}, u32[]{:S(2)}) copy-start(bf16[128,512]{1,0:T(8,128)(2,1)S(1)} %get-tuple-element.18) | copy-start | bytes 393220
  18.2 0.8 %copy-start.7 = (bf16[128,512]{1,0:T(8,128)(2,1)}, bf16[128,512]{1,0:T(8,128)(2,1)S(1)}, u32[]{:S(2)}) copy-start(bf16[128,512]{1,0:T(8,128)(2,1)S(1)} %get-tuple-element.19) | copy-start | bytes 393220
  19.0 11.4 %copy-start.2 = (bf16[32,512]{1,0:T(8,128)(2,1)S(1)}, bf16[32,512]{1,0:T(8,128)(2,1)}, u32[]{:S(2)}) copy-start(bf16[32,512]{1,0:T(8,128)(2,1)} %param.7) | copy-start | bytes 98308
  19.3 1.6 %collective-permute-start.6 = (bf16[256,512]{1,0:T(8,128)(2,1)S(1)}, bf16[256,512]{1,0:T(8,128)(2,1)S(1)}, u32[]{:S(2)}, u32[]{:S(2)}) collective-permute-start(bf16[256,512]{1,0:T(8,128)(2,1)S(1)} %convolution_convert_fusion), channel_id=1, source_target_pairs={{0,1},{1,0},{2,3},{3,2},{4,5},{5,4},{6,7},{7,6},{8,9},{9,8},{10,11... | collective-permute-start | bytes 786440 | tf_op jit(solution)/shard_map/ppermute | solution.py:26
  21.2 7.0 %collective-permute-start.9 = (bf16[64,512]{1,0:T(8,128)(2,1)S(1)}, bf16[64,512]{1,0:T(8,128)(2,1)S(1)}, u32[]{:S(2)}, u32[]{:S(2)}) collective-permute-start(bf16[64,512]{1,0:T(8,128)(2,1)S(1)} %bitcast.127), channel_id=1, source_target_pairs={{0,4},{4,8},{8,12},{12,0},{1,5},{5,9},{9,13},{13,1},{2,6},{6,10},{... | collective-permute-start | bytes 196616 | tf_op jit(solution)/shard_map/ppermute | solution.py:26
  21.6 8.5 %collective-permute-start.8 = (bf16[64,512]{1,0:T(8,128)(2,1)S(1)}, bf16[64,512]{1,0:T(8,128)(2,1)S(1)}, u32[]{:S(2)}, u32[]{:S(2)}) collective-permute-start(bf16[64,512]{1,0:T(8,128)(2,1)S(1)} %bitcast.125), channel_id=1, source_target_pairs={{0,8},{4,12},{8,0},{12,4},{1,9},{5,13},{9,1},{13,5},{2,10},{6,14},... | collective-permute-start | bytes 196616 | tf_op jit(solution)/shard_map/ppermute | solution.py:26
  25.0 5.3 %collective-permute-start.7 = (bf16[64,512]{1,0:T(8,128)(2,1)S(1)}, bf16[64,512]{1,0:T(8,128)(2,1)S(1)}, u32[]{:S(2)}, u32[]{:S(2)}) collective-permute-start(bf16[64,512]{1,0:T(8,128)(2,1)S(1)} %bitcast.124), channel_id=1, source_target_pairs={{0,12},{4,0},{8,4},{12,8},{1,13},{5,1},{9,5},{13,9},{2,14},{6,2},{... | collective-permute-start | bytes 196616 | tf_op jit(solution)/shard_map/ppermute | solution.py:26
  31.0 4.6 %collective-permute-start.10 = (bf16[2,32,512]{2,1,0:T(8,128)(2,1)}, bf16[2,32,512]{2,1,0:T(8,128)(2,1)}, u32[]{:S(2)}, u32[]{:S(2)}) collective-permute-start(bf16[2,32,512]{2,1,0:T(8,128)(2,1)} %pad_maximum_fusion.5), channel_id=1, source_target_pairs={{0,2},{2,0},{1,3},{3,1},{4,6},{6,4},{5,7},{7,5},{8,10},{10,8},{9,1... | collective-permute-start | bytes 196616 | tf_op jit(solution)/shard_map/ppermute | solution.py:26
  37.2 4.5 %collective-permute-start.13 = (bf16[64,512]{1,0:T(8,128)(2,1)S(1)}, bf16[64,512]{1,0:T(8,128)(2,1)S(1)}, u32[]{:S(2)}, u32[]{:S(2)}) collective-permute-start(bf16[64,512]{1,0:T(8,128)(2,1)S(1)} %get-tuple-element.25), channel_id=1, source_target_pairs={{0,12},{4,0},{8,4},{12,8},{1,13},{5,1},{9,5},{13,9},{2,14},{6,2},{... | collective-permute-start | bytes 196616 | tf_op jit(solution)/shard_map/ppermute | solution.py:26
  39.8 5.3 %collective-permute-start.12 = (bf16[64,512]{1,0:T(8,128)(2,1)S(1)}, bf16[64,512]{1,0:T(8,128)(2,1)S(1)}, u32[]{:S(2)}, u32[]{:S(2)}) collective-permute-start(bf16[64,512]{1,0:T(8,128)(2,1)S(1)} %get-tuple-element.24), channel_id=1, source_target_pairs={{0,8},{4,12},{8,0},{12,4},{1,9},{5,13},{9,1},{13,5},{2,10},{6,14},... | collective-permute-start | bytes 196616 | tf_op jit(solution)/shard_map/ppermute | solution.py:26
  40.3 6.1 %collective-permute-start.11 = (bf16[64,512]{1,0:T(8,128)(2,1)S(1)}, bf16[64,512]{1,0:T(8,128)(2,1)S(1)}, u32[]{:S(2)}, u32[]{:S(2)}) collective-permute-start(bf16[64,512]{1,0:T(8,128)(2,1)S(1)} %get-tuple-element.23), channel_id=1, source_target_pairs={{0,4},{4,8},{8,12},{12,0},{1,5},{5,9},{9,13},{13,1},{2,6},{6,10},{... | collective-permute-start | bytes 196616 | tf_op jit(solution)/shard_map/ppermute | solution.py:26
  46.5 1.6 %collective-permute-start.14 = (bf16[256,512]{1,0:T(8,128)(2,1)S(1)}, bf16[256,512]{1,0:T(8,128)(2,1)S(1)}, u32[]{:S(2)}, u32[]{:S(2)}) collective-permute-start(bf16[256,512]{1,0:T(8,128)(2,1)S(1)} %bitcast.116), channel_id=1, source_target_pairs={{0,1},{1,0},{2,3},{3,2},{4,5},{5,4},{6,7},{7,6},{8,9},{9,8},{10,11... | collective-permute-start | bytes 786440 | tf_op jit(solution)/shard_map/ppermute | solution.py:26
  48.5 1.4 %copy-start.4 = (bf16[128,512]{1,0:T(8,128)(2,1)S(1)}, bf16[128,512]{1,0:T(8,128)(2,1)}, u32[]{:S(2)}) copy-start(bf16[128,512]{1,0:T(8,128)(2,1)} %copy-done.3) | copy-start | bytes 393220
  48.5 1.4 %copy-start.6 = (bf16[128,512]{1,0:T(8,128)(2,1)S(1)}, bf16[128,512]{1,0:T(8,128)(2,1)}, u32[]{:S(2)}) copy-start(bf16[128,512]{1,0:T(8,128)(2,1)} %copy-done.5) | copy-start | bytes 393220
  48.5 1.4 %copy-start.8 = (bf16[128,512]{1,0:T(8,128)(2,1)S(1)}, bf16[128,512]{1,0:T(8,128)(2,1)}, u32[]{:S(2)}) copy-start(bf16[128,512]{1,0:T(8,128)(2,1)} %copy-done.7) | copy-start | bytes 393220
  48.6 1.4 %copy-start.13 = (f32[2,192]{1,0:T(2,128)S(1)}, f32[2,192]{1,0:T(2,128)}, u32[]{:S(2)}) copy-start(f32[2,192]{1,0:T(2,128)} %copy-done.12) | copy-start | bytes 4612

commit v3 on v0

--- a/solution.py
+++ b/solution.py
@@ -3,40 +3,415 @@
 import jax
 import jax.numpy as jnp
 from jax import lax
+from jax.experimental import pallas as pl
+from jax.experimental.pallas import tpu as pltpu
 from jax.sharding import PartitionSpec as P
-
-D = 1024
-HID = 384
-
 
 learn_rate = 1.0
 
 
 def soften(latent, fan_in):
     row_scale = jnp.mean(jnp.abs(latent), axis=-1, keepdims=True) + 1e-06
-    normed = latent / row_scale
-    lower = jnp.tanh(4.0 * (normed - 0.5))
-    upper = jnp.tanh(4.0 * (normed + 0.5))
+    steep = latent * (4.0 / row_scale)
+    lower = jnp.tanh(steep - 2.0)
+    upper = jnp.tanh(steep + 2.0)
     fan_root = 1.0 / math.sqrt(fan_in)
-    weight = (row_scale * 0.5 * (lower + upper) * fan_root).astype(jnp.bfloat16)
-    slope = 2.0 * (2.0 - lower * lower - upper * upper) * fan_root
+    weight = ((row_scale * (0.5 * fan_root)) * (lower + upper)).astype(jnp.bfloat16)
+    slope = (4.0 * fan_root) - (2.0 * fan_root) * (lower * lower + upper * upper)
     return (weight, slope)
 
 
-def dispatch_rows(outbox):
+def ahead(place, step, size):
+    return place ^ step if size & (size - 1) == 0 else (place + step) % size
+
+
+def back(place, step, size):
+    return place ^ step if size & (size - 1) == 0 else (place - step) % size
+
+
+def shift(x, axis, step, way=ahead):
+    size = lax.axis_size(axis)
+    if step == 0:
+        return x
+    return lax.ppermute(x, axis, [(i, way(i, step, size)) for i in range(size)])
+
+
+def in_order(size):
+    return [k for k in (2, 1, 3) if k < size] + [0] + list(range(4, size))
+
+
+def other_rep(x):
+    return shift(x, "rep", 1)
+
+
+def exchange(outbox):
     return lax.all_to_all(outbox, ("inner", "outer"), split_axis=0, concat_axis=0, tiled=True)
 
 
-def combine_rows(outbox):
-    return lax.all_to_all(outbox, ("inner", "outer"), split_axis=0, concat_axis=0, tiled=True)
-
-
-def upstream_rows(outbox):
-    return lax.all_to_all(outbox, ("inner", "outer"), split_axis=0, concat_axis=0, tiled=True)
-
-
-def on_device(tokens, teacher, expert_ids, gate_codes, gate_up_latent, down_latent):
+MEBI = 2**20
+
+
+def dot(left, right, left_dim, right_dim):
+    return lax.dot_general(
+        left, right, (((left_dim,), (right_dim,)), ((), ())), preferred_element_type=jnp.float32
+    )
+
+
+def whole():
+    return pl.BlockSpec(memory_space=pltpu.VMEM)
+
+
+def like(shape, dtype):
+    return jax.ShapeDtypeStruct(shape, dtype)
+
+
+def halves(rep_ref, part_width):
+    mine = pl.multiple_of(rep_ref[0] * part_width, part_width)
+    theirs = pl.multiple_of((1 - rep_ref[0]) * part_width, part_width)
+    return mine, theirs
+
+
+def upright(gate):
+    def body(flat, tall):
+        tall[...] = flat[...].T
+
+    return pl.pallas_call(
+        body,
+        in_specs=[whole()],
+        out_specs=whole(),
+        out_shape=like(gate.shape[::-1], gate.dtype),
+        compiler_params=pltpu.CompilerParams(vmem_limit_bytes=2 * MEBI),
+        name="upright",
+    )(gate)
+
+
+def soften_all(gate_up, down, gate_fan, down_fan):
+    _, pair, hid, wide = gate_up.shape
+    cuts = 2 if hid % 32 == 0 else 1
+    rows = hid // cuts
+    pieces = [(i, c) for i in range(pair + 1) for c in range(cuts)]
+
+    def body(gu_ref, dn_ref, gu_weight, dn_weight, gu_slope, dn_slope, latent, sems):
+        copies = []
+        for n, (i, c) in enumerate(pieces):
+            at = pl.ds(c * rows, rows)
+            source = gu_ref.at[0, i, at] if i < pair else dn_ref.at[0, at]
+            copies.append(pltpu.make_async_copy(source, latent.at[n], sems.at[n]))
+            copies[-1].start()
+        for n, (i, c) in enumerate(pieces):
+            copies[n].wait()
+            at = pl.ds(c * rows, rows)
+            if i < pair:
+                gu_weight[i, at], gu_slope[i, at] = soften(latent[n], gate_fan)
+            else:
+                dn_weight[at], dn_slope[at] = soften(latent[n], down_fan)
+
+    return pl.pallas_call(
+        body,
+        in_specs=[pl.BlockSpec(memory_space=pltpu.HBM) for _ in range(2)],
+        out_specs=[whole() for _ in range(4)],
+        out_shape=[
+            like((pair, hid, wide), jnp.bfloat16),
+            like((hid, wide), jnp.bfloat16),
+            like((pair, hid, wide), jnp.float32),
+            like((hid, wide), jnp.float32),
+        ],
+        scratch_shapes=[
+            pltpu.VMEM((len(pieces), rows, wide), jnp.float32),
+            pltpu.SemaphoreType.DMA((len(pieces),)),
+        ],
+        compiler_params=pltpu.CompilerParams(vmem_limit_bytes=8 * MEBI),
+        name="soften_all",
+    )(pltpu.with_memory_space_constraint(gate_up, pltpu.HBM), pltpu.with_memory_space_constraint(down, pltpu.HBM))
+
+
+def forward(rep, mine, theirs, gu_weight, dn_weight):
+    hid = dn_weight.shape[0]
+    rows, part = mine.shape
+
+    def body(rep_ref, mine_ref, theirs_ref, gu_ref, dn_ref, hidden, by_gate, by_up, keep, send):
+        here, there = halves(rep_ref, part)
+        x_mine = mine_ref[...]
+        x_theirs = theirs_ref[...]
+
+        def project(which):
+            return dot(gu_ref[which, :, pl.ds(here, part)], x_mine, 1, 1) + dot(
+                gu_ref[which, :, pl.ds(there, part)], x_theirs, 1, 1
+            )
+
+        pre_gate = project(0)
+        pre_up = project(1)
+        sigmoid_gate = jax.nn.sigmoid(pre_gate)
+        activated = pre_gate * sigmoid_gate
+        rounded = (activated * pre_up).astype(jnp.bfloat16)
+        send[...] = dot(rounded, dn_ref[:, pl.ds(there, part)], 0, 0).astype(jnp.bfloat16)
+        keep[...] = dot(rounded, dn_ref[:, pl.ds(here, part)], 0, 0)
+        hidden[...] = rounded
+        by_gate[...] = pre_up * sigmoid_gate * (1.0 + pre_gate * (1.0 - sigmoid_gate))
+        by_up[...] = activated
+
+    return pl.pallas_call(
+        body,
+        in_specs=[pl.BlockSpec(memory_space=pltpu.SMEM)] + [whole() for _ in range(4)],
+        out_specs=[whole() for _ in range(5)],
+        out_shape=[
+            like((hid, rows), jnp.bfloat16),
+            like((hid, rows), jnp.float32),
+            like((hid, rows), jnp.float32),
+            like((rows, part), jnp.float32),
+            like((rows, part), jnp.bfloat16),
+        ],
+        compiler_params=pltpu.CompilerParams(vmem_limit_bytes=8 * MEBI),
+        name="forward",
+    )(rep, mine, theirs, gu_weight, dn_weight)
+
+
+def pack(keeps, arrivals, depth):
+    width = len(keeps)
+    rows, part = keeps[0].shape
+    block = rows // depth
+
+    def body(*refs):
+        for j in range(width):
+            total = (refs[j][...] + refs[width + j][...].astype(jnp.float32)).astype(jnp.bfloat16)
+            for k in range(depth):
+                refs[2 * width + k][j * block : (j + 1) * block, :] = total[
+                    k * block : (k + 1) * block
+                ]
+
+    return pl.pallas_call(
+        body,
+        in_specs=[whole() for _ in range(2 * width)],
+        out_specs=[whole() for _ in range(depth)],
+        out_shape=[like((width * block, part), jnp.bfloat16) for _ in range(depth)],
+        compiler_params=pltpu.CompilerParams(vmem_limit_bytes=4 * MEBI),
+        name="pack",
+    )(*keeps, *arrivals)
+
+
+def mix(gate, picked, teacher):
+    rows, part = picked[0].shape
+    own = teacher.shape[0]
+
+    def body(*refs):
+        gate_ref, teacher_ref = refs[:2]
+        total_ref, sent_ref = refs[-2:]
+        gates = gate_ref[...]
+        total = 0.0
+        for k, ref in enumerate(refs[2:-2]):
+            total = total + gates[:, k : k + 1] * ref[...].astype(jnp.float32)
+        total_ref[...] = total
+        sent_ref[:own, :] = (total[:own] - teacher_ref[...].astype(jnp.float32)).astype(
+            jnp.bfloat16
+        )
+        sent_ref[own:, :] = total[own:].astype(jnp.bfloat16)
+
+    return pl.pallas_call(
+        body,
+        in_specs=[whole() for _ in range(2 + len(picked))],
+        out_specs=[whole(), whole()],
+        out_shape=[like((rows, part), jnp.float32), like((rows, part), jnp.bfloat16)],
+        compiler_params=pltpu.CompilerParams(vmem_limit_bytes=4 * MEBI),
+        name="mix",
+    )(gate, teacher, *picked)
+
+
+def upstream(gate, total, arrivals, teacher, depth):
+    rows, part = total.shape
+    own = teacher.shape[0]
+    width = rows // own
+
+    def body(*refs):
+        gate_ref, teacher_ref, total_ref = refs[:3]
+        arrived = refs[3 : 3 + len(arrivals)]
+        outs = refs[3 + len(arrivals) :]
+        gates = gate_ref[...]
+        for j in range(width):
+            at = slice(j * own, (j + 1) * own)
+            residual = total_ref[at, :]
+            for step in range(1, width):
+                source = back(j, step, width)
+                residual = residual + arrived[step - 1][
+                    source * own : (source + 1) * own, :
+                ].astype(jnp.float32)
+            if j == 0:
+                residual = residual - teacher_ref[...].astype(jnp.float32)
+            for k in range(depth):
+                outs[k][at, :] = (gates[at, k : k + 1] * residual).astype(jnp.bfloat16)
+
+    return pl.pallas_call(
+        body,
+        in_specs=[whole() for _ in range(3 + len(arrivals))],
+        out_specs=[whole() for _ in range(depth)],
+        out_shape=[like((rows, part), jnp.bfloat16) for _ in range(depth)],
+        compiler_params=pltpu.CompilerParams(vmem_limit_bytes=4 * MEBI),
+        name="upstream",
+    )(gate, teacher, total, *arrivals)
+
+
+def backward(rep, grads, rows_of, factors, weights, slopes, latents):
+    gate_up, down = latents
+    _, pair, hid, wide = gate_up.shape
+    width = len(factors)
+    depth = len(grads[0])
+    part = grads[0][0].shape[1]
+    block = grads[0][0].shape[0] // width
+    flat = [*grads[0], grads[1], *rows_of[0], *rows_of[1]]
+    for triple in factors:
+        flat.extend(triple)
+    flat.extend([weights, *slopes, gate_up, down])
+
+    def body(*refs):
+        refs = list(refs)
+        rep_ref = refs.pop(0)
+        mine_refs = [refs.pop(0) for _ in range(depth)]
+        theirs_ref = refs.pop(0)
+        x_mine = [refs.pop(0) for _ in range(width)]
+        x_theirs = [refs.pop(0) for _ in range(width)]
+        triples = [[refs.pop(0) for _ in range(3)] for _ in range(width)]
+        dn_weight, gu_slope, dn_slope, gu_ref, dn_ref = [refs.pop(0) for _ in range(5)]
+        gu_out, dn_out, gu_new, dn_new, sems = refs
+        here, there = halves(rep_ref, part)
+        at_of = (here, there)
+
+        def group(which, j):
+            at = slice(j * block, (j + 1) * block)
+            if which == 0:
+                return jnp.concatenate([ref[at, :] for ref in mine_refs], axis=0)
+            rows = width * block
+            return jnp.concatenate(
+                [theirs_ref[k * rows + j * block : k * rows + (j + 1) * block, :] for k in range(depth)],
+                axis=0,
+            )
+
+        groups = [[group(which, j) for j in range(width)] for which in range(2)]
+        copies = []
+
+        def send(source, target, sem):
+            copy = pltpu.make_async_copy(source, target, sem)
+            copy.start()
+            copies.append(copy)
+
+        for which in range(2):
+            at = pl.ds(at_of[which], part)
+            grad = sum(dot(triples[j][0][...], groups[which][j], 1, 0) for j in range(width))
+            dn_new[which] = dn_ref[0, :, at] - dn_slope[:, at] * grad
+            send(dn_new.at[which], dn_out.at[0, :, at], sems.at[2 * pair + which])
+        row_grads = []
+        for j in range(width):
+            hidden_grad = dot(dn_weight[:, pl.ds(here, part)], groups[0][j], 1, 1) + dot(
+                dn_weight[:, pl.ds(there, part)], groups[1][j], 1, 1
+            )
+            row_grads.append(
+                [(hidden_grad * triples[j][1 + i][...]).astype(jnp.bfloat16) for i in range(pair)]
+            )
+        for i in range(pair):
+            for which in range(2):
+                at = pl.ds(at_of[which], part)
+                rows = (x_mine, x_theirs)[which]
+                grad = sum(dot(row_grads[j][i], rows[j][...], 1, 0) for j in range(width))
+                gu_new[i, which] = gu_ref[0, i, :, at] - gu_slope[i, :, at] * grad
+                send(gu_new.at[i, which], gu_out.at[0, i, :, at], sems.at[2 * i + which])
+        for copy in copies:
+            copy.wait()
+
+    return pl.pallas_call(
+        body,
+        in_specs=[pl.BlockSpec(memory_space=pltpu.SMEM)] + [whole() for _ in flat],
+        out_specs=[pl.BlockSpec(memory_space=pl.ANY), pl.BlockSpec(memory_space=pl.ANY)],
+        out_shape=[like(gate_up.shape, jnp.float32), like(down.shape, jnp.float32)],
+        scratch_shapes=[
+            pltpu.VMEM((pair, 2, hid, part), jnp.float32),
+            pltpu.VMEM((2, hid, part), jnp.float32),
+            pltpu.SemaphoreType.DMA((2 * pair + 2,)),
+        ],
+        compiler_params=pltpu.CompilerParams(vmem_limit_bytes=8 * MEBI),
+        name="backward",
+    )(rep, *flat)
+
+
+def dense_step(tokens, teacher, expert_ids, gate_codes, gate_up_latent, down_latent):
+    depth = lax.axis_size("inner")
+    width = lax.axis_size("outer")
+    reps = lax.axis_size("rep")
+    tok_rows, part_width = tokens.shape
+    rep = lax.axis_index("rep").astype(jnp.int32)[None]
+    inner = lax.axis_index("inner")
+    outer = lax.axis_index("outer")
+    f32 = jnp.float32
+    bf16 = jnp.bfloat16
+    tokens, rep, inner, outer = lax.optimization_barrier((tokens, rep, inner, outer))
+
+    def over_inner(messages, way):
+        arrived = {k: shift(messages[k], "inner", k, way) for k in in_order(depth)}
+        return [arrived[k] for k in range(depth)]
+
+    def code_of(column):
+        expert = ahead(inner, jnp.arange(depth, dtype=jnp.int32), depth) * width + column
+        chosen = expert_ids[None] == expert[:, None, None]
+        return jnp.sum(jnp.where(chosen, gate_codes[None], 0), axis=2)
+
+    blocks = over_inner([tokens] * depth, ahead)
+    softened = soften_all(
+        gate_up_latent, down_latent, part_width * reps, down_latent.shape[1] * reps
+    )
+    blocks[-1], *softened = lax.optimization_barrier((blocks[-1], *softened))
+    gu_weight, dn_weight, gu_slope, dn_slope = softened
+
+    tok_groups = [jnp.concatenate(blocks, axis=0)]
+    code_groups = [code_of(outer)]
+    pad_rows = -depth % 8
+    for j in range(1, width):
+        codes = code_of(ahead(outer, j, width))
+        pieces = jnp.concatenate([codes // 256, codes % 256], axis=1).astype(bf16)
+        pieces = jnp.pad(pieces, ((0, pad_rows), (0, part_width - 2 * tok_rows)))
+        arrived = shift(jnp.concatenate([tok_groups[0], pieces], axis=0), "outer", j)
+        tok_groups.append(arrived[: depth * tok_rows])
+        pieces = arrived[depth * tok_rows : depth * tok_rows + depth].astype(f32)
+        code_groups.append(256.0 * pieces[:, :tok_rows] + pieces[:, tok_rows : 2 * tok_rows])
+    gate = jnp.concatenate([c.astype(f32) for c in code_groups], axis=1) / 65536.0
+    gate = upright(jnp.pad(gate, ((0, -depth % 8), (0, -gate.shape[1] % 128))))
+    gate = gate[: width * tok_rows]
+
+    their_groups, factors, keeps, arrivals = [], [], [], []
+    for group in tok_groups:
+        theirs = other_rep(group)
+        hidden, by_gate, by_up, keep, send = forward(rep, group, theirs, gu_weight, dn_weight)
+        their_groups.append(theirs)
+        factors.append((hidden, by_gate, by_up))
+        keeps.append(keep)
+        arrivals.append(other_rep(send))
+    messages = pack(keeps, arrivals, depth)
+
+    picked = over_inner(messages, back)
+    total, sent = mix(gate, picked, teacher)
+    arrivals = [shift(sent, "outer", step) for step in range(1, width)]
+    outgoing = upstream(gate, total, arrivals, teacher, depth)
+    grads = over_inner(outgoing, ahead)
+    total, *arrivals, last = lax.optimization_barrier((total, *arrivals, grads[-1]))
+    grads[-1] = last
+    mixed = total[:tok_rows]
+    for step in range(1, width):
+        source = back(0, step, width)
+        mixed = mixed + arrivals[step - 1][source * tok_rows : (source + 1) * tok_rows].astype(f32)
+    student_out = mixed.astype(bf16)
+
+    their_grads = other_rep(jnp.concatenate(grads, axis=0))
+    new_gate_up, new_down = backward(
+        rep,
+        (grads, their_grads),
+        (tok_groups, their_groups),
+        factors,
+        dn_weight,
+        (gu_slope, dn_slope),
+        (gate_up_latent, down_latent),
+    )
+    return (student_out, new_gate_up, new_down)
+
+
+def routed_step(tokens, teacher, expert_ids, gate_codes, gate_up_latent, down_latent):
     experts = lax.axis_size("inner") * lax.axis_size("outer")
+    reps = lax.axis_size("rep")
     tok_rows, top_count = expert_ids.shape
     part_width = tokens.shape[1]
     capacity = min(tok_rows, 2 * tok_rows * top_count // experts)
@@ -47,10 +422,10 @@
     target = flat_ids * capacity + route_slot
     payload = jnp.repeat(tokens, top_count, axis=0)
     outbox = jnp.zeros((experts * capacity, part_width), jnp.bfloat16).at[target].set(payload)
-    received = dispatch_rows(outbox)
+    received = exchange(outbox)
     expert_rows = lax.all_gather(received, "rep", axis=1, tiled=True)
-    gu_weight, gu_slope = soften(gate_up_latent[0], D)
-    dn_weight, dn_slope = soften(down_latent[0], HID)
+    gu_weight, gu_slope = soften(gate_up_latent[0], part_width * reps)
+    dn_weight, dn_slope = soften(down_latent[0], down_latent.shape[1] * reps)
     projected = lax.dot_general(
         gu_weight, expert_rows, (((2,), (1,)), ((), ())), preferred_element_type=jnp.float32
     )
@@ -61,11 +436,14 @@
     hidden = (activated * pre_up).astype(jnp.bfloat16)
     partial_out = lax.dot_general(
         hidden, dn_weight, (((0,), (0,)), ((), ())), preferred_element_type=jnp.float32
-    )
-    expert_out = lax.psum_scatter(
-        partial_out.astype(jnp.bfloat16), "rep", scatter_dimension=1, tiled=True
-    )
-    returned = combine_rows(expert_out)
+    ).astype(jnp.bfloat16)
+    rep = lax.axis_index("rep")
+    keep = lax.dynamic_slice_in_dim(partial_out, rep * part_width, part_width, 1)
+    send = lax.dynamic_slice_in_dim(partial_out, (1 - rep) * part_width, part_width, 1)
+    expert_out = (keep.astype(jnp.float32) + other_rep(send).astype(jnp.float32)).astype(
+        jnp.bfloat16
+    )
+    returned = exchange(expert_out)
     picked = returned[target].reshape(tok_rows, top_count, part_width)
     gating = gate_codes.astype(jnp.float32) / 65536.0
     mixed = jnp.sum(gating[:, :, None] * picked.astype(jnp.float32), axis=1)
@@ -77,7 +455,7 @@
     grad_outbox = (
         jnp.zeros((experts * capacity, part_width), jnp.bfloat16).at[target].set(pair_grad)
     )
-    grad_part = upstream_rows(grad_outbox)
+    grad_part = exchange(grad_outbox)
     out_grad = lax.all_gather(grad_part, "rep", axis=1, tiled=True)
     down_grad = jnp.dot(hidden, out_grad, preferred_element_type=jnp.float32)
     hidden_grad = lax.dot_general(
@@ -96,6 +474,12 @@
     new_gate_up = gate_up_latent - learn_rate * (gu_slope * weight_grads)[None]
     new_down = down_latent - learn_rate * (dn_slope * down_grad)[None]
     return (student_out, new_gate_up, new_down)
+
+
+def on_device(tokens, teacher, expert_ids, gate_codes, gate_up_latent, down_latent):
+    experts = lax.axis_size("inner") * lax.axis_size("outer")
+    step = dense_step if expert_ids.shape[1] == experts else routed_step
+    return step(tokens, teacher, expert_ids, gate_codes, gate_up_latent, down_latent)
 
 
 def solution(mesh):

time: 86.4 us -> 46.5 us (0.54)
  blocking collectives: 16.7 us -> 0 us
  between operations: 14.2 us -> 0.81 us
  matrix products: 7.07 us -> 0 us
  Pallas kernels: 0 us -> 6.83 us
  waiting for transfers between devices: 23.3 us -> 17.6 us
  starting transfers between devices: 13.2 us -> 18.5 us
  local copies, waits for them, and re-layouts: 5.57 us -> 0.83 us
  other arithmetic: 5.84 us -> 1.69 us
    ppermute x0 -> x16, starting transfers between devices: none -> 18.5 us  [shift(): return lax.ppermute(x, axis, [(i, way(i, step, size)) for i in range(size)])]
    ppermute x0 -> x16, waiting for transfers between devices: none -> 17.6 us  [shift(): return lax.ppermute(x, axis, [(i, way(i, step, size)) for i in range(size)])]
    all_to_all x2 -> x0, waiting for transfers between devices: 16.2 us -> none  [the longest x1 9.22 us: combine_rows(): lax.all_to_all(outbox, ('inner', 'outer'), split_axis=0, concat_axis=0, t...]
    all_to_all x2 -> x0, starting transfers between devices: 13.1 us -> none  [the longest x1 7.28 us: dispatch_rows(): lax.all_to_all(outbox, ('inner', 'outer'), split_axis=0, concat_axis=0, t...]
    all_to_all x1 -> x0, blocking collectives: 12.4 us -> none  [upstream_rows(): lax.all_to_all(outbox, ('inner', 'outer'), split_axis=0, concat_axis=0, t...]
    reduce_scatter x1 -> x0, waiting for transfers between devices: 7.13 us -> none  [on_device(): lax.psum_scatter(partial_out.astype(jnp.bfloat16), 'rep', scatter_dimensi...]
    dot_general x5 -> x0, matrix products: 7.07 us -> none  [the longest x1 2 us: on_device(): lax.dot_general(jnp.stack([gate_grad, up_grad]), expert_rows, (((2,), (0,...]
    pallas_call x0 -> x8, Pallas kernels: none -> 6.83 us  [the longest x1 3.15 us: soften_all(): pl.pallas_call(body, in_specs=[pl.BlockSpec(memory_space=pltpu.HBM) for _...]
  transfers between devices with their start and end apart: 3 -> 16, of which waited for: 3 -> 11; matrix products, arithmetic and copies ran while one was open for 2% -> 5% of each run, Pallas kernels for 0% -> 10%
where the time goes in v3:
time: 46.5 us; the launch traced here: 46.2 us
  starting transfers between devices  18.5 us (40%)
  waiting for transfers between devices  17.6 us (38%)
  Pallas kernels  6.83 us (15%)
  other arithmetic  1.69 us (4%)
  local copies, waits for them, and re-layouts  0.83 us (2%)
  between operations  0.81 us (2%)
    ppermute x16, starting transfers between devices, shift(): return lax.ppermute(x, axis, [(i, way(i, step, size)) for i in range(size)])  18.5 us
    ppermute x16, waiting for transfers between devices, shift(): return lax.ppermute(x, axis, [(i, way(i, step, size)) for i in range(size)])  17.6 us
    pallas_call x1, Pallas kernels, soften_all(): pl.pallas_call(body, in_specs=[pl.BlockSpec(memory_space=pltpu.HBM) for _...  3.15 us
    pallas_call x1, Pallas kernels, backward(): pl.pallas_call(body, in_specs=[pl.BlockSpec(memory_space=pltpu.SMEM)] + [...  2.08 us
    pallas_call x2, Pallas kernels, forward(): pl.pallas_call(body, in_specs=[pl.BlockSpec(memory_space=pltpu.SMEM)] + [...  1.22 us
  transfers between devices with their start and end apart: 16, of which 11 were waited for; matrix products, arithmetic and copies ran while one was open for 5% of the time, Pallas kernels for 10%

profile of v3, /device:TPU:0, one launch (start us, length us, event | category | flops | bytes accessed | tf_op | source)
XLA Modules:
  0.0 46.2 jit_solution(6210916295950943275)
XLA Ops:
  0.6 5.1 %collective-permute-start.2 = (bf16[32,512]{1,0:T(8,128)(2,1)}, bf16[32,512]{1,0:T(8,128)(2,1)S(1)}, u32[]{:S(2)}, u32[]{:S(2)}) collective-permute-start(bf16[32,512]{1,0:T(8,128)(2,1)} %param.6), channel_id=1, source_target_pairs={{0,12},{4,8},{8,4},{12,0},{1,13},{5,9},{9,5},{13,1},{2,14},{6,10},... | collective-permute-start | bytes 98312 | tf_op jit(solution)/shard_map/ppermute | solution.py:36
  5.8 0.0 collective-permute-start.1
  5.8 0.6 %collective-permute-start = (bf16[32,512]{1,0:T(8,128)(2,1)}, bf16[32,512]{1,0:T(8,128)(2,1)S(1)}, u32[]{:S(2)}, u32[]{:S(2)}) collective-permute-start(bf16[32,512]{1,0:T(8,128)(2,1)} %param.6), channel_id=1, source_target_pairs={{0,4},{4,0},{8,12},{12,8},{1,5},{5,1},{9,13},{13,9},{2,6},{6,2},{1... | collective-permute-start | bytes 98312 | tf_op jit(solution)/shard_map/ppermute | solution.py:36
  6.4 0.8 %select_reduce_fusion.1 = (s32[4,32]{1,0:T(4,128)S(1)}, s32[4,32]{1,0:T(4,128)S(1)}) fusion(s32[32,8]{0,1:T(8,128)} %param.9, s32[32,8]{0,1:T(8,128)} %param.8, s32[4]{0:T(128)S(1)} %get-tuple-element.92, s32[4]{0:T(128)S(1)} %get-tuple-element.91), kind=kLoop, calls=%fused_computation.17 | loop fusion | flops 5888 | bytes 3104 | tf_op jit(solution)/shard_map/reduce_sum | solution.py:352
  7.2 0.8 %constant_dynamic-update-slice_fusion.8 = (bf16[128,512]{1,0:T(8,128)(2,1)S(1)}, bf16[136,512]{1,0:T(8,128)(2,1)S(1)}) fusion(bf16[32,512]{1,0:T(8,128)(2,1)} %param.6), kind=kLoop, calls=%fused_computation.10 | loop fusion | bytes 98304
  8.0 3.1 %soften_all.1 = (bf16[2,192,1024]{2,1,0:T(8,128)(2,1)S(1)}, bf16[192,1024]{1,0:T(8,128)(2,1)S(1)}, f32[2,192,1024]{2,1,0:T(8,128)S(1)}, f32[192,1024]{1,0:T(8,128)S(1)}) custom-call(f32[1,2,192,1024]{3,2,1,0:T(8,128)} %refs_19_.1, f32[1,192,1024]{2,1,0:T(8,128)} %refs_20_.1), custom_call_target="tpu_custom_call" | custom-call | tf_op jit(solution)/shard_map/soften_all/pallas_call | solution.py:109
  11.2 0.0 collective-permute-done
  11.2 0.0 collective-permute-done.2
  11.2 0.0 collective-permute-done.1
  11.2 0.1 constant_dynamic-update-slice_fusion
  11.3 1.6 %collective-permute-start.3 = (bf16[136,512]{1,0:T(8,128)(2,1)S(1)}, bf16[136,512]{1,0:T(8,128)(2,1)S(1)}, u32[]{:S(2)}, u32[]{:S(2)}) collective-permute-start(bf16[136,512]{1,0:T(8,128)(2,1)S(1)} %constant_dynamic-update-slice_fusion), channel_id=1, source_target_pairs={{0,2},{2,0},{1,3},{3,1},{4,6},{6,4},{5,7},{7,5},{8,10},{10,8},{9,1... | collective-permute-start | bytes 417800 | tf_op jit(solution)/shard_map/ppermute | solution.py:36
  13.0 0.0 collective-permute-start.4
  13.0 1.3 %collective-permute-done.4.theirs_ref.refs_8_ = bf16[128,512]{1,0:T(8,128)(2,1)S(1)} collective-permute-done((bf16[128,512]{1,0:T(8,128)(2,1)S(1)}, bf16[128,512]{1,0:T(8,128)(2,1)S(1)}, u32[]{:S(2)}, u32[]{:S(2)}) %collective-permute-start.4) | collective-permute-done | bytes 131104 | tf_op jit(solution)/shard_map/ppermute | solution.py:36
  14.3 0.6 %forward.2 = (bf16[192,128]{1,0:T(8,128)(2,1)S(1)}, f32[192,128]{1,0:T(8,128)S(1)}, f32[192,128]{1,0:T(8,128)S(1)}, f32[128,512]{1,0:T(8,128)S(1)}, bf16[128,512]{1,0:T(8,128)(2,1)S(1)}) custom-call(s32[1]{0:T(128)} %bitcast.rep_ref.refs_0_, bf16[128,512]{1,0:T(8,128)(2,1)S(1)} %get-tuple-element.81.mine_ref.refs_6_, ...), custom_call_target="tpu_custom_call" | custom-call | tf_op jit(solution)/shard_map/forward/pallas_call | solution.py:153
  14.9 0.0 copy-start.2
  14.9 0.2 collective-permute-start.6
  15.1 1.2 %collective-permute-done.3 = bf16[136,512]{1,0:T(8,128)(2,1)S(1)} collective-permute-done((bf16[136,512]{1,0:T(8,128)(2,1)S(1)}, bf16[136,512]{1,0:T(8,128)(2,1)S(1)}, u32[]{:S(2)}, u32[]{:S(2)}) %collective-permute-start.3) | collective-permute-done | bytes 139296 | tf_op jit(solution)/shard_map/ppermute | solution.py:36
  16.4 0.1 collective-permute-start.5
  16.5 0.0 copy-start
  16.5 0.0 copy-start.1
  16.5 1.3 %collective-permute-done.5.theirs_ref.refs_9_ = bf16[128,512]{1,0:T(8,128)(2,1)S(1)} collective-permute-done((bf16[128,512]{1,0:T(8,128)(2,1)S(1)}, bf16[128,512]{1,0:T(8,128)(2,1)S(1)}, u32[]{:S(2)}, u32[]{:S(2)}) %collective-permute-start.5) | collective-permute-done | bytes 131104 | tf_op jit(solution)/shard_map/ppermute | solution.py:36
  17.8 0.6 %forward.3 = (bf16[192,128]{1,0:T(8,128)(2,1)S(1)}, f32[192,128]{1,0:T(8,128)S(1)}, f32[192,128]{1,0:T(8,128)S(1)}, f32[128,512]{1,0:T(8,128)S(1)}, bf16[128,512]{1,0:T(8,128)(2,1)S(1)}) custom-call(s32[1]{0:T(128)} %bitcast.rep_ref.refs_0_, bf16[128,512]{1,0:T(8,128)(2,1)S(1)} %slice.32.mine_ref.refs_7_, ...), custom_call_target="tpu_custom_call" | custom-call | tf_op jit(solution)/shard_map/forward/pallas_call | solution.py:153
  18.4 0.2 collective-permute-start.7
  18.6 0.1 slice_add_fusion
  18.7 0.0 collective-permute-done.6.refs_2_
  18.7 1.1 %collective-permute-done.7.refs_3_ = bf16[128,512]{1,0:T(8,128)(2,1)S(1)} collective-permute-done((bf16[128,512]{1,0:T(8,128)(2,1)S(1)}, bf16[128,512]{1,0:T(8,128)(2,1)S(1)}, u32[]{:S(2)}, u32[]{:S(2)}) %collective-permute-start.7) | collective-permute-done | bytes 131104 | tf_op jit(solution)/shard_map/ppermute | solution.py:36
  19.9 1.4 %collective-permute-start.8 = (bf16[64,512]{1,0:T(8,128)(2,1)S(1)}, bf16[64,512]{1,0:T(8,128)(2,1)S(1)}, u32[]{:S(2)}, u32[]{:S(2)}) collective-permute-start(bf16[64,512]{1,0:T(8,128)(2,1)S(1)} %get-tuple-element.57), channel_id=1, source_target_pairs={{0,4},{4,0},{8,12},{12,8},{1,5},{5,1},{9,13},{13,9},{2,6},{6,2},{1... | collective-permute-start | bytes 196616 | tf_op jit(solution)/shard_map/ppermute | solution.py:36
  21.3 2.9 %collective-permute-start.9 = (bf16[64,512]{1,0:T(8,128)(2,1)S(1)}, bf16[64,512]{1,0:T(8,128)(2,1)S(1)}, u32[]{:S(2)}, u32[]{:S(2)}) collective-permute-start(bf16[64,512]{1,0:T(8,128)(2,1)S(1)} %get-tuple-element.58), channel_id=1, source_target_pairs={{0,8},{4,12},{8,0},{12,4},{1,9},{5,13},{9,1},{13,5},{2,10},{6,14},... | collective-permute-start | bytes 196616 | tf_op jit(solution)/shard_map/ppermute | solution.py:36
  24.3 0.1 collective-permute-start.10
  24.3 0.1 maximum_multiply_fusion
  24.4 0.1 upright.1
  24.5 0.0 collective-permute-done.8.refs_3_
  24.5 3.7 %collective-permute-done.9.refs_4_ = bf16[64,512]{1,0:T(8,128)(2,1)S(1)} collective-permute-done((bf16[64,512]{1,0:T(8,128)(2,1)S(1)}, bf16[64,512]{1,0:T(8,128)(2,1)S(1)}, u32[]{:S(2)}, u32[]{:S(2)}) %collective-permute-start.9) | collective-permute-done | bytes 65568 | tf_op jit(solution)/shard_map/ppermute | solution.py:36
  28.3 2.1 %collective-permute-done.10.refs_5_ = bf16[64,512]{1,0:T(8,128)(2,1)S(1)} collective-permute-done((bf16[64,512]{1,0:T(8,128)(2,1)S(1)}, bf16[64,512]{1,0:T(8,128)(2,1)S(1)}, u32[]{:S(2)}, u32[]{:S(2)}) %collective-permute-start.10) | collective-permute-done | bytes 65568 | tf_op jit(solution)/shard_map/ppermute | solution.py:36
  30.4 0.0 copy-done.2
  30.4 0.1 mix.1
  30.6 1.6 %collective-permute-start.11 = (bf16[64,512]{1,0:T(8,128)(2,1)S(1)}, bf16[64,512]{1,0:T(8,128)(2,1)S(1)}, u32[]{:S(2)}, u32[]{:S(2)}) collective-permute-start(bf16[64,512]{1,0:T(8,128)(2,1)S(1)} %get-tuple-element.61), channel_id=1, source_target_pairs={{0,2},{2,0},{1,3},{3,1},{4,6},{6,4},{5,7},{7,5},{8,10},{10,8},{9,1... | collective-permute-start | bytes 196616 | tf_op jit(solution)/shard_map/ppermute | solution.py:36
  32.1 2.8 %collective-permute-done.11.refs_3_ = bf16[64,512]{1,0:T(8,128)(2,1)S(1)} collective-permute-done((bf16[64,512]{1,0:T(8,128)(2,1)S(1)}, bf16[64,512]{1,0:T(8,128)(2,1)S(1)}, u32[]{:S(2)}, u32[]{:S(2)}) %collective-permute-start.11) | collective-permute-done | bytes 65568 | tf_op jit(solution)/shard_map/ppermute | solution.py:36
  34.9 0.1 upstream.1
  35.0 2.0 %collective-permute-start.12 = (bf16[64,512]{1,0:T(8,128)(2,1)S(1)}, bf16[64,512]{1,0:T(8,128)(2,1)S(1)}, u32[]{:S(2)}, u32[]{:S(2)}) collective-permute-start(bf16[64,512]{1,0:T(8,128)(2,1)S(1)} %get-tuple-element.62), channel_id=1, source_target_pairs={{0,12},{4,8},{8,4},{12,0},{1,13},{5,9},{9,5},{13,1},{2,14},{6,10},... | collective-permute-start | bytes 196616 | tf_op jit(solution)/shard_map/ppermute | solution.py:36
  37.0 0.4 collective-permute-start.13
  37.3 2.1 %collective-permute-start.14 = (bf16[64,512]{1,0:T(8,128)(2,1)S(1)}, bf16[64,512]{1,0:T(8,128)(2,1)S(1)}, u32[]{:S(2)}, u32[]{:S(2)}) collective-permute-start(bf16[64,512]{1,0:T(8,128)(2,1)S(1)} %get-tuple-element.67), channel_id=1, source_target_pairs={{0,8},{4,12},{8,0},{12,4},{1,9},{5,13},{9,1},{13,5},{2,10},{6,14},... | collective-permute-start | bytes 196616 | tf_op jit(solution)/shard_map/ppermute | solution.py:36
  39.5 1.7 %collective-permute-done.12.refs_4_ = bf16[64,512]{1,0:T(8,128)(2,1)S(1)} collective-permute-done((bf16[64,512]{1,0:T(8,128)(2,1)S(1)}, bf16[64,512]{1,0:T(8,128)(2,1)S(1)}, u32[]{:S(2)}, u32[]{:S(2)}) %collective-permute-start.12) | collective-permute-done | bytes 65568 | tf_op jit(solution)/shard_map/ppermute | solution.py:36
  41.2 0.7 %collective-permute-done.13.refs_2_ = bf16[64,512]{1,0:T(8,128)(2,1)S(1)} collective-permute-done((bf16[64,512]{1,0:T(8,128)(2,1)S(1)}, bf16[64,512]{1,0:T(8,128)(2,1)S(1)}, u32[]{:S(2)}, u32[]{:S(2)}) %collective-permute-start.13) | collective-permute-done | bytes 65568 | tf_op jit(solution)/shard_map/ppermute | solution.py:36
  41.8 0.7 %collective-permute-done.14.refs_3_ = bf16[64,512]{1,0:T(8,128)(2,1)S(1)} collective-permute-done((bf16[64,512]{1,0:T(8,128)(2,1)S(1)}, bf16[64,512]{1,0:T(8,128)(2,1)S(1)}, u32[]{:S(2)}, u32[]{:S(2)}) %collective-permute-start.14) | collective-permute-done | bytes 65568 | tf_op jit(solution)/shard_map/ppermute | solution.py:36
  42.6 0.1 collective-permute-start.15
  42.6 0.6 %add_convert_fusion = bf16[32,512]{1,0:T(8,128)(2,1)} fusion(f32[64,512]{1,0:T(8,128)S(1)} %get-tuple-element.63.refs_2_, bf16[64,512]{1,0:T(8,128)(2,1)S(1)} %collective-permute-done.11.refs_3_), kind=kLoop, calls=%fused_computation.1 | loop fusion | flops 49152 | bytes 131072 | tf_op jit(solution)/shard_map/convert_element_type | solution.py:397
  43.3 0.9 %collective-permute-done.15.refs_5_ = bf16[256,512]{1,0:T(8,128)(2,1)S(1)} collective-permute-done((bf16[256,512]{1,0:T(8,128)(2,1)S(1)}, bf16[256,512]{1,0:T(8,128)(2,1)S(1)}, u32[]{:S(2)}, u32[]{:S(2)}) %collective-permute-start.15) | collective-permute-done | bytes 262176 | tf_op jit(solution)/shard_map/ppermute | solution.py:36
  44.2 0.0 copy-done
  44.2 0.0 copy-done.1
  44.2 2.1 %backward.1 = (f32[1,2,192,1024]{3,2,1,0:T(8,128)}, f32[1,192,1024]{2,1,0:T(8,128)}) custom-call(s32[1]{0:T(128)} %bitcast.rep_ref.refs_0_, bf16[64,512]{1,0:T(8,128)(2,1)S(1)} %get-tuple-element.65.refs_1_, bf16[64,512]{1,0:T(8,128)(2,1)S(1)} %collective-permute-done.13.refs_2_, bf16[64,512]{1,0:T(8,128)(2,1)S(1)} %collective-permute-done.14.refs_3_, ...), custom_call_target="tpu_custom_call" | custom-call | tf_op jit(solution)/shard_map/backward/pallas_call | solution.py:318
  (12 shorter events, 0.1 us)
Async XLA Ops:
  0.6 10.6 %collective-permute-start.2 = (bf16[32,512]{1,0:T(8,128)(2,1)}, bf16[32,512]{1,0:T(8,128)(2,1)S(1)}, u32[]{:S(2)}, u32[]{:S(2)}) collective-permute-start(bf16[32,512]{1,0:T(8,128)(2,1)} %param.6), channel_id=1, source_target_pairs={{0,12},{4,8},{8,4},{12,0},{1,13},{5,9},{9,5},{13,1},{2,14},{6,10},... | collective-permute-start | bytes 98312 | tf_op jit(solution)/shard_map/ppermute | solution.py:36
  5.8 5.4 %collective-permute-start.1 = (bf16[32,512]{1,0:T(8,128)(2,1)}, bf16[32,512]{1,0:T(8,128)(2,1)S(1)}, u32[]{:S(2)}, u32[]{:S(2)}) collective-permute-start(bf16[32,512]{1,0:T(8,128)(2,1)} %param.6), channel_id=1, source_target_pairs={{0,8},{4,12},{8,0},{12,4},{1,9},{5,13},{9,1},{13,5},{2,10},{6,14},... | collective-permute-start | bytes 98312 | tf_op jit(solution)/shard_map/ppermute | solution.py:36
  5.8 5.4 %collective-permute-start = (bf16[32,512]{1,0:T(8,128)(2,1)}, bf16[32,512]{1,0:T(8,128)(2,1)S(1)}, u32[]{:S(2)}, u32[]{:S(2)}) collective-permute-start(bf16[32,512]{1,0:T(8,128)(2,1)} %param.6), channel_id=1, source_target_pairs={{0,4},{4,0},{8,12},{12,8},{1,5},{5,1},{9,13},{13,9},{2,6},{6,2},{1... | collective-permute-start | bytes 98312 | tf_op jit(solution)/shard_map/ppermute | solution.py:36
  11.3 5.1 %collective-permute-start.3 = (bf16[136,512]{1,0:T(8,128)(2,1)S(1)}, bf16[136,512]{1,0:T(8,128)(2,1)S(1)}, u32[]{:S(2)}, u32[]{:S(2)}) collective-permute-start(bf16[136,512]{1,0:T(8,128)(2,1)S(1)} %constant_dynamic-update-slice_fusion), channel_id=1, source_target_pairs={{0,2},{2,0},{1,3},{3,1},{4,6},{6,4},{5,7},{7,5},{8,10},{10,8},{9,1... | collective-permute-start | bytes 417800 | tf_op jit(solution)/shard_map/ppermute | solution.py:36
  13.0 1.3 %collective-permute-start.4 = (bf16[128,512]{1,0:T(8,128)(2,1)S(1)}, bf16[128,512]{1,0:T(8,128)(2,1)S(1)}, u32[]{:S(2)}, u32[]{:S(2)}) collective-permute-start(bf16[128,512]{1,0:T(8,128)(2,1)S(1)} %get-tuple-element.81.mine_ref.refs_6_), channel_id=1, source_target_pairs={{0,1},{1,0},{2,3},{3,2},{4,5},{5,4},{6,7},{7,6},{8,9},{9,8},{10,11... | collective-permute-start | bytes 393224 | tf_op jit(solution)/shard_map/ppermute | solution.py:36
  14.9 15.5 %copy-start.2 = (bf16[32,512]{1,0:T(8,128)(2,1)S(1)}, bf16[32,512]{1,0:T(8,128)(2,1)}, u32[]{:S(2)}) copy-start(bf16[32,512]{1,0:T(8,128)(2,1)} %refs_1_.3) | copy-start | bytes 98308
  14.9 3.8 %collective-permute-start.6 = (bf16[128,512]{1,0:T(8,128)(2,1)S(1)}, bf16[128,512]{1,0:T(8,128)(2,1)S(1)}, u32[]{:S(2)}, u32[]{:S(2)}) collective-permute-start(bf16[128,512]{1,0:T(8,128)(2,1)S(1)} %get-tuple-element.54), channel_id=1, source_target_pairs={{0,1},{1,0},{2,3},{3,2},{4,5},{5,4},{6,7},{7,6},{8,9},{9,8},{10,11... | collective-permute-start | bytes 393224 | tf_op jit(solution)/shard_map/ppermute | solution.py:36
  16.4 1.4 %collective-permute-start.5 = (bf16[128,512]{1,0:T(8,128)(2,1)S(1)}, bf16[128,512]{1,0:T(8,128)(2,1)S(1)}, u32[]{:S(2)}, u32[]{:S(2)}) collective-permute-start(bf16[128,512]{1,0:T(8,128)(2,1)S(1)} %slice.32.mine_ref.refs_7_), channel_id=1, source_target_pairs={{0,1},{1,0},{2,3},{3,2},{4,5},{5,4},{6,7},{7,6},{8,9},{9,8},{10,11... | collective-permute-start | bytes 393224 | tf_op jit(solution)/shard_map/ppermute | solution.py:36
  16.5 27.7 %copy-start = (f32[1,2,192,1024]{3,2,1,0:T(8,128)S(1)}, f32[1,2,192,1024]{3,2,1,0:T(8,128)}, u32[]{:S(2)}) copy-start(f32[1,2,192,1024]{3,2,1,0:T(8,128)} %refs_19_.1) | copy-start | bytes 4718596
  16.5 27.7 %copy-start.1 = (f32[1,192,1024]{2,1,0:T(8,128)S(1)}, f32[1,192,1024]{2,1,0:T(8,128)}, u32[]{:S(2)}) copy-start(f32[1,192,1024]{2,1,0:T(8,128)} %refs_20_.1) | copy-start | bytes 2359300
  18.4 1.4 %collective-permute-start.7 = (bf16[128,512]{1,0:T(8,128)(2,1)S(1)}, bf16[128,512]{1,0:T(8,128)(2,1)S(1)}, u32[]{:S(2)}, u32[]{:S(2)}) collective-permute-start(bf16[128,512]{1,0:T(8,128)(2,1)S(1)} %get-tuple-element.55), channel_id=1, source_target_pairs={{0,1},{1,0},{2,3},{3,2},{4,5},{5,4},{6,7},{7,6},{8,9},{9,8},{10,11... | collective-permute-start | bytes 393224 | tf_op jit(solution)/shard_map/ppermute | solution.py:36
  19.9 4.7 %collective-permute-start.8 = (bf16[64,512]{1,0:T(8,128)(2,1)S(1)}, bf16[64,512]{1,0:T(8,128)(2,1)S(1)}, u32[]{:S(2)}, u32[]{:S(2)}) collective-permute-start(bf16[64,512]{1,0:T(8,128)(2,1)S(1)} %get-tuple-element.57), channel_id=1, source_target_pairs={{0,4},{4,0},{8,12},{12,8},{1,5},{5,1},{9,13},{13,9},{2,6},{6,2},{1... | collective-permute-start | bytes 196616 | tf_op jit(solution)/shard_map/ppermute | solution.py:36
  21.3 6.9 %collective-permute-start.9 = (bf16[64,512]{1,0:T(8,128)(2,1)S(1)}, bf16[64,512]{1,0:T(8,128)(2,1)S(1)}, u32[]{:S(2)}, u32[]{:S(2)}) collective-permute-start(bf16[64,512]{1,0:T(8,128)(2,1)S(1)} %get-tuple-element.58), channel_id=1, source_target_pairs={{0,8},{4,12},{8,0},{12,4},{1,9},{5,13},{9,1},{13,5},{2,10},{6,14},... | collective-permute-start | bytes 196616 | tf_op jit(solution)/shard_map/ppermute | solution.py:36
  24.3 6.2 %collective-permute-start.10 = (bf16[64,512]{1,0:T(8,128)(2,1)S(1)}, bf16[64,512]{1,0:T(8,128)(2,1)S(1)}, u32[]{:S(2)}, u32[]{:S(2)}) collective-permute-start(bf16[64,512]{1,0:T(8,128)(2,1)S(1)} %get-tuple-element.59), channel_id=1, source_target_pairs={{0,12},{4,8},{8,4},{12,0},{1,13},{5,9},{9,5},{13,1},{2,14},{6,10},... | collective-permute-start | bytes 196616 | tf_op jit(solution)/shard_map/ppermute | solution.py:36
  30.6 4.3 %collective-permute-start.11 = (bf16[64,512]{1,0:T(8,128)(2,1)S(1)}, bf16[64,512]{1,0:T(8,128)(2,1)S(1)}, u32[]{:S(2)}, u32[]{:S(2)}) collective-permute-start(bf16[64,512]{1,0:T(8,128)(2,1)S(1)} %get-tuple-element.61), channel_id=1, source_target_pairs={{0,2},{2,0},{1,3},{3,1},{4,6},{6,4},{5,7},{7,5},{8,10},{10,8},{9,1... | collective-permute-start | bytes 196616 | tf_op jit(solution)/shard_map/ppermute | solution.py:36
  35.0 6.2 %collective-permute-start.12 = (bf16[64,512]{1,0:T(8,128)(2,1)S(1)}, bf16[64,512]{1,0:T(8,128)(2,1)S(1)}, u32[]{:S(2)}, u32[]{:S(2)}) collective-permute-start(bf16[64,512]{1,0:T(8,128)(2,1)S(1)} %get-tuple-element.62), channel_id=1, source_target_pairs={{0,12},{4,8},{8,4},{12,0},{1,13},{5,9},{9,5},{13,1},{2,14},{6,10},... | collective-permute-start | bytes 196616 | tf_op jit(solution)/shard_map/ppermute | solution.py:36
  37.0 4.9 %collective-permute-start.13 = (bf16[64,512]{1,0:T(8,128)(2,1)S(1)}, bf16[64,512]{1,0:T(8,128)(2,1)S(1)}, u32[]{:S(2)}, u32[]{:S(2)}) collective-permute-start(bf16[64,512]{1,0:T(8,128)(2,1)S(1)} %get-tuple-element.66), channel_id=1, source_target_pairs={{0,4},{4,0},{8,12},{12,8},{1,5},{5,1},{9,13},{13,9},{2,6},{6,2},{1... | collective-permute-start | bytes 196616 | tf_op jit(solution)/shard_map/ppermute | solution.py:36
  37.3 5.2 %collective-permute-start.14 = (bf16[64,512]{1,0:T(8,128)(2,1)S(1)}, bf16[64,512]{1,0:T(8,128)(2,1)S(1)}, u32[]{:S(2)}, u32[]{:S(2)}) collective-permute-start(bf16[64,512]{1,0:T(8,128)(2,1)S(1)} %get-tuple-element.67), channel_id=1, source_target_pairs={{0,8},{4,12},{8,0},{12,4},{1,9},{5,13},{9,1},{13,5},{2,10},{6,14},... | collective-permute-start | bytes 196616 | tf_op jit(solution)/shard_map/ppermute | solution.py:36
  42.6 1.6 %collective-permute-start.15 = (bf16[256,512]{1,0:T(8,128)(2,1)S(1)}, bf16[256,512]{1,0:T(8,128)(2,1)S(1)}, u32[]{:S(2)}, u32[]{:S(2)}) collective-permute-start(bf16[256,512]{1,0:T(8,128)(2,1)S(1)} %pad_maximum_fusion), channel_id=1, source_target_pairs={{0,1},{1,0},{2,3},{3,2},{4,5},{5,4},{6,7},{7,6},{8,9},{9,8},{10,11... | collective-permute-start | bytes 786440 | tf_op jit(solution)/shard_map/ppermute | solution.py:36

commit v4 on v3

--- a/solution.py
+++ b/solution.py
@@ -7,18 +7,29 @@
 from jax.experimental.pallas import tpu as pltpu
 from jax.sharding import PartitionSpec as P
 
+
 learn_rate = 1.0
 
 
-def soften(latent, fan_in):
+def soft_ternary(latent):
     row_scale = jnp.mean(jnp.abs(latent), axis=-1, keepdims=True) + 1e-06
     steep = latent * (4.0 / row_scale)
-    lower = jnp.tanh(steep - 2.0)
-    upper = jnp.tanh(steep + 2.0)
-    fan_root = 1.0 / math.sqrt(fan_in)
-    weight = ((row_scale * (0.5 * fan_root)) * (lower + upper)).astype(jnp.bfloat16)
-    slope = (4.0 * fan_root) - (2.0 * fan_root) * (lower * lower + upper * upper)
-    return (weight, slope)
+    return row_scale, jnp.tanh(steep - 2.0), jnp.tanh(steep + 2.0)
+
+
+def weight_of(latent, fan_in):
+    row_scale, lower, upper = soft_ternary(latent)
+    return (row_scale * (0.5 / math.sqrt(fan_in)) * (lower + upper)).astype(jnp.bfloat16)
+
+
+def slope_of(latent, fan_in):
+    _, lower, upper = soft_ternary(latent)
+    root = 2.0 / math.sqrt(fan_in)
+    return 2.0 * root - root * (lower * lower + upper * upper)
+
+
+def soften(latent, fan_in):
+    return weight_of(latent, fan_in), slope_of(latent, fan_in)
 
 
 def ahead(place, step, size):
@@ -34,10 +45,6 @@
     if step == 0:
         return x
     return lax.ppermute(x, axis, [(i, way(i, step, size)) for i in range(size)])
-
-
-def in_order(size):
-    return [k for k in (2, 1, 3) if k < size] + [0] + list(range(4, size))
 
 
 def other_rep(x):
@@ -85,48 +92,45 @@
     )(gate)
 
 
-def soften_all(gate_up, down, gate_fan, down_fan):
-    _, pair, hid, wide = gate_up.shape
-    cuts = 2 if hid % 32 == 0 else 1
-    rows = hid // cuts
-    pieces = [(i, c) for i in range(pair + 1) for c in range(cuts)]
-
-    def body(gu_ref, dn_ref, gu_weight, dn_weight, gu_slope, dn_slope, latent, sems):
+def per_entry(rule, latents, fans, dtype):
+    pieces = []
+    for n, latent in enumerate(latents):
+        cuts = 2 if latent.shape[-2] % 32 == 0 else 1
+        rows = latent.shape[-2] // cuts
+        lead = [()]
+        for size in latent.shape[:-2]:
+            lead = [(*at, i) for at in lead for i in range(size)]
+        pieces.extend((n, at, c * rows) for at in lead for c in range(cuts))
+    wide = latents[0].shape[-1]
+
+    def body(*refs):
+        sources = refs[: len(latents)]
+        targets = refs[len(latents) : -2]
+        held, sems = refs[-2:]
         copies = []
-        for n, (i, c) in enumerate(pieces):
-            at = pl.ds(c * rows, rows)
-            source = gu_ref.at[0, i, at] if i < pair else dn_ref.at[0, at]
-            copies.append(pltpu.make_async_copy(source, latent.at[n], sems.at[n]))
+        for slot, (n, at, row) in enumerate(pieces):
+            source = sources[n].at[(*at, pl.ds(row, rows))]
+            copies.append(pltpu.make_async_copy(source, held.at[slot], sems.at[slot]))
             copies[-1].start()
-        for n, (i, c) in enumerate(pieces):
-            copies[n].wait()
-            at = pl.ds(c * rows, rows)
-            if i < pair:
-                gu_weight[i, at], gu_slope[i, at] = soften(latent[n], gate_fan)
-            else:
-                dn_weight[at], dn_slope[at] = soften(latent[n], down_fan)
-
-    return pl.pallas_call(
-        body,
-        in_specs=[pl.BlockSpec(memory_space=pltpu.HBM) for _ in range(2)],
-        out_specs=[whole() for _ in range(4)],
-        out_shape=[
-            like((pair, hid, wide), jnp.bfloat16),
-            like((hid, wide), jnp.bfloat16),
-            like((pair, hid, wide), jnp.float32),
-            like((hid, wide), jnp.float32),
-        ],
+        for slot, (n, at, row) in enumerate(pieces):
+            copies[slot].wait()
+            targets[n][(*at, pl.ds(row, rows))] = rule(held[slot], fans[n])
+
+    return pl.pallas_call(
+        body,
+        in_specs=[pl.BlockSpec(memory_space=pltpu.HBM) for _ in latents],
+        out_specs=[whole() for _ in latents],
+        out_shape=[like(latent.shape, dtype) for latent in latents],
         scratch_shapes=[
             pltpu.VMEM((len(pieces), rows, wide), jnp.float32),
             pltpu.SemaphoreType.DMA((len(pieces),)),
         ],
         compiler_params=pltpu.CompilerParams(vmem_limit_bytes=8 * MEBI),
-        name="soften_all",
-    )(pltpu.with_memory_space_constraint(gate_up, pltpu.HBM), pltpu.with_memory_space_constraint(down, pltpu.HBM))
+    )(*[pltpu.with_memory_space_constraint(latent, pltpu.HBM) for latent in latents])
 
 
 def forward(rep, mine, theirs, gu_weight, dn_weight):
-    hid = dn_weight.shape[0]
+    hid = dn_weight.shape[1]
     rows, part = mine.shape
 
     def body(rep_ref, mine_ref, theirs_ref, gu_ref, dn_ref, hidden, by_gate, by_up, keep, send):
@@ -135,8 +139,8 @@
         x_theirs = theirs_ref[...]
 
         def project(which):
-            return dot(gu_ref[which, :, pl.ds(here, part)], x_mine, 1, 1) + dot(
-                gu_ref[which, :, pl.ds(there, part)], x_theirs, 1, 1
+            return dot(gu_ref[0, which, :, pl.ds(here, part)], x_mine, 1, 1) + dot(
+                gu_ref[0, which, :, pl.ds(there, part)], x_theirs, 1, 1
             )
 
         pre_gate = project(0)
@@ -144,8 +148,8 @@
         sigmoid_gate = jax.nn.sigmoid(pre_gate)
         activated = pre_gate * sigmoid_gate
         rounded = (activated * pre_up).astype(jnp.bfloat16)
-        send[...] = dot(rounded, dn_ref[:, pl.ds(there, part)], 0, 0).astype(jnp.bfloat16)
-        keep[...] = dot(rounded, dn_ref[:, pl.ds(here, part)], 0, 0)
+        send[...] = dot(rounded, dn_ref[0, :, pl.ds(there, part)], 0, 0).astype(jnp.bfloat16)
+        keep[...] = dot(rounded, dn_ref[0, :, pl.ds(here, part)], 0, 0)
         hidden[...] = rounded
         by_gate[...] = pre_up * sigmoid_gate * (1.0 + pre_gate * (1.0 - sigmoid_gate))
         by_up[...] = activated
@@ -251,12 +255,12 @@
 
 def backward(rep, grads, rows_of, factors, weights, slopes, latents):
     gate_up, down = latents
-    _, pair, hid, wide = gate_up.shape
+    _, pair, hid, _ = gate_up.shape
     width = len(factors)
     depth = len(grads[0])
     part = grads[0][0].shape[1]
     block = grads[0][0].shape[0] // width
-    flat = [*grads[0], grads[1], *rows_of[0], *rows_of[1]]
+    flat = [*grads[0], *grads[1], *rows_of[0], *rows_of[1]]
     for triple in factors:
         flat.extend(triple)
     flat.extend([weights, *slopes, gate_up, down])
@@ -265,7 +269,7 @@
         refs = list(refs)
         rep_ref = refs.pop(0)
         mine_refs = [refs.pop(0) for _ in range(depth)]
-        theirs_ref = refs.pop(0)
+        theirs_refs = [refs.pop(0) for _ in range(depth)]
         x_mine = [refs.pop(0) for _ in range(width)]
         x_theirs = [refs.pop(0) for _ in range(width)]
         triples = [[refs.pop(0) for _ in range(3)] for _ in range(width)]
@@ -276,13 +280,8 @@
 
         def group(which, j):
             at = slice(j * block, (j + 1) * block)
-            if which == 0:
-                return jnp.concatenate([ref[at, :] for ref in mine_refs], axis=0)
-            rows = width * block
-            return jnp.concatenate(
-                [theirs_ref[k * rows + j * block : k * rows + (j + 1) * block, :] for k in range(depth)],
-                axis=0,
-            )
+            refs_of = (mine_refs, theirs_refs)[which]
+            return jnp.concatenate([ref[at, :] for ref in refs_of], axis=0)
 
         groups = [[group(which, j) for j in range(width)] for which in range(2)]
         copies = []
@@ -295,12 +294,12 @@
         for which in range(2):
             at = pl.ds(at_of[which], part)
             grad = sum(dot(triples[j][0][...], groups[which][j], 1, 0) for j in range(width))
-            dn_new[which] = dn_ref[0, :, at] - dn_slope[:, at] * grad
+            dn_new[which] = dn_ref[0, :, at] - dn_slope[0, :, at] * grad
             send(dn_new.at[which], dn_out.at[0, :, at], sems.at[2 * pair + which])
         row_grads = []
         for j in range(width):
-            hidden_grad = dot(dn_weight[:, pl.ds(here, part)], groups[0][j], 1, 1) + dot(
-                dn_weight[:, pl.ds(there, part)], groups[1][j], 1, 1
+            hidden_grad = dot(dn_weight[0, :, pl.ds(here, part)], groups[0][j], 1, 1) + dot(
+                dn_weight[0, :, pl.ds(there, part)], groups[1][j], 1, 1
             )
             row_grads.append(
                 [(hidden_grad * triples[j][1 + i][...]).astype(jnp.bfloat16) for i in range(pair)]
@@ -310,7 +309,7 @@
                 at = pl.ds(at_of[which], part)
                 rows = (x_mine, x_theirs)[which]
                 grad = sum(dot(row_grads[j][i], rows[j][...], 1, 0) for j in range(width))
-                gu_new[i, which] = gu_ref[0, i, :, at] - gu_slope[i, :, at] * grad
+                gu_new[i, which] = gu_ref[0, i, :, at] - gu_slope[0, i, :, at] * grad
                 send(gu_new.at[i, which], gu_out.at[0, i, :, at], sems.at[2 * i + which])
         for copy in copies:
             copy.wait()
@@ -343,8 +342,10 @@
     tokens, rep, inner, outer = lax.optimization_barrier((tokens, rep, inner, outer))
 
     def over_inner(messages, way):
-        arrived = {k: shift(messages[k], "inner", k, way) for k in in_order(depth)}
-        return [arrived[k] for k in range(depth)]
+        arrived = []
+        for k, message in enumerate(messages):
+            arrived.append(shift(message, "inner", k, way))
+        return arrived
 
     def code_of(column):
         expert = ahead(inner, jnp.arange(depth, dtype=jnp.int32), depth) * width + column
@@ -352,11 +353,10 @@
         return jnp.sum(jnp.where(chosen, gate_codes[None], 0), axis=2)
 
     blocks = over_inner([tokens] * depth, ahead)
-    softened = soften_all(
-        gate_up_latent, down_latent, part_width * reps, down_latent.shape[1] * reps
-    )
-    blocks[-1], *softened = lax.optimization_barrier((blocks[-1], *softened))
-    gu_weight, dn_weight, gu_slope, dn_slope = softened
+    gate_fan = part_width * reps
+    down_fan = down_latent.shape[1] * reps
+    (gu_weight,) = per_entry(weight_of, [gate_up_latent], [gate_fan], bf16)
+    blocks[-1], gu_weight = lax.optimization_barrier((blocks[-1], gu_weight))
 
     tok_groups = [jnp.concatenate(blocks, axis=0)]
     code_groups = [code_of(outer)]
@@ -373,6 +373,7 @@
     gate = upright(jnp.pad(gate, ((0, -depth % 8), (0, -gate.shape[1] % 128))))
     gate = gate[: width * tok_rows]
 
+    (dn_weight,) = per_entry(weight_of, [down_latent], [down_fan], bf16)
     their_groups, factors, keeps, arrivals = [], [], [], []
     for group in tok_groups:
         theirs = other_rep(group)
@@ -381,9 +382,13 @@
         factors.append((hidden, by_gate, by_up))
         keeps.append(keep)
         arrivals.append(other_rep(send))
-    messages = pack(keeps, arrivals, depth)
-
+    messages = list(pack(keeps, arrivals, depth))
+
+    latents = [gate_up_latent, down_latent]
+    messages[0], *latents = lax.optimization_barrier((messages[0], *latents))
     picked = over_inner(messages, back)
+    slopes = per_entry(slope_of, latents, [gate_fan, down_fan], f32)
+    picked[-1], *slopes = lax.optimization_barrier((picked[-1], *slopes))
     total, sent = mix(gate, picked, teacher)
     arrivals = [shift(sent, "outer", step) for step in range(1, width)]
     outgoing = upstream(gate, total, arrivals, teacher, depth)
@@ -396,15 +401,15 @@
         mixed = mixed + arrivals[step - 1][source * tok_rows : (source + 1) * tok_rows].astype(f32)
     student_out = mixed.astype(bf16)
 
-    their_grads = other_rep(jnp.concatenate(grads, axis=0))
+    their_grads = [other_rep(grad) for grad in grads]
     new_gate_up, new_down = backward(
         rep,
         (grads, their_grads),
         (tok_groups, their_groups),
         factors,
         dn_weight,
-        (gu_slope, dn_slope),
-        (gate_up_latent, down_latent),
+        slopes,
+        latents,
     )
     return (student_out, new_gate_up, new_down)
 

time: 46.5 us -> 45.1 us (0.970)
  waiting for transfers between devices: 17.6 us -> 13.3 us
  Pallas kernels: 6.83 us -> 9.63 us
    ppermute x16 -> x19, waiting for transfers between devices: 17.6 us -> 13.3 us  [shift(): return lax.ppermute(x, axis, [(i, way(i, step, size)) for i in range(size)])]
    pallas_call x1 -> x3, Pallas kernels: 3.15 us -> 5.99 us  [per_entry(): pl.pallas_call(body, in_specs=[pl.BlockSpec(memory_space=pltpu.HBM) for _...]
    ppermute x16 -> x19, starting transfers between devices: 18.5 us -> 18.6 us  [shift(): return lax.ppermute(x, axis, [(i, way(i, step, size)) for i in range(size)])]
  transfers between devices with their start and end apart: 16 -> 19, of which waited for: 11 -> 10; matrix products, arithmetic and copies ran while one was open for 5% -> 5% of each run, Pallas kernels for 10% -> 16%
where the time goes in v4:
time: 45.1 us; the launch traced here: 44.8 us
  starting transfers between devices  18.6 us (41%)
  waiting for transfers between devices  13.3 us (29%)
  Pallas kernels  9.63 us (21%)
  other arithmetic  1.67 us (4%)
  local copies, waits for them, and re-layouts  0.82 us (2%)
  between operations  0.8 us (2%)
    ppermute x19, starting transfers between devices, shift(): return lax.ppermute(x, axis, [(i, way(i, step, size)) for i in range(size)])  18.6 us
    ppermute x19, waiting for transfers between devices, shift(): return lax.ppermute(x, axis, [(i, way(i, step, size)) for i in range(size)])  13.3 us
    pallas_call x3, Pallas kernels, per_entry(): pl.pallas_call(body, in_specs=[pl.BlockSpec(memory_space=pltpu.HBM) for _...  5.99 us
    pallas_call x1, Pallas kernels, backward(): pl.pallas_call(body, in_specs=[pl.BlockSpec(memory_space=pltpu.SMEM)] + [...  2.05 us
    pallas_call x2, Pallas kernels, forward(): pl.pallas_call(body, in_specs=[pl.BlockSpec(memory_space=pltpu.SMEM)] + [...  1.22 us
  transfers between devices with their start and end apart: 19, of which 10 were waited for; matrix products, arithmetic and copies ran while one was open for 5% of the time, Pallas kernels for 16%

profile of v4, /device:TPU:0, one launch (start us, length us, event | category | flops | bytes accessed | tf_op | source)
XLA Modules:
  0.0 44.8 jit_solution(3217389789989394738)
XLA Ops:
  0.6 5.1 %collective-permute-start.2 = (bf16[32,512]{1,0:T(8,128)(2,1)}, bf16[32,512]{1,0:T(8,128)(2,1)S(1)}, u32[]{:S(2)}, u32[]{:S(2)}) collective-permute-start(bf16[32,512]{1,0:T(8,128)(2,1)} %param.6), channel_id=1, source_target_pairs={{0,12},{4,8},{8,4},{12,0},{1,13},{5,9},{9,5},{13,1},{2,14},{6,10},... | collective-permute-start | bytes 98312 | tf_op jit(solution)/shard_map/ppermute | solution.py:47
  5.8 0.0 collective-permute-start.1
  5.8 0.6 %collective-permute-start = (bf16[32,512]{1,0:T(8,128)(2,1)}, bf16[32,512]{1,0:T(8,128)(2,1)S(1)}, u32[]{:S(2)}, u32[]{:S(2)}) collective-permute-start(bf16[32,512]{1,0:T(8,128)(2,1)} %param.6), channel_id=1, source_target_pairs={{0,4},{4,0},{8,12},{12,8},{1,5},{5,1},{9,13},{13,9},{2,6},{6,2},{1... | collective-permute-start | bytes 98312 | tf_op jit(solution)/shard_map/ppermute | solution.py:47
  6.4 0.8 %select_reduce_fusion.1 = (s32[4,32]{1,0:T(4,128)S(1)}, s32[4,32]{1,0:T(4,128)S(1)}) fusion(s32[32,8]{0,1:T(8,128)} %param.9, s32[32,8]{0,1:T(8,128)} %param.8, s32[4]{0:T(128)S(1)} %get-tuple-element.94, s32[4]{0:T(128)S(1)} %get-tuple-element.93), kind=kLoop, calls=%fused_computation.16 | loop fusion | flops 5888 | bytes 3104 | tf_op jit(solution)/shard_map/reduce_sum | solution.py:353
  7.2 0.8 %constant_dynamic-update-slice_fusion.8 = (bf16[128,512]{1,0:T(8,128)(2,1)S(1)}, bf16[136,512]{1,0:T(8,128)(2,1)S(1)}) fusion(bf16[32,512]{1,0:T(8,128)(2,1)} %param.6), kind=kLoop, calls=%fused_computation.9 | loop fusion | bytes 98304
  8.0 1.9 %shard_map.85.gu_ref = bf16[1,2,192,1024]{3,2,1,0:T(8,128)(2,1)S(1)} custom-call(f32[1,2,192,1024]{3,2,1,0:T(8,128)} %refs_22_), custom_call_target="tpu_custom_call" | custom-call | tf_op jit(solution)/shard_map/pallas_call | solution.py:119
  9.9 0.0 collective-permute-done
  9.9 0.0 collective-permute-done.2
  9.9 0.9 %collective-permute-done.1 = bf16[32,512]{1,0:T(8,128)(2,1)S(1)} collective-permute-done((bf16[32,512]{1,0:T(8,128)(2,1)}, bf16[32,512]{1,0:T(8,128)(2,1)S(1)}, u32[]{:S(2)}, u32[]{:S(2)}) %collective-permute-start.1) | collective-permute-done | bytes 32800 | tf_op jit(solution)/shard_map/ppermute | solution.py:47
  10.8 0.1 constant_dynamic-update-slice_fusion
  10.9 1.5 %collective-permute-start.3 = (bf16[136,512]{1,0:T(8,128)(2,1)S(1)}, bf16[136,512]{1,0:T(8,128)(2,1)S(1)}, u32[]{:S(2)}, u32[]{:S(2)}) collective-permute-start(bf16[136,512]{1,0:T(8,128)(2,1)S(1)} %constant_dynamic-update-slice_fusion), channel_id=1, source_target_pairs={{0,2},{2,0},{1,3},{3,1},{4,6},{6,4},{5,7},{7,5},{8,10},{10,8},{9,1... | collective-permute-start | bytes 417800 | tf_op jit(solution)/shard_map/ppermute | solution.py:47
  12.4 0.0 collective-permute-start.4
  12.4 1.4 %shard_map.86.dn_ref.refs_19_ = bf16[1,192,1024]{2,1,0:T(8,128)(2,1)S(1)} custom-call(f32[1,192,1024]{2,1,0:T(8,128)} %refs_23_), custom_call_target="tpu_custom_call" | custom-call | tf_op jit(solution)/shard_map/pallas_call | solution.py:119
  13.8 0.0 collective-permute-done.4.theirs_ref.refs_11_
  13.9 0.6 %forward.2 = (bf16[192,128]{1,0:T(8,128)(2,1)S(1)}, f32[192,128]{1,0:T(8,128)S(1)}, f32[192,128]{1,0:T(8,128)S(1)}, f32[128,512]{1,0:T(8,128)S(1)}, bf16[128,512]{1,0:T(8,128)(2,1)S(1)}) custom-call(s32[1]{0:T(128)} %bitcast.rep_ref.refs_0_, bf16[128,512]{1,0:T(8,128)(2,1)S(1)} %get-tuple-element.83.mine_ref.refs_9_, ...), custom_call_target="tpu_custom_call" | custom-call | tf_op jit(solution)/shard_map/forward/pallas_call | solution.py:157
  14.5 0.6 %collective-permute-start.6 = (bf16[128,512]{1,0:T(8,128)(2,1)S(1)}, bf16[128,512]{1,0:T(8,128)(2,1)S(1)}, u32[]{:S(2)}, u32[]{:S(2)}) collective-permute-start(bf16[128,512]{1,0:T(8,128)(2,1)S(1)} %get-tuple-element.50), channel_id=1, source_target_pairs={{0,1},{1,0},{2,3},{3,2},{4,5},{5,4},{6,7},{7,6},{8,9},{9,8},{10,11... | collective-permute-start | bytes 393224 | tf_op jit(solution)/shard_map/ppermute | solution.py:47
  15.1 0.9 %collective-permute-done.3 = bf16[136,512]{1,0:T(8,128)(2,1)S(1)} collective-permute-done((bf16[136,512]{1,0:T(8,128)(2,1)S(1)}, bf16[136,512]{1,0:T(8,128)(2,1)S(1)}, u32[]{:S(2)}, u32[]{:S(2)}) %collective-permute-start.3) | collective-permute-done | bytes 139296 | tf_op jit(solution)/shard_map/ppermute | solution.py:47
  16.0 0.1 collective-permute-start.5
  16.1 1.3 %collective-permute-done.5.theirs_ref.refs_12_ = bf16[128,512]{1,0:T(8,128)(2,1)S(1)} collective-permute-done((bf16[128,512]{1,0:T(8,128)(2,1)S(1)}, bf16[128,512]{1,0:T(8,128)(2,1)S(1)}, u32[]{:S(2)}, u32[]{:S(2)}) %collective-permute-start.5) | collective-permute-done | bytes 131104 | tf_op jit(solution)/shard_map/ppermute | solution.py:47
  17.4 0.6 %forward.3 = (bf16[192,128]{1,0:T(8,128)(2,1)S(1)}, f32[192,128]{1,0:T(8,128)S(1)}, f32[192,128]{1,0:T(8,128)S(1)}, f32[128,512]{1,0:T(8,128)S(1)}, bf16[128,512]{1,0:T(8,128)(2,1)S(1)}) custom-call(s32[1]{0:T(128)} %bitcast.rep_ref.refs_0_, bf16[128,512]{1,0:T(8,128)(2,1)S(1)} %slice.32.mine_ref.refs_10_, ...), custom_call_target="tpu_custom_call" | custom-call | tf_op jit(solution)/shard_map/forward/pallas_call | solution.py:157
  18.0 0.2 collective-permute-start.7
  18.2 0.1 slice_add_fusion
  18.3 0.0 collective-permute-done.6.refs_2_
  18.3 1.1 %collective-permute-done.7.refs_3_ = bf16[128,512]{1,0:T(8,128)(2,1)S(1)} collective-permute-done((bf16[128,512]{1,0:T(8,128)(2,1)S(1)}, bf16[128,512]{1,0:T(8,128)(2,1)S(1)}, u32[]{:S(2)}, u32[]{:S(2)}) %collective-permute-start.7) | collective-permute-done | bytes 131104 | tf_op jit(solution)/shard_map/ppermute | solution.py:47
  19.4 0.0 copy-start.2
  19.5 0.6 %collective-permute-start.8 = (bf16[64,512]{1,0:T(8,128)(2,1)S(1)}, bf16[64,512]{1,0:T(8,128)(2,1)S(1)}, u32[]{:S(2)}, u32[]{:S(2)}) collective-permute-start(bf16[64,512]{1,0:T(8,128)(2,1)S(1)} %get-tuple-element.54), channel_id=1, source_target_pairs={{0,4},{4,0},{8,12},{12,8},{1,5},{5,1},{9,13},{13,9},{2,6},{6,2},{1... | collective-permute-start | bytes 196616 | tf_op jit(solution)/shard_map/ppermute | solution.py:47
  20.1 2.9 %collective-permute-start.9 = (bf16[64,512]{1,0:T(8,128)(2,1)S(1)}, bf16[64,512]{1,0:T(8,128)(2,1)S(1)}, u32[]{:S(2)}, u32[]{:S(2)}) collective-permute-start(bf16[64,512]{1,0:T(8,128)(2,1)S(1)} %get-tuple-element.55), channel_id=1, source_target_pairs={{0,8},{4,12},{8,0},{12,4},{1,9},{5,13},{9,1},{13,5},{2,10},{6,14},... | collective-permute-start | bytes 196616 | tf_op jit(solution)/shard_map/ppermute | solution.py:47
  23.0 0.9 %collective-permute-start.10 = (bf16[64,512]{1,0:T(8,128)(2,1)S(1)}, bf16[64,512]{1,0:T(8,128)(2,1)S(1)}, u32[]{:S(2)}, u32[]{:S(2)}) collective-permute-start(bf16[64,512]{1,0:T(8,128)(2,1)S(1)} %get-tuple-element.56), channel_id=1, source_target_pairs={{0,12},{4,8},{8,4},{12,0},{1,13},{5,9},{9,5},{13,1},{2,14},{6,10},... | collective-permute-start | bytes 196616 | tf_op jit(solution)/shard_map/ppermute | solution.py:47
  23.9 0.1 maximum_multiply_fusion
  24.0 0.1 upright.1
  24.1 0.0 copy-start
  24.1 0.0 copy-start.1
  24.1 2.7 %shard_map.87 = (f32[1,2,192,1024]{3,2,1,0:T(8,128)S(1)}, f32[1,192,1024]{2,1,0:T(8,128)S(1)}) custom-call(f32[1,2,192,1024]{3,2,1,0:T(8,128)} %refs_22_, f32[1,192,1024]{2,1,0:T(8,128)} %refs_23_), custom_call_target="tpu_custom_call" | custom-call | tf_op jit(solution)/shard_map/pallas_call | solution.py:119
  26.8 2.4 %collective-permute-done.10.refs_5_ = bf16[64,512]{1,0:T(8,128)(2,1)S(1)} collective-permute-done((bf16[64,512]{1,0:T(8,128)(2,1)S(1)}, bf16[64,512]{1,0:T(8,128)(2,1)S(1)}, u32[]{:S(2)}, u32[]{:S(2)}) %collective-permute-start.10) | collective-permute-done | bytes 65568 | tf_op jit(solution)/shard_map/ppermute | solution.py:47
  29.2 0.0 collective-permute-done.8.refs_3_
  29.2 0.0 collective-permute-done.9.refs_4_
  29.2 0.0 copy-done.2
  29.2 0.1 mix.1
  29.3 1.6 %collective-permute-start.11 = (bf16[64,512]{1,0:T(8,128)(2,1)S(1)}, bf16[64,512]{1,0:T(8,128)(2,1)S(1)}, u32[]{:S(2)}, u32[]{:S(2)}) collective-permute-start(bf16[64,512]{1,0:T(8,128)(2,1)S(1)} %get-tuple-element.63), channel_id=1, source_target_pairs={{0,2},{2,0},{1,3},{3,1},{4,6},{6,4},{5,7},{7,5},{8,10},{10,8},{9,1... | collective-permute-start | bytes 196616 | tf_op jit(solution)/shard_map/ppermute | solution.py:47
  30.9 2.8 %collective-permute-done.11.refs_3_ = bf16[64,512]{1,0:T(8,128)(2,1)S(1)} collective-permute-done((bf16[64,512]{1,0:T(8,128)(2,1)S(1)}, bf16[64,512]{1,0:T(8,128)(2,1)S(1)}, u32[]{:S(2)}, u32[]{:S(2)}) %collective-permute-start.11) | collective-permute-done | bytes 65568 | tf_op jit(solution)/shard_map/ppermute | solution.py:47
  33.6 0.1 upstream.1
  33.8 2.2 %collective-permute-start.12 = (bf16[64,512]{1,0:T(8,128)(2,1)S(1)}, bf16[64,512]{1,0:T(8,128)(2,1)S(1)}, u32[]{:S(2)}, u32[]{:S(2)}) collective-permute-start(bf16[64,512]{1,0:T(8,128)(2,1)S(1)} %get-tuple-element.64), channel_id=1, source_target_pairs={{0,12},{4,8},{8,4},{12,0},{1,13},{5,9},{9,5},{13,1},{2,14},{6,10},... | collective-permute-start | bytes 196616 | tf_op jit(solution)/shard_map/ppermute | solution.py:47
  36.0 0.4 collective-permute-start.13
  36.4 1.9 %collective-permute-start.14 = (bf16[64,512]{1,0:T(8,128)(2,1)S(1)}, bf16[64,512]{1,0:T(8,128)(2,1)S(1)}, u32[]{:S(2)}, u32[]{:S(2)}) collective-permute-start(bf16[64,512]{1,0:T(8,128)(2,1)S(1)} %get-tuple-element.69), channel_id=1, source_target_pairs={{0,8},{4,12},{8,0},{12,4},{1,9},{5,13},{9,1},{13,5},{2,10},{6,14},... | collective-permute-start | bytes 196616 | tf_op jit(solution)/shard_map/ppermute | solution.py:47
  38.2 0.0 collective-permute-start.15
  38.2 1.7 %collective-permute-done.12.refs_4_ = bf16[64,512]{1,0:T(8,128)(2,1)S(1)} collective-permute-done((bf16[64,512]{1,0:T(8,128)(2,1)S(1)}, bf16[64,512]{1,0:T(8,128)(2,1)S(1)}, u32[]{:S(2)}, u32[]{:S(2)}) %collective-permute-start.12) | collective-permute-done | bytes 65568 | tf_op jit(solution)/shard_map/ppermute | solution.py:47
  39.9 0.0 collective-permute-start.18
  39.9 0.7 %collective-permute-done.13.refs_2_ = bf16[64,512]{1,0:T(8,128)(2,1)S(1)} collective-permute-done((bf16[64,512]{1,0:T(8,128)(2,1)S(1)}, bf16[64,512]{1,0:T(8,128)(2,1)S(1)}, u32[]{:S(2)}, u32[]{:S(2)}) %collective-permute-start.13) | collective-permute-done | bytes 65568 | tf_op jit(solution)/shard_map/ppermute | solution.py:47
  40.6 0.0 collective-permute-start.16
  40.6 0.9 %collective-permute-done.14.refs_3_ = bf16[64,512]{1,0:T(8,128)(2,1)S(1)} collective-permute-done((bf16[64,512]{1,0:T(8,128)(2,1)S(1)}, bf16[64,512]{1,0:T(8,128)(2,1)S(1)}, u32[]{:S(2)}, u32[]{:S(2)}) %collective-permute-start.14) | collective-permute-done | bytes 65568 | tf_op jit(solution)/shard_map/ppermute | solution.py:47
  41.5 0.0 collective-permute-start.17
  41.5 0.6 %add_convert_fusion = bf16[32,512]{1,0:T(8,128)(2,1)} fusion(f32[64,512]{1,0:T(8,128)S(1)} %get-tuple-element.65.refs_2_, bf16[64,512]{1,0:T(8,128)(2,1)S(1)} %collective-permute-done.11.refs_3_), kind=kLoop, calls=%fused_computation | loop fusion | flops 49152 | bytes 131072 | tf_op jit(solution)/shard_map/convert_element_type | solution.py:402
  42.1 0.0 collective-permute-done.15.refs_5_
  42.2 0.0 collective-permute-done.18.refs_8_
  42.2 0.0 collective-permute-done.16.refs_6_
  42.2 0.6 %collective-permute-done.17.refs_7_ = bf16[64,512]{1,0:T(8,128)(2,1)S(1)} collective-permute-done((bf16[64,512]{1,0:T(8,128)(2,1)S(1)}, bf16[64,512]{1,0:T(8,128)(2,1)S(1)}, u32[]{:S(2)}, u32[]{:S(2)}) %collective-permute-start.17) | collective-permute-done | bytes 65568 | tf_op jit(solution)/shard_map/ppermute | solution.py:47
  42.8 0.0 copy-done
  42.8 0.0 copy-done.1
  42.8 2.0 %backward.1 = (f32[1,2,192,1024]{3,2,1,0:T(8,128)}, f32[1,192,1024]{2,1,0:T(8,128)}) custom-call(s32[1]{0:T(128)} %bitcast.rep_ref.refs_0_, bf16[64,512]{1,0:T(8,128)(2,1)S(1)} %get-tuple-element.67.refs_1_, bf16[64,512]{1,0:T(8,128)(2,1)S(1)} %collective-permute-done.13.refs_2_, bf16[64,512]{1,0:T(8,128)(2,1)S(1)} %collective-permute-done.14.refs_3_, ...), custom_call_target="tpu_custom_call" | custom-call | tf_op jit(solution)/shard_map/backward/pallas_call | solution.py:317
  (11 shorter events, 0.1 us)
Async XLA Ops:
  0.6 9.3 %collective-permute-start.2 = (bf16[32,512]{1,0:T(8,128)(2,1)}, bf16[32,512]{1,0:T(8,128)(2,1)S(1)}, u32[]{:S(2)}, u32[]{:S(2)}) collective-permute-start(bf16[32,512]{1,0:T(8,128)(2,1)} %param.6), channel_id=1, source_target_pairs={{0,12},{4,8},{8,4},{12,0},{1,13},{5,9},{9,5},{13,1},{2,14},{6,10},... | collective-permute-start | bytes 98312 | tf_op jit(solution)/shard_map/ppermute | solution.py:47
  5.8 5.0 %collective-permute-start.1 = (bf16[32,512]{1,0:T(8,128)(2,1)}, bf16[32,512]{1,0:T(8,128)(2,1)S(1)}, u32[]{:S(2)}, u32[]{:S(2)}) collective-permute-start(bf16[32,512]{1,0:T(8,128)(2,1)} %param.6), channel_id=1, source_target_pairs={{0,8},{4,12},{8,0},{12,4},{1,9},{5,13},{9,1},{13,5},{2,10},{6,14},... | collective-permute-start | bytes 98312 | tf_op jit(solution)/shard_map/ppermute | solution.py:47
  5.8 4.1 %collective-permute-start = (bf16[32,512]{1,0:T(8,128)(2,1)}, bf16[32,512]{1,0:T(8,128)(2,1)S(1)}, u32[]{:S(2)}, u32[]{:S(2)}) collective-permute-start(bf16[32,512]{1,0:T(8,128)(2,1)} %param.6), channel_id=1, source_target_pairs={{0,4},{4,0},{8,12},{12,8},{1,5},{5,1},{9,13},{13,9},{2,6},{6,2},{1... | collective-permute-start | bytes 98312 | tf_op jit(solution)/shard_map/ppermute | solution.py:47
  10.9 5.1 %collective-permute-start.3 = (bf16[136,512]{1,0:T(8,128)(2,1)S(1)}, bf16[136,512]{1,0:T(8,128)(2,1)S(1)}, u32[]{:S(2)}, u32[]{:S(2)}) collective-permute-start(bf16[136,512]{1,0:T(8,128)(2,1)S(1)} %constant_dynamic-update-slice_fusion), channel_id=1, source_target_pairs={{0,2},{2,0},{1,3},{3,1},{4,6},{6,4},{5,7},{7,5},{8,10},{10,8},{9,1... | collective-permute-start | bytes 417800 | tf_op jit(solution)/shard_map/ppermute | solution.py:47
  12.4 1.5 %collective-permute-start.4 = (bf16[128,512]{1,0:T(8,128)(2,1)S(1)}, bf16[128,512]{1,0:T(8,128)(2,1)S(1)}, u32[]{:S(2)}, u32[]{:S(2)}) collective-permute-start(bf16[128,512]{1,0:T(8,128)(2,1)S(1)} %get-tuple-element.83.mine_ref.refs_9_), channel_id=1, source_target_pairs={{0,1},{1,0},{2,3},{3,2},{4,5},{5,4},{6,7},{7,6},{8,9},{9,8},{10,11... | collective-permute-start | bytes 393224 | tf_op jit(solution)/shard_map/ppermute | solution.py:47
  14.5 3.8 %collective-permute-start.6 = (bf16[128,512]{1,0:T(8,128)(2,1)S(1)}, bf16[128,512]{1,0:T(8,128)(2,1)S(1)}, u32[]{:S(2)}, u32[]{:S(2)}) collective-permute-start(bf16[128,512]{1,0:T(8,128)(2,1)S(1)} %get-tuple-element.50), channel_id=1, source_target_pairs={{0,1},{1,0},{2,3},{3,2},{4,5},{5,4},{6,7},{7,6},{8,9},{9,8},{10,11... | collective-permute-start | bytes 393224 | tf_op jit(solution)/shard_map/ppermute | solution.py:47
  16.0 1.4 %collective-permute-start.5 = (bf16[128,512]{1,0:T(8,128)(2,1)S(1)}, bf16[128,512]{1,0:T(8,128)(2,1)S(1)}, u32[]{:S(2)}, u32[]{:S(2)}) collective-permute-start(bf16[128,512]{1,0:T(8,128)(2,1)S(1)} %slice.32.mine_ref.refs_10_), channel_id=1, source_target_pairs={{0,1},{1,0},{2,3},{3,2},{4,5},{5,4},{6,7},{7,6},{8,9},{9,8},{10,11... | collective-permute-start | bytes 393224 | tf_op jit(solution)/shard_map/ppermute | solution.py:47
  18.0 1.4 %collective-permute-start.7 = (bf16[128,512]{1,0:T(8,128)(2,1)S(1)}, bf16[128,512]{1,0:T(8,128)(2,1)S(1)}, u32[]{:S(2)}, u32[]{:S(2)}) collective-permute-start(bf16[128,512]{1,0:T(8,128)(2,1)S(1)} %get-tuple-element.51), channel_id=1, source_target_pairs={{0,1},{1,0},{2,3},{3,2},{4,5},{5,4},{6,7},{7,6},{8,9},{9,8},{10,11... | collective-permute-start | bytes 393224 | tf_op jit(solution)/shard_map/ppermute | solution.py:47
  19.4 9.8 %copy-start.2 = (bf16[32,512]{1,0:T(8,128)(2,1)S(1)}, bf16[32,512]{1,0:T(8,128)(2,1)}, u32[]{:S(2)}) copy-start(bf16[32,512]{1,0:T(8,128)(2,1)} %refs_1_.4) | copy-start | bytes 98308
  19.5 9.7 %collective-permute-start.8 = (bf16[64,512]{1,0:T(8,128)(2,1)S(1)}, bf16[64,512]{1,0:T(8,128)(2,1)S(1)}, u32[]{:S(2)}, u32[]{:S(2)}) collective-permute-start(bf16[64,512]{1,0:T(8,128)(2,1)S(1)} %get-tuple-element.54), channel_id=1, source_target_pairs={{0,4},{4,0},{8,12},{12,8},{1,5},{5,1},{9,13},{13,9},{2,6},{6,2},{1... | collective-permute-start | bytes 196616 | tf_op jit(solution)/shard_map/ppermute | solution.py:47
  20.1 9.1 %collective-permute-start.9 = (bf16[64,512]{1,0:T(8,128)(2,1)S(1)}, bf16[64,512]{1,0:T(8,128)(2,1)S(1)}, u32[]{:S(2)}, u32[]{:S(2)}) collective-permute-start(bf16[64,512]{1,0:T(8,128)(2,1)S(1)} %get-tuple-element.55), channel_id=1, source_target_pairs={{0,8},{4,12},{8,0},{12,4},{1,9},{5,13},{9,1},{13,5},{2,10},{6,14},... | collective-permute-start | bytes 196616 | tf_op jit(solution)/shard_map/ppermute | solution.py:47
  23.0 6.2 %collective-permute-start.10 = (bf16[64,512]{1,0:T(8,128)(2,1)S(1)}, bf16[64,512]{1,0:T(8,128)(2,1)S(1)}, u32[]{:S(2)}, u32[]{:S(2)}) collective-permute-start(bf16[64,512]{1,0:T(8,128)(2,1)S(1)} %get-tuple-element.56), channel_id=1, source_target_pairs={{0,12},{4,8},{8,4},{12,0},{1,13},{5,9},{9,5},{13,1},{2,14},{6,10},... | collective-permute-start | bytes 196616 | tf_op jit(solution)/shard_map/ppermute | solution.py:47
  24.1 18.7 %copy-start = (f32[1,2,192,1024]{3,2,1,0:T(8,128)S(1)}, f32[1,2,192,1024]{3,2,1,0:T(8,128)}, u32[]{:S(2)}) copy-start(f32[1,2,192,1024]{3,2,1,0:T(8,128)} %refs_22_) | copy-start | bytes 4718596
  24.1 18.7 %copy-start.1 = (f32[1,192,1024]{2,1,0:T(8,128)S(1)}, f32[1,192,1024]{2,1,0:T(8,128)}, u32[]{:S(2)}) copy-start(f32[1,192,1024]{2,1,0:T(8,128)} %refs_23_) | copy-start | bytes 2359300
  29.3 4.3 %collective-permute-start.11 = (bf16[64,512]{1,0:T(8,128)(2,1)S(1)}, bf16[64,512]{1,0:T(8,128)(2,1)S(1)}, u32[]{:S(2)}, u32[]{:S(2)}) collective-permute-start(bf16[64,512]{1,0:T(8,128)(2,1)S(1)} %get-tuple-element.63), channel_id=1, source_target_pairs={{0,2},{2,0},{1,3},{3,1},{4,6},{6,4},{5,7},{7,5},{8,10},{10,8},{9,1... | collective-permute-start | bytes 196616 | tf_op jit(solution)/shard_map/ppermute | solution.py:47
  33.8 6.2 %collective-permute-start.12 = (bf16[64,512]{1,0:T(8,128)(2,1)S(1)}, bf16[64,512]{1,0:T(8,128)(2,1)S(1)}, u32[]{:S(2)}, u32[]{:S(2)}) collective-permute-start(bf16[64,512]{1,0:T(8,128)(2,1)S(1)} %get-tuple-element.64), channel_id=1, source_target_pairs={{0,12},{4,8},{8,4},{12,0},{1,13},{5,9},{9,5},{13,1},{2,14},{6,10},... | collective-permute-start | bytes 196616 | tf_op jit(solution)/shard_map/ppermute | solution.py:47
  36.0 4.6 %collective-permute-start.13 = (bf16[64,512]{1,0:T(8,128)(2,1)S(1)}, bf16[64,512]{1,0:T(8,128)(2,1)S(1)}, u32[]{:S(2)}, u32[]{:S(2)}) collective-permute-start(bf16[64,512]{1,0:T(8,128)(2,1)S(1)} %get-tuple-element.68), channel_id=1, source_target_pairs={{0,4},{4,0},{8,12},{12,8},{1,5},{5,1},{9,13},{13,9},{2,6},{6,2},{1... | collective-permute-start | bytes 196616 | tf_op jit(solution)/shard_map/ppermute | solution.py:47
  36.4 5.2 %collective-permute-start.14 = (bf16[64,512]{1,0:T(8,128)(2,1)S(1)}, bf16[64,512]{1,0:T(8,128)(2,1)S(1)}, u32[]{:S(2)}, u32[]{:S(2)}) collective-permute-start(bf16[64,512]{1,0:T(8,128)(2,1)S(1)} %get-tuple-element.69), channel_id=1, source_target_pairs={{0,8},{4,12},{8,0},{12,4},{1,9},{5,13},{9,1},{13,5},{2,10},{6,14},... | collective-permute-start | bytes 196616 | tf_op jit(solution)/shard_map/ppermute | solution.py:47
  38.2 3.9 %collective-permute-start.15 = (bf16[64,512]{1,0:T(8,128)(2,1)S(1)}, bf16[64,512]{1,0:T(8,128)(2,1)S(1)}, u32[]{:S(2)}, u32[]{:S(2)}) collective-permute-start(bf16[64,512]{1,0:T(8,128)(2,1)S(1)} %get-tuple-element.67.refs_1_), channel_id=1, source_target_pairs={{0,1},{1,0},{2,3},{3,2},{4,5},{5,4},{6,7},{7,6},{8,9},{9,8},{10,11... | collective-permute-start | bytes 196616 | tf_op jit(solution)/shard_map/ppermute | solution.py:47
  39.9 2.2 %collective-permute-start.18 = (bf16[64,512]{1,0:T(8,128)(2,1)S(1)}, bf16[64,512]{1,0:T(8,128)(2,1)S(1)}, u32[]{:S(2)}, u32[]{:S(2)}) collective-permute-start(bf16[64,512]{1,0:T(8,128)(2,1)S(1)} %collective-permute-done.12.refs_4_), channel_id=1, source_target_pairs={{0,1},{1,0},{2,3},{3,2},{4,5},{5,4},{6,7},{7,6},{8,9},{9,8},{10,11... | collective-permute-start | bytes 196616 | tf_op jit(solution)/shard_map/ppermute | solution.py:47
  40.6 1.6 %collective-permute-start.16 = (bf16[64,512]{1,0:T(8,128)(2,1)S(1)}, bf16[64,512]{1,0:T(8,128)(2,1)S(1)}, u32[]{:S(2)}, u32[]{:S(2)}) collective-permute-start(bf16[64,512]{1,0:T(8,128)(2,1)S(1)} %collective-permute-done.13.refs_2_), channel_id=1, source_target_pairs={{0,1},{1,0},{2,3},{3,2},{4,5},{5,4},{6,7},{7,6},{8,9},{9,8},{10,11... | collective-permute-start | bytes 196616 | tf_op jit(solution)/shard_map/ppermute | solution.py:47
  41.5 1.3 %collective-permute-start.17 = (bf16[64,512]{1,0:T(8,128)(2,1)S(1)}, bf16[64,512]{1,0:T(8,128)(2,1)S(1)}, u32[]{:S(2)}, u32[]{:S(2)}) collective-permute-start(bf16[64,512]{1,0:T(8,128)(2,1)S(1)} %collective-permute-done.14.refs_3_), channel_id=1, source_target_pairs={{0,1},{1,0},{2,3},{3,2},{4,5},{5,4},{6,7},{7,6},{8,9},{9,8},{10,11... | collective-permute-start | bytes 196616 | tf_op jit(solution)/shard_map/ppermute | solution.py:47

commit v5 on v4

--- a/solution.py
+++ b/solution.py
@@ -92,7 +92,7 @@
     )(gate)
 
 
-def per_entry(rule, latents, fans, dtype):
+def per_entry(rule, latents, fans, dtype, carried=()):
     pieces = []
     for n, latent in enumerate(latents):
         cuts = 2 if latent.shape[-2] % 32 == 0 else 1
@@ -104,70 +104,112 @@
     wide = latents[0].shape[-1]
 
     def body(*refs):
-        sources = refs[: len(latents)]
-        targets = refs[len(latents) : -2]
+        count = len(latents) + len(carried)
+        sources = refs[:count]
+        targets = refs[count:-2]
         held, sems = refs[-2:]
         copies = []
+        for n in range(len(latents), count):
+            sem = sems.at[len(pieces) + n - len(latents)]
+            copies.append(pltpu.make_async_copy(sources[n], targets[n], sem))
+            copies[-1].start()
         for slot, (n, at, row) in enumerate(pieces):
             source = sources[n].at[(*at, pl.ds(row, rows))]
             copies.append(pltpu.make_async_copy(source, held.at[slot], sems.at[slot]))
             copies[-1].start()
         for slot, (n, at, row) in enumerate(pieces):
-            copies[slot].wait()
+            copies[len(carried) + slot].wait()
             targets[n][(*at, pl.ds(row, rows))] = rule(held[slot], fans[n])
-
-    return pl.pallas_call(
-        body,
-        in_specs=[pl.BlockSpec(memory_space=pltpu.HBM) for _ in latents],
-        out_specs=[whole() for _ in latents],
-        out_shape=[like(latent.shape, dtype) for latent in latents],
+        for copy in copies[: len(carried)]:
+            copy.wait()
+
+    inputs = [*latents, *carried]
+    return pl.pallas_call(
+        body,
+        in_specs=[pl.BlockSpec(memory_space=pltpu.HBM) for _ in inputs],
+        out_specs=[whole() for _ in inputs],
+        out_shape=[like(latent.shape, dtype) for latent in latents]
+        + [like(array.shape, array.dtype) for array in carried],
         scratch_shapes=[
             pltpu.VMEM((len(pieces), rows, wide), jnp.float32),
-            pltpu.SemaphoreType.DMA((len(pieces),)),
+            pltpu.SemaphoreType.DMA((len(pieces) + len(carried),)),
         ],
         compiler_params=pltpu.CompilerParams(vmem_limit_bytes=8 * MEBI),
-    )(*[pltpu.with_memory_space_constraint(latent, pltpu.HBM) for latent in latents])
-
-
-def forward(rep, mine, theirs, gu_weight, dn_weight):
+    )(*[pltpu.with_memory_space_constraint(array, pltpu.HBM) for array in inputs])
+
+
+def project(rep, mine, gu_weight):
+    pair, hid = gu_weight.shape[1:3]
+    rows, part = mine.shape
+
+    def body(rep_ref, mine_ref, gu_ref, out):
+        here, _ = halves(rep_ref, part)
+        for i in range(pair):
+            out[i] = dot(gu_ref[0, i, :, pl.ds(here, part)], mine_ref[...], 1, 1)
+
+    return pl.pallas_call(
+        body,
+        in_specs=[pl.BlockSpec(memory_space=pltpu.SMEM), whole(), whole()],
+        out_specs=whole(),
+        out_shape=like((pair, hid, rows), jnp.float32),
+        compiler_params=pltpu.CompilerParams(vmem_limit_bytes=4 * MEBI),
+        name="project",
+    )(rep, mine, gu_weight)
+
+
+def forward(rep, started, theirs, gu_weight, dn_weight):
     hid = dn_weight.shape[1]
-    rows, part = mine.shape
-
-    def body(rep_ref, mine_ref, theirs_ref, gu_ref, dn_ref, hidden, by_gate, by_up, keep, send):
-        here, there = halves(rep_ref, part)
-        x_mine = mine_ref[...]
-        x_theirs = theirs_ref[...]
-
-        def project(which):
-            return dot(gu_ref[0, which, :, pl.ds(here, part)], x_mine, 1, 1) + dot(
-                gu_ref[0, which, :, pl.ds(there, part)], x_theirs, 1, 1
-            )
-
-        pre_gate = project(0)
-        pre_up = project(1)
-        sigmoid_gate = jax.nn.sigmoid(pre_gate)
-        activated = pre_gate * sigmoid_gate
-        rounded = (activated * pre_up).astype(jnp.bfloat16)
-        send[...] = dot(rounded, dn_ref[0, :, pl.ds(there, part)], 0, 0).astype(jnp.bfloat16)
-        keep[...] = dot(rounded, dn_ref[0, :, pl.ds(here, part)], 0, 0)
+    rows, part = theirs.shape
+    pair = gu_weight.shape[1]
+
+    def body(rep_ref, started_ref, theirs_ref, gu_ref, dn_ref, pre, hidden, send):
+        _, there = halves(rep_ref, part)
+        at = pl.ds(there, part)
+        for i in range(pair):
+            pre[i] = started_ref[i] + dot(gu_ref[0, i, :, at], theirs_ref[...], 1, 1)
+        pre_gate = pre[0]
+        rounded = (pre_gate * jax.nn.sigmoid(pre_gate) * pre[1]).astype(jnp.bfloat16)
         hidden[...] = rounded
-        by_gate[...] = pre_up * sigmoid_gate * (1.0 + pre_gate * (1.0 - sigmoid_gate))
-        by_up[...] = activated
+        send[...] = dot(rounded, dn_ref[0, :, at], 0, 0).astype(jnp.bfloat16)
 
     return pl.pallas_call(
         body,
         in_specs=[pl.BlockSpec(memory_space=pltpu.SMEM)] + [whole() for _ in range(4)],
-        out_specs=[whole() for _ in range(5)],
+        out_specs=[whole() for _ in range(3)],
         out_shape=[
+            like((pair, hid, rows), jnp.float32),
             like((hid, rows), jnp.bfloat16),
-            like((hid, rows), jnp.float32),
-            like((hid, rows), jnp.float32),
-            like((rows, part), jnp.float32),
             like((rows, part), jnp.bfloat16),
         ],
         compiler_params=pltpu.CompilerParams(vmem_limit_bytes=8 * MEBI),
         name="forward",
-    )(rep, mine, theirs, gu_weight, dn_weight)
+    )(rep, started, theirs, gu_weight, dn_weight)
+
+
+def keep_share(rep, pre, hidden, dn_weight):
+    hid, rows = hidden.shape
+    part = dn_weight.shape[2] // 2
+
+    def body(rep_ref, pre_ref, hidden_ref, dn_ref, keep, by_gate, by_up):
+        here, _ = halves(rep_ref, part)
+        keep[...] = dot(hidden_ref[...], dn_ref[0, :, pl.ds(here, part)], 0, 0)
+        pre_gate = pre_ref[0]
+        sigmoid_gate = jax.nn.sigmoid(pre_gate)
+        by_gate[...] = pre_ref[1] * sigmoid_gate * (1.0 + pre_gate * (1.0 - sigmoid_gate))
+        by_up[...] = pre_gate * sigmoid_gate
+
+    return pl.pallas_call(
+        body,
+        in_specs=[pl.BlockSpec(memory_space=pltpu.SMEM)] + [whole() for _ in range(3)],
+        out_specs=[whole() for _ in range(3)],
+        out_shape=[
+            like((rows, part), jnp.float32),
+            like((hid, rows), jnp.float32),
+            like((hid, rows), jnp.float32),
+        ],
+        compiler_params=pltpu.CompilerParams(vmem_limit_bytes=8 * MEBI),
+        name="keep_share",
+    )(rep, pre, hidden, dn_weight)
 
 
 def pack(keeps, arrivals, depth):
@@ -253,64 +295,92 @@
     )(gate, teacher, total, *arrivals)
 
 
-def backward(rep, grads, rows_of, factors, weights, slopes, latents):
+def joined(refs, block, width):
+    return jnp.concatenate(
+        [ref[j * block : (j + 1) * block, :] for j in range(width) for ref in refs], axis=0
+    )
+
+
+def begin(rep, grads, hiddens, weight, slope, latent):
+    hid = latent.shape[1]
+    width = len(hiddens)
+    depth = len(grads)
+    block = grads[0].shape[0] // width
+    part = grads[0].shape[1]
+    rows = width * depth * block
+
+    def body(rep_ref, *refs):
+        grad_refs = refs[:depth]
+        hidden_refs = refs[depth : depth + width]
+        weight_ref, slope_ref, latent_ref, hidden_grad, new_down = refs[depth + width :]
+        here, _ = halves(rep_ref, part)
+        at = pl.ds(here, part)
+        mine = joined(grad_refs, block, width)
+        hidden_grad[...] = dot(weight_ref[0, :, at], mine, 1, 1)
+        hidden = jnp.concatenate([ref[...] for ref in hidden_refs], axis=1)
+        new_down[...] = latent_ref[0, :, at] - slope_ref[0, :, at] * dot(hidden, mine, 1, 0)
+
+    return pl.pallas_call(
+        body,
+        in_specs=[pl.BlockSpec(memory_space=pltpu.SMEM)]
+        + [whole() for _ in range(depth + width + 3)],
+        out_specs=[whole(), whole()],
+        out_shape=[like((hid, rows), jnp.float32), like((hid, part), jnp.float32)],
+        compiler_params=pltpu.CompilerParams(vmem_limit_bytes=4 * MEBI),
+        name="begin",
+    )(rep, *grads, *hiddens, weight, slope, latent)
+
+
+def backward(rep, begun, grads, rows_of, factors, weights, slopes, latents):
     gate_up, down = latents
     _, pair, hid, _ = gate_up.shape
     width = len(factors)
-    depth = len(grads[0])
-    part = grads[0][0].shape[1]
-    block = grads[0][0].shape[0] // width
-    flat = [*grads[0], *grads[1], *rows_of[0], *rows_of[1]]
+    depth = len(grads)
+    part = grads[0].shape[1]
+    block = grads[0].shape[0] // width
+    flat = [*begun, *grads, *rows_of[0], *rows_of[1]]
     for triple in factors:
         flat.extend(triple)
     flat.extend([weights, *slopes, gate_up, down])
 
     def body(*refs):
         refs = list(refs)
-        rep_ref = refs.pop(0)
-        mine_refs = [refs.pop(0) for _ in range(depth)]
-        theirs_refs = [refs.pop(0) for _ in range(depth)]
-        x_mine = [refs.pop(0) for _ in range(width)]
-        x_theirs = [refs.pop(0) for _ in range(width)]
+        rep_ref, started_ref, dn_mine = [refs.pop(0) for _ in range(3)]
+        grad_refs = [refs.pop(0) for _ in range(depth)]
+        x_refs = [[refs.pop(0) for _ in range(width)] for _ in range(2)]
         triples = [[refs.pop(0) for _ in range(3)] for _ in range(width)]
         dn_weight, gu_slope, dn_slope, gu_ref, dn_ref = [refs.pop(0) for _ in range(5)]
         gu_out, dn_out, gu_new, dn_new, sems = refs
         here, there = halves(rep_ref, part)
-        at_of = (here, there)
-
-        def group(which, j):
-            at = slice(j * block, (j + 1) * block)
-            refs_of = (mine_refs, theirs_refs)[which]
-            return jnp.concatenate([ref[at, :] for ref in refs_of], axis=0)
-
-        groups = [[group(which, j) for j in range(width)] for which in range(2)]
         copies = []
 
-        def send(source, target, sem):
-            copy = pltpu.make_async_copy(source, target, sem)
+        def send(source, target):
+            copy = pltpu.make_async_copy(source, target, sems.at[len(copies)])
             copy.start()
             copies.append(copy)
 
-        for which in range(2):
-            at = pl.ds(at_of[which], part)
-            grad = sum(dot(triples[j][0][...], groups[which][j], 1, 0) for j in range(width))
-            dn_new[which] = dn_ref[0, :, at] - dn_slope[0, :, at] * grad
-            send(dn_new.at[which], dn_out.at[0, :, at], sems.at[2 * pair + which])
-        row_grads = []
-        for j in range(width):
-            hidden_grad = dot(dn_weight[0, :, pl.ds(here, part)], groups[0][j], 1, 1) + dot(
-                dn_weight[0, :, pl.ds(there, part)], groups[1][j], 1, 1
-            )
-            row_grads.append(
-                [(hidden_grad * triples[j][1 + i][...]).astype(jnp.bfloat16) for i in range(pair)]
-            )
-        for i in range(pair):
-            for which in range(2):
-                at = pl.ds(at_of[which], part)
-                rows = (x_mine, x_theirs)[which]
-                grad = sum(dot(row_grads[j][i], rows[j][...], 1, 0) for j in range(width))
-                gu_new[i, which] = gu_ref[0, i, :, at] - gu_slope[0, i, :, at] * grad
-                send(gu_new.at[i, which], gu_out.at[0, i, :, at], sems.at[2 * i + which])
+        send(dn_mine, dn_out.at[0, :, pl.ds(here, part)])
+        theirs = joined(grad_refs, block, width)
+        hidden, by_gate, by_up = [
+            jnp.concatenate([triple[n][...] for triple in triples], axis=1) for n in range(3)
+        ]
+        at = pl.ds(there, part)
+        hidden_grad = started_ref[...] + dot(dn_weight[0, :, at], theirs, 1, 1)
+        row_grads = jnp.concatenate(
+            [(hidden_grad * factor).astype(jnp.bfloat16) for factor in (by_gate, by_up)], axis=0
+        )
+        for which, place in enumerate((here, there)):
+            inputs = jnp.concatenate([ref[...] for ref in x_refs[which]], axis=0)
+            grad = dot(row_grads, inputs, 1, 0)
+            at = pl.ds(place, part)
+            for i in range(pair):
+                gu_new[i, which] = (
+                    gu_ref[0, i, :, at] - gu_slope[0, i, :, at] * grad[i * hid : (i + 1) * hid]
+                )
+                send(gu_new.at[i, which], gu_out.at[0, i, :, at])
+        at = pl.ds(there, part)
+        dn_new[...] = dn_ref[0, :, at] - dn_slope[0, :, at] * dot(hidden, theirs, 1, 0)
+        send(dn_new, dn_out.at[0, :, at])
         for copy in copies:
             copy.wait()
 
@@ -321,7 +391,7 @@
         out_shape=[like(gate_up.shape, jnp.float32), like(down.shape, jnp.float32)],
         scratch_shapes=[
             pltpu.VMEM((pair, 2, hid, part), jnp.float32),
-            pltpu.VMEM((2, hid, part), jnp.float32),
+            pltpu.VMEM((hid, part), jnp.float32),
             pltpu.SemaphoreType.DMA((2 * pair + 2,)),
         ],
         compiler_params=pltpu.CompilerParams(vmem_limit_bytes=8 * MEBI),
@@ -347,41 +417,51 @@
             arrived.append(shift(message, "inner", k, way))
         return arrived
 
+    blocks = over_inner([tokens] * depth, ahead)
+    crossed = []
+    for j in range(1, width):
+        crossed.append(shift(tokens, "outer", j))
+    gate_fan = part_width * reps
+    down_fan = down_latent.shape[1] * reps
+    gu_weight, blocks[0], ids, codes = per_entry(
+        weight_of, [gate_up_latent], [gate_fan], bf16, carried=(tokens, expert_ids.T, gate_codes.T)
+    )
+    blocks[-1], gu_weight, late_down = lax.optimization_barrier(
+        (blocks[-1], gu_weight, down_latent)
+    )
+
     def code_of(column):
         expert = ahead(inner, jnp.arange(depth, dtype=jnp.int32), depth) * width + column
-        chosen = expert_ids[None] == expert[:, None, None]
-        return jnp.sum(jnp.where(chosen, gate_codes[None], 0), axis=2)
-
-    blocks = over_inner([tokens] * depth, ahead)
-    gate_fan = part_width * reps
-    down_fan = down_latent.shape[1] * reps
-    (gu_weight,) = per_entry(weight_of, [gate_up_latent], [gate_fan], bf16)
-    blocks[-1], gu_weight = lax.optimization_barrier((blocks[-1], gu_weight))
+        chosen = ids[None] == expert[:, None, None]
+        return jnp.sum(jnp.where(chosen, codes[None], 0), axis=1)
 
     tok_groups = [jnp.concatenate(blocks, axis=0)]
     code_groups = [code_of(outer)]
     pad_rows = -depth % 8
+    rest = (depth - 1) * tok_rows
     for j in range(1, width):
-        codes = code_of(ahead(outer, j, width))
-        pieces = jnp.concatenate([codes // 256, codes % 256], axis=1).astype(bf16)
+        partner_codes = code_of(ahead(outer, j, width))
+        pieces = jnp.concatenate([partner_codes // 256, partner_codes % 256], axis=1).astype(bf16)
         pieces = jnp.pad(pieces, ((0, pad_rows), (0, part_width - 2 * tok_rows)))
-        arrived = shift(jnp.concatenate([tok_groups[0], pieces], axis=0), "outer", j)
-        tok_groups.append(arrived[: depth * tok_rows])
-        pieces = arrived[depth * tok_rows : depth * tok_rows + depth].astype(f32)
+        arrived = shift(jnp.concatenate([*blocks[1:], pieces], axis=0), "outer", j)
+        tok_groups.append(jnp.concatenate([crossed[j - 1], arrived[:rest]], axis=0))
+        pieces = arrived[rest : rest + depth].astype(f32)
         code_groups.append(256.0 * pieces[:, :tok_rows] + pieces[:, tok_rows : 2 * tok_rows])
     gate = jnp.concatenate([c.astype(f32) for c in code_groups], axis=1) / 65536.0
     gate = upright(jnp.pad(gate, ((0, -depth % 8), (0, -gate.shape[1] % 128))))
     gate = gate[: width * tok_rows]
 
-    (dn_weight,) = per_entry(weight_of, [down_latent], [down_fan], bf16)
+    (dn_weight,) = per_entry(weight_of, [late_down], [down_fan], bf16)
     their_groups, factors, keeps, arrivals = [], [], [], []
     for group in tok_groups:
         theirs = other_rep(group)
-        hidden, by_gate, by_up, keep, send = forward(rep, group, theirs, gu_weight, dn_weight)
+        started = project(rep, group, gu_weight)
+        pre, hidden, send = forward(rep, started, theirs, gu_weight, dn_weight)
+        arrivals.append(other_rep(send))
+        keep, by_gate, by_up = keep_share(rep, pre, hidden, dn_weight)
         their_groups.append(theirs)
         factors.append((hidden, by_gate, by_up))
         keeps.append(keep)
-        arrivals.append(other_rep(send))
     messages = list(pack(keeps, arrivals, depth))
 
     latents = [gate_up_latent, down_latent]
@@ -393,18 +473,20 @@
     arrivals = [shift(sent, "outer", step) for step in range(1, width)]
     outgoing = upstream(gate, total, arrivals, teacher, depth)
     grads = over_inner(outgoing, ahead)
-    total, *arrivals, last = lax.optimization_barrier((total, *arrivals, grads[-1]))
-    grads[-1] = last
     mixed = total[:tok_rows]
     for step in range(1, width):
         source = back(0, step, width)
         mixed = mixed + arrivals[step - 1][source * tok_rows : (source + 1) * tok_rows].astype(f32)
     student_out = mixed.astype(bf16)
 
-    their_grads = [other_rep(grad) for grad in grads]
+    their_grads = []
+    for grad in grads:
+        their_grads.append(other_rep(grad))
+    begun = begin(rep, grads, [triple[0] for triple in factors], dn_weight, slopes[1], latents[1])
     new_gate_up, new_down = backward(
         rep,
-        (grads, their_grads),
+        begun,
+        their_grads,
         (tok_groups, their_groups),
         factors,
         dn_weight,

time: 45.1 us -> 46.2 us (1.024)
  waiting for transfers between devices: 13.3 us -> 15.2 us
  local copies, waits for them, and re-layouts: 0.82 us -> 0.05 us
  Pallas kernels: 9.63 us -> 10.4 us
  other arithmetic: 1.67 us -> 0.99 us
    ppermute x19 -> x20, waiting for transfers between devices: 13.3 us -> 15.2 us  [shift(): return lax.ppermute(x, axis, [(i, way(i, step, size)) for i in range(size)])]
    pallas_call x0 -> x5, Pallas kernels: none -> 1.23 us  [the longest x2 0.51 us: project(): pl.pallas_call(body, in_specs=[pl.BlockSpec(memory_space=pltpu.SMEM), who...]
    unnamed x9, local copies, waits for them, and re-layouts: 0.79 us -> 0.02 us
    reduce_sum x1, other arithmetic: 0.79 us -> 0.09 us  [code_of(): return jnp.sum(jnp.where(chosen, codes[None], 0), axis=1)]
    ppermute x19 -> x20, starting transfers between devices: 18.6 us -> 18.5 us  [shift(): return lax.ppermute(x, axis, [(i, way(i, step, size)) for i in range(size)])]
  transfers between devices with their start and end apart: 19 -> 20, of which waited for: 10 -> 9; matrix products, arithmetic and copies ran while one was open for 5% -> 2% of each run, Pallas kernels for 16% -> 18%
where the time goes in v5:
time: 46.2 us; the launch traced here: 46.1 us
  starting transfers between devices  18.5 us (40%)
  waiting for transfers between devices  15.2 us (33%)
  Pallas kernels  10.4 us (23%)
  other arithmetic  0.99 us (2%)
  between operations  0.87 us (2%)
    ppermute x20, starting transfers between devices, shift(): return lax.ppermute(x, axis, [(i, way(i, step, size)) for i in range(size)])  18.5 us
    ppermute x20, waiting for transfers between devices, shift(): return lax.ppermute(x, axis, [(i, way(i, step, size)) for i in range(size)])  15.2 us
    pallas_call x3, Pallas kernels, per_entry(): pl.pallas_call(body, in_specs=[pl.BlockSpec(memory_space=pltpu.HBM) for _...  5.99 us
    pallas_call x1, Pallas kernels, backward(): pl.pallas_call(body, in_specs=[pl.BlockSpec(memory_space=pltpu.SMEM)] + [...  1.89 us
    pallas_call x2, Pallas kernels, forward(): pl.pallas_call(body, in_specs=[pl.BlockSpec(memory_space=pltpu.SMEM)] + [...  0.94 us
  transfers between devices with their start and end apart: 20, of which 9 were waited for; matrix products, arithmetic and copies ran while one was open for 2% of the time, Pallas kernels for 18%

profile of v5, /device:TPU:0, one launch (start us, length us, event | category | flops | bytes accessed | tf_op | source)
XLA Modules:
  0.0 46.1 jit_solution(15022849844404414620)
XLA Ops:
  0.6 3.0 %collective-permute-start.5 = (bf16[32,512]{1,0:T(8,128)(2,1)}, bf16[32,512]{1,0:T(8,128)(2,1)S(1)}, u32[]{:S(2)}, u32[]{:S(2)}) collective-permute-start(bf16[32,512]{1,0:T(8,128)(2,1)} %refs_1_.2), channel_id=1, source_target_pairs={{0,2},{2,0},{1,3},{3,1},{4,6},{6,4},{5,7},{7,5},{8,10},{10,8},{9,1... | collective-permute-start | bytes 98312 | tf_op jit(solution)/shard_map/ppermute | solution.py:47
  3.7 3.6 %collective-permute-start.2 = (bf16[32,512]{1,0:T(8,128)(2,1)}, bf16[32,512]{1,0:T(8,128)(2,1)S(1)}, u32[]{:S(2)}, u32[]{:S(2)}) collective-permute-start(bf16[32,512]{1,0:T(8,128)(2,1)} %refs_1_.2), channel_id=1, source_target_pairs={{0,12},{4,8},{8,4},{12,0},{1,13},{5,9},{9,5},{13,1},{2,14},{6,10},... | collective-permute-start | bytes 98312 | tf_op jit(solution)/shard_map/ppermute | solution.py:47
  7.3 0.0 collective-permute-start.1
  7.3 0.8 %collective-permute-start = (bf16[32,512]{1,0:T(8,128)(2,1)}, bf16[32,512]{1,0:T(8,128)(2,1)S(1)}, u32[]{:S(2)}, u32[]{:S(2)}) collective-permute-start(bf16[32,512]{1,0:T(8,128)(2,1)} %refs_1_.2), channel_id=1, source_target_pairs={{0,4},{4,0},{8,12},{12,8},{1,5},{5,1},{9,13},{13,9},{2,6},{6,2},{1... | collective-permute-start | bytes 98312 | tf_op jit(solution)/shard_map/ppermute | solution.py:47
  8.1 2.0 %shard_map.85 = (bf16[1,2,192,1024]{3,2,1,0:T(8,128)(2,1)S(1)}, bf16[32,512]{1,0:T(8,128)(2,1)S(1)}, s32[8,32]{1,0:T(8,128)S(1)}, s32[8,32]{1,0:T(8,128)S(1)}) custom-call(f32[1,2,192,1024]{3,2,1,0:T(8,128)} %refs_20_, bf16[32,512]{1,0:T(8,128)(2,1)} %refs_1_.2, s32[8,32]{1,0:T(8,128)} %bitcast.3, s32[8,32]{1,0:T(8,128)} %bitcast.4), custom_call_target="tpu_custom_call" | custom-call | tf_op jit(solution)/shard_map/pallas_call | solution.py:127
  10.0 0.1 select_reduce_fusion.1
  10.2 0.1 fusion.5
  10.2 0.0 collective-permute-done.2
  10.3 2.0 %collective-permute-done.1 = bf16[32,512]{1,0:T(8,128)(2,1)S(1)} collective-permute-done((bf16[32,512]{1,0:T(8,128)(2,1)}, bf16[32,512]{1,0:T(8,128)(2,1)S(1)}, u32[]{:S(2)}, u32[]{:S(2)}) %collective-permute-start.1) | collective-permute-done | bytes 32800 | tf_op jit(solution)/shard_map/ppermute | solution.py:47
  12.3 0.0 collective-permute-done
  12.3 0.6 %collective-permute-start.3 = (bf16[104,512]{1,0:T(8,128)(2,1)S(1)}, bf16[104,512]{1,0:T(8,128)(2,1)S(1)}, u32[]{:S(2)}, u32[]{:S(2)}) collective-permute-start(bf16[104,512]{1,0:T(8,128)(2,1)S(1)} %pad_maximum_fusion.1), channel_id=1, source_target_pairs={{0,2},{2,0},{1,3},{3,1},{4,6},{6,4},{5,7},{7,5},{8,10},{10,8},{9,1... | collective-permute-start | bytes 319496 | tf_op jit(solution)/shard_map/ppermute | solution.py:47
  12.9 0.1 collective-permute-start.4
  13.0 1.4 %shard_map.86.dn_ref.refs_6_.refs_17_ = bf16[1,192,1024]{2,1,0:T(8,128)(2,1)S(1)} custom-call(f32[1,192,1024]{2,1,0:T(8,128)} %refs_21_), custom_call_target="tpu_custom_call" | custom-call | tf_op jit(solution)/shard_map/pallas_call | solution.py:127
  14.5 0.3 project.2.started_ref
  14.7 2.4 %collective-permute-done.3 = bf16[104,512]{1,0:T(8,128)(2,1)S(1)} collective-permute-done((bf16[104,512]{1,0:T(8,128)(2,1)S(1)}, bf16[104,512]{1,0:T(8,128)(2,1)S(1)}, u32[]{:S(2)}, u32[]{:S(2)}) %collective-permute-start.3) | collective-permute-done | bytes 106528 | tf_op jit(solution)/shard_map/ppermute | solution.py:47
  17.1 0.0 collective-permute-done.5
  17.1 0.1 collective-permute-start.6
  17.2 0.3 project.3.started_ref
  17.5 0.0 collective-permute-done.4.theirs_ref.refs_9_
  17.5 0.5 %forward.2 = (f32[2,192,128]{2,1,0:T(8,128)S(1)}, bf16[192,128]{1,0:T(8,128)(2,1)S(1)}, bf16[128,512]{1,0:T(8,128)(2,1)S(1)}) custom-call(s32[1]{0:T(128)} %bitcast.rep_ref.refs_0_, f32[2,192,128]{2,1,0:T(8,128)S(1)} %project.2.started_ref, bf16[128,512]{1,0:T(8,128)(2,1)S(1)} %collective-permute-done.4.theirs_ref.refs_9_, ...), custom_call_target="tpu_custom_call" | custom-call | tf_op jit(solution)/shard_map/forward/pallas_call | solution.py:175
  18.0 0.6 %collective-permute-start.7 = (bf16[128,512]{1,0:T(8,128)(2,1)S(1)}, bf16[128,512]{1,0:T(8,128)(2,1)S(1)}, u32[]{:S(2)}, u32[]{:S(2)}) collective-permute-start(bf16[128,512]{1,0:T(8,128)(2,1)S(1)} %get-tuple-element.65), channel_id=1, source_target_pairs={{0,1},{1,0},{2,3},{3,2},{4,5},{5,4},{6,7},{7,6},{8,9},{9,8},{10,11... | collective-permute-start | bytes 393224 | tf_op jit(solution)/shard_map/ppermute | solution.py:47
  18.5 0.0 collective-permute-done.6.theirs_ref.refs_10_
  18.5 0.5 %forward.3 = (f32[2,192,128]{2,1,0:T(8,128)S(1)}, bf16[192,128]{1,0:T(8,128)(2,1)S(1)}, bf16[128,512]{1,0:T(8,128)(2,1)S(1)}) custom-call(s32[1]{0:T(128)} %bitcast.rep_ref.refs_0_, f32[2,192,128]{2,1,0:T(8,128)S(1)} %project.3.started_ref, bf16[128,512]{1,0:T(8,128)(2,1)S(1)} %collective-permute-done.6.theirs_ref.refs_10_, ...), custom_call_target="tpu_custom_call" | custom-call | tf_op jit(solution)/shard_map/forward/pallas_call | solution.py:175
  19.0 0.2 collective-permute-start.8
  19.2 0.1 slice_add_fusion
  19.3 0.2 keep_share.2
  19.5 0.2 keep_share.3
  19.7 0.0 collective-permute-done.7.refs_2_
  19.7 0.7 %collective-permute-done.8.refs_3_ = bf16[128,512]{1,0:T(8,128)(2,1)S(1)} collective-permute-done((bf16[128,512]{1,0:T(8,128)(2,1)S(1)}, bf16[128,512]{1,0:T(8,128)(2,1)S(1)}, u32[]{:S(2)}, u32[]{:S(2)}) %collective-permute-start.8) | collective-permute-done | bytes 131104 | tf_op jit(solution)/shard_map/ppermute | solution.py:47
  20.4 0.0 copy-start.2
  20.5 0.1 collective-permute-start.9
  20.6 2.1 %collective-permute-start.10 = (bf16[64,512]{1,0:T(8,128)(2,1)S(1)}, bf16[64,512]{1,0:T(8,128)(2,1)S(1)}, u32[]{:S(2)}, u32[]{:S(2)}) collective-permute-start(bf16[64,512]{1,0:T(8,128)(2,1)S(1)} %get-tuple-element.70), channel_id=1, source_target_pairs={{0,8},{4,12},{8,0},{12,4},{1,9},{5,13},{9,1},{13,5},{2,10},{6,14},... | collective-permute-start | bytes 196616 | tf_op jit(solution)/shard_map/ppermute | solution.py:47
  22.7 2.2 %collective-permute-start.11 = (bf16[64,512]{1,0:T(8,128)(2,1)S(1)}, bf16[64,512]{1,0:T(8,128)(2,1)S(1)}, u32[]{:S(2)}, u32[]{:S(2)}) collective-permute-start(bf16[64,512]{1,0:T(8,128)(2,1)S(1)} %get-tuple-element.71), channel_id=1, source_target_pairs={{0,12},{4,8},{8,4},{12,0},{1,13},{5,9},{9,5},{13,1},{2,14},{6,10},... | collective-permute-start | bytes 196616 | tf_op jit(solution)/shard_map/ppermute | solution.py:47
  24.9 0.1 maximum_multiply_fusion
  25.0 0.1 upright.1
  25.1 2.6 %shard_map.87 = (f32[1,2,192,1024]{3,2,1,0:T(8,128)S(1)}, f32[1,192,1024]{2,1,0:T(8,128)S(1)}) custom-call(f32[1,2,192,1024]{3,2,1,0:T(8,128)} %refs_20_, f32[1,192,1024]{2,1,0:T(8,128)} %refs_21_), custom_call_target="tpu_custom_call" | custom-call | tf_op jit(solution)/shard_map/pallas_call | solution.py:127
  27.7 0.0 copy-start
  27.7 1.2 %collective-permute-done.11.refs_5_ = bf16[64,512]{1,0:T(8,128)(2,1)S(1)} collective-permute-done((bf16[64,512]{1,0:T(8,128)(2,1)S(1)}, bf16[64,512]{1,0:T(8,128)(2,1)S(1)}, u32[]{:S(2)}, u32[]{:S(2)}) %collective-permute-start.11) | collective-permute-done | bytes 65568 | tf_op jit(solution)/shard_map/ppermute | solution.py:47
  29.0 0.0 collective-permute-done.9.refs_3_
  29.0 0.0 collective-permute-done.10.refs_4_
  29.0 0.0 copy-done.2
  29.0 0.1 mix.1
  29.1 0.6 %collective-permute-start.12 = (bf16[64,512]{1,0:T(8,128)(2,1)S(1)}, bf16[64,512]{1,0:T(8,128)(2,1)S(1)}, u32[]{:S(2)}, u32[]{:S(2)}) collective-permute-start(bf16[64,512]{1,0:T(8,128)(2,1)S(1)} %get-tuple-element.78), channel_id=1, source_target_pairs={{0,2},{2,0},{1,3},{3,1},{4,6},{6,4},{5,7},{7,5},{8,10},{10,8},{9,1... | collective-permute-start | bytes 196616 | tf_op jit(solution)/shard_map/ppermute | solution.py:47
  29.7 3.7 %collective-permute-done.12.refs_3_ = bf16[64,512]{1,0:T(8,128)(2,1)S(1)} collective-permute-done((bf16[64,512]{1,0:T(8,128)(2,1)S(1)}, bf16[64,512]{1,0:T(8,128)(2,1)S(1)}, u32[]{:S(2)}, u32[]{:S(2)}) %collective-permute-start.12) | collective-permute-done | bytes 65568 | tf_op jit(solution)/shard_map/ppermute | solution.py:47
  33.4 0.1 upstream.1
  33.5 1.7 %collective-permute-start.13 = (bf16[64,512]{1,0:T(8,128)(2,1)S(1)}, bf16[64,512]{1,0:T(8,128)(2,1)S(1)}, u32[]{:S(2)}, u32[]{:S(2)}) collective-permute-start(bf16[64,512]{1,0:T(8,128)(2,1)S(1)} %get-tuple-element.80), channel_id=1, source_target_pairs={{0,4},{4,0},{8,12},{12,8},{1,5},{5,1},{9,13},{13,9},{2,6},{6,2},{1... | collective-permute-start | bytes 196616 | tf_op jit(solution)/shard_map/ppermute | solution.py:47
  35.2 1.5 %collective-permute-start.14 = (bf16[64,512]{1,0:T(8,128)(2,1)S(1)}, bf16[64,512]{1,0:T(8,128)(2,1)S(1)}, u32[]{:S(2)}, u32[]{:S(2)}) collective-permute-start(bf16[64,512]{1,0:T(8,128)(2,1)S(1)} %get-tuple-element.81), channel_id=1, source_target_pairs={{0,8},{4,12},{8,0},{12,4},{1,9},{5,13},{9,1},{13,5},{2,10},{6,14},... | collective-permute-start | bytes 196616 | tf_op jit(solution)/shard_map/ppermute | solution.py:47
  36.8 1.3 %collective-permute-start.15 = (bf16[64,512]{1,0:T(8,128)(2,1)S(1)}, bf16[64,512]{1,0:T(8,128)(2,1)S(1)}, u32[]{:S(2)}, u32[]{:S(2)}) collective-permute-start(bf16[64,512]{1,0:T(8,128)(2,1)S(1)} %get-tuple-element.82), channel_id=1, source_target_pairs={{0,12},{4,8},{8,4},{12,0},{1,13},{5,9},{9,5},{13,1},{2,14},{6,10},... | collective-permute-start | bytes 196616 | tf_op jit(solution)/shard_map/ppermute | solution.py:47
  38.0 0.0 collective-permute-start.16
  38.0 0.4 collective-permute-done.13.refs_1_
  38.4 0.1 collective-permute-start.17
  38.5 3.2 %collective-permute-done.14.refs_2_ = bf16[64,512]{1,0:T(8,128)(2,1)S(1)} collective-permute-done((bf16[64,512]{1,0:T(8,128)(2,1)S(1)}, bf16[64,512]{1,0:T(8,128)(2,1)S(1)}, u32[]{:S(2)}, u32[]{:S(2)}) %collective-permute-start.14) | collective-permute-done | bytes 65568 | tf_op jit(solution)/shard_map/ppermute | solution.py:47
  41.7 0.0 collective-permute-start.18
  41.7 1.2 %collective-permute-done.15.refs_3_ = bf16[64,512]{1,0:T(8,128)(2,1)S(1)} collective-permute-done((bf16[64,512]{1,0:T(8,128)(2,1)S(1)}, bf16[64,512]{1,0:T(8,128)(2,1)S(1)}, u32[]{:S(2)}, u32[]{:S(2)}) %collective-permute-start.15) | collective-permute-done | bytes 65568 | tf_op jit(solution)/shard_map/ppermute | solution.py:47
  42.9 0.0 collective-permute-start.19
  42.9 0.6 %add_convert_fusion = bf16[32,512]{1,0:T(8,128)(2,1)} fusion(f32[64,512]{1,0:T(8,128)S(1)} %get-tuple-element.77.refs_2_, bf16[64,512]{1,0:T(8,128)(2,1)S(1)} %collective-permute-done.12.refs_3_), kind=kLoop, calls=%fused_computation.2 | loop fusion | flops 49152 | bytes 131072 | tf_op jit(solution)/shard_map/convert_element_type | solution.py:480
  43.6 0.0 copy-done.1
  43.6 0.3 begin.1
  43.9 0.0 collective-permute-done.16.refs_3_
  43.9 0.0 collective-permute-done.17.refs_4_
  43.9 0.0 collective-permute-done.18.refs_5_
  43.9 0.3 collective-permute-done.19.refs_6_
  44.2 0.0 copy-done
  44.2 1.9 %backward.1 = (f32[1,2,192,1024]{3,2,1,0:T(8,128)}, f32[1,192,1024]{2,1,0:T(8,128)}) custom-call(s32[1]{0:T(128)} %bitcast.rep_ref.refs_0_, f32[192,256]{1,0:T(8,128)S(1)} %get-tuple-element.84.refs_1_, f32[192,512]{1,0:T(8,128)S(1)} %get-tuple-element.85.refs_2_, bf16[64,512]{1,0:T(8,128)(2,1)S(1)} %collective-permute-done.16.refs_3_, ...), custom_call_target="tpu_custom_call" | custom-call | tf_op jit(solution)/shard_map/backward/pallas_call | solution.py:387
  (15 shorter events, 0.1 us)
Async XLA Ops:
  0.6 16.5 %collective-permute-start.5 = (bf16[32,512]{1,0:T(8,128)(2,1)}, bf16[32,512]{1,0:T(8,128)(2,1)S(1)}, u32[]{:S(2)}, u32[]{:S(2)}) collective-permute-start(bf16[32,512]{1,0:T(8,128)(2,1)} %refs_1_.2), channel_id=1, source_target_pairs={{0,2},{2,0},{1,3},{3,1},{4,6},{6,4},{5,7},{7,5},{8,10},{10,8},{9,1... | collective-permute-start | bytes 98312 | tf_op jit(solution)/shard_map/ppermute | solution.py:47
  3.7 6.6 %collective-permute-start.2 = (bf16[32,512]{1,0:T(8,128)(2,1)}, bf16[32,512]{1,0:T(8,128)(2,1)S(1)}, u32[]{:S(2)}, u32[]{:S(2)}) collective-permute-start(bf16[32,512]{1,0:T(8,128)(2,1)} %refs_1_.2), channel_id=1, source_target_pairs={{0,12},{4,8},{8,4},{12,0},{1,13},{5,9},{9,5},{13,1},{2,14},{6,10},... | collective-permute-start | bytes 98312 | tf_op jit(solution)/shard_map/ppermute | solution.py:47
  7.3 5.0 %collective-permute-start.1 = (bf16[32,512]{1,0:T(8,128)(2,1)}, bf16[32,512]{1,0:T(8,128)(2,1)S(1)}, u32[]{:S(2)}, u32[]{:S(2)}) collective-permute-start(bf16[32,512]{1,0:T(8,128)(2,1)} %refs_1_.2), channel_id=1, source_target_pairs={{0,8},{4,12},{8,0},{12,4},{1,9},{5,13},{9,1},{13,5},{2,10},{6,14},... | collective-permute-start | bytes 98312 | tf_op jit(solution)/shard_map/ppermute | solution.py:47
  7.3 5.0 %collective-permute-start = (bf16[32,512]{1,0:T(8,128)(2,1)}, bf16[32,512]{1,0:T(8,128)(2,1)S(1)}, u32[]{:S(2)}, u32[]{:S(2)}) collective-permute-start(bf16[32,512]{1,0:T(8,128)(2,1)} %refs_1_.2), channel_id=1, source_target_pairs={{0,4},{4,0},{8,12},{12,8},{1,5},{5,1},{9,13},{13,9},{2,6},{6,2},{1... | collective-permute-start | bytes 98312 | tf_op jit(solution)/shard_map/ppermute | solution.py:47
  12.3 4.8 %collective-permute-start.3 = (bf16[104,512]{1,0:T(8,128)(2,1)S(1)}, bf16[104,512]{1,0:T(8,128)(2,1)S(1)}, u32[]{:S(2)}, u32[]{:S(2)}) collective-permute-start(bf16[104,512]{1,0:T(8,128)(2,1)S(1)} %pad_maximum_fusion.1), channel_id=1, source_target_pairs={{0,2},{2,0},{1,3},{3,1},{4,6},{6,4},{5,7},{7,5},{8,10},{10,8},{9,1... | collective-permute-start | bytes 319496 | tf_op jit(solution)/shard_map/ppermute | solution.py:47
  12.9 4.6 %collective-permute-start.4 = (bf16[128,512]{1,0:T(8,128)(2,1)S(1)}, bf16[128,512]{1,0:T(8,128)(2,1)S(1)}, u32[]{:S(2)}, u32[]{:S(2)}) collective-permute-start(bf16[128,512]{1,0:T(8,128)(2,1)S(1)} %constant_dynamic-update-slice_fusion.mine_ref.refs_7_), channel_id=1, source_target_pairs={{0,1},{1,0},{2,3},{3,2},{4,5},{5,4},{6,7},{7,6},{8,9},{9,8},{10,11... | collective-permute-start | bytes 393224 | tf_op jit(solution)/shard_map/ppermute | solution.py:47
  17.1 1.4 %collective-permute-start.6 = (bf16[128,512]{1,0:T(8,128)(2,1)S(1)}, bf16[128,512]{1,0:T(8,128)(2,1)S(1)}, u32[]{:S(2)}, u32[]{:S(2)}) collective-permute-start(bf16[128,512]{1,0:T(8,128)(2,1)S(1)} %pad_maximum_fusion.mine_ref.refs_8_), channel_id=1, source_target_pairs={{0,1},{1,0},{2,3},{3,2},{4,5},{5,4},{6,7},{7,6},{8,9},{9,8},{10,11... | collective-permute-start | bytes 393224 | tf_op jit(solution)/shard_map/ppermute | solution.py:47
  18.0 1.8 %collective-permute-start.7 = (bf16[128,512]{1,0:T(8,128)(2,1)S(1)}, bf16[128,512]{1,0:T(8,128)(2,1)S(1)}, u32[]{:S(2)}, u32[]{:S(2)}) collective-permute-start(bf16[128,512]{1,0:T(8,128)(2,1)S(1)} %get-tuple-element.65), channel_id=1, source_target_pairs={{0,1},{1,0},{2,3},{3,2},{4,5},{5,4},{6,7},{7,6},{8,9},{9,8},{10,11... | collective-permute-start | bytes 393224 | tf_op jit(solution)/shard_map/ppermute | solution.py:47
  19.0 1.4 %collective-permute-start.8 = (bf16[128,512]{1,0:T(8,128)(2,1)S(1)}, bf16[128,512]{1,0:T(8,128)(2,1)S(1)}, u32[]{:S(2)}, u32[]{:S(2)}) collective-permute-start(bf16[128,512]{1,0:T(8,128)(2,1)S(1)} %get-tuple-element.66), channel_id=1, source_target_pairs={{0,1},{1,0},{2,3},{3,2},{4,5},{5,4},{6,7},{7,6},{8,9},{9,8},{10,11... | collective-permute-start | bytes 393224 | tf_op jit(solution)/shard_map/ppermute | solution.py:47
  20.4 8.5 %copy-start.2 = (bf16[32,512]{1,0:T(8,128)(2,1)S(1)}, bf16[32,512]{1,0:T(8,128)(2,1)}, u32[]{:S(2)}) copy-start(bf16[32,512]{1,0:T(8,128)(2,1)} %refs_1_.5) | copy-start | bytes 98308
  20.5 8.5 %collective-permute-start.9 = (bf16[64,512]{1,0:T(8,128)(2,1)S(1)}, bf16[64,512]{1,0:T(8,128)(2,1)S(1)}, u32[]{:S(2)}, u32[]{:S(2)}) collective-permute-start(bf16[64,512]{1,0:T(8,128)(2,1)S(1)} %get-tuple-element.69), channel_id=1, source_target_pairs={{0,4},{4,0},{8,12},{12,8},{1,5},{5,1},{9,13},{13,9},{2,6},{6,2},{1... | collective-permute-start | bytes 196616 | tf_op jit(solution)/shard_map/ppermute | solution.py:47
  20.6 8.4 %collective-permute-start.10 = (bf16[64,512]{1,0:T(8,128)(2,1)S(1)}, bf16[64,512]{1,0:T(8,128)(2,1)S(1)}, u32[]{:S(2)}, u32[]{:S(2)}) collective-permute-start(bf16[64,512]{1,0:T(8,128)(2,1)S(1)} %get-tuple-element.70), channel_id=1, source_target_pairs={{0,8},{4,12},{8,0},{12,4},{1,9},{5,13},{9,1},{13,5},{2,10},{6,14},... | collective-permute-start | bytes 196616 | tf_op jit(solution)/shard_map/ppermute | solution.py:47
  22.7 6.3 %collective-permute-start.11 = (bf16[64,512]{1,0:T(8,128)(2,1)S(1)}, bf16[64,512]{1,0:T(8,128)(2,1)S(1)}, u32[]{:S(2)}, u32[]{:S(2)}) collective-permute-start(bf16[64,512]{1,0:T(8,128)(2,1)S(1)} %get-tuple-element.71), channel_id=1, source_target_pairs={{0,12},{4,8},{8,4},{12,0},{1,13},{5,9},{9,5},{13,1},{2,14},{6,10},... | collective-permute-start | bytes 196616 | tf_op jit(solution)/shard_map/ppermute | solution.py:47
  25.1 18.4 %copy-start.1 = (f32[1,192,1024]{2,1,0:T(8,128)S(1)}, f32[1,192,1024]{2,1,0:T(8,128)}, u32[]{:S(2)}) copy-start(f32[1,192,1024]{2,1,0:T(8,128)} %refs_21_) | copy-start | bytes 2359300
  27.7 16.5 %copy-start = (f32[1,2,192,1024]{3,2,1,0:T(8,128)S(1)}, f32[1,2,192,1024]{3,2,1,0:T(8,128)}, u32[]{:S(2)}) copy-start(f32[1,2,192,1024]{3,2,1,0:T(8,128)} %refs_20_) | copy-start | bytes 4718596
  29.1 4.3 %collective-permute-start.12 = (bf16[64,512]{1,0:T(8,128)(2,1)S(1)}, bf16[64,512]{1,0:T(8,128)(2,1)S(1)}, u32[]{:S(2)}, u32[]{:S(2)}) collective-permute-start(bf16[64,512]{1,0:T(8,128)(2,1)S(1)} %get-tuple-element.78), channel_id=1, source_target_pairs={{0,2},{2,0},{1,3},{3,1},{4,6},{6,4},{5,7},{7,5},{8,10},{10,8},{9,1... | collective-permute-start | bytes 196616 | tf_op jit(solution)/shard_map/ppermute | solution.py:47
  33.5 4.9 %collective-permute-start.13 = (bf16[64,512]{1,0:T(8,128)(2,1)S(1)}, bf16[64,512]{1,0:T(8,128)(2,1)S(1)}, u32[]{:S(2)}, u32[]{:S(2)}) collective-permute-start(bf16[64,512]{1,0:T(8,128)(2,1)S(1)} %get-tuple-element.80), channel_id=1, source_target_pairs={{0,4},{4,0},{8,12},{12,8},{1,5},{5,1},{9,13},{13,9},{2,6},{6,2},{1... | collective-permute-start | bytes 196616 | tf_op jit(solution)/shard_map/ppermute | solution.py:47
  35.2 6.5 %collective-permute-start.14 = (bf16[64,512]{1,0:T(8,128)(2,1)S(1)}, bf16[64,512]{1,0:T(8,128)(2,1)S(1)}, u32[]{:S(2)}, u32[]{:S(2)}) collective-permute-start(bf16[64,512]{1,0:T(8,128)(2,1)S(1)} %get-tuple-element.81), channel_id=1, source_target_pairs={{0,8},{4,12},{8,0},{12,4},{1,9},{5,13},{9,1},{13,5},{2,10},{6,14},... | collective-permute-start | bytes 196616 | tf_op jit(solution)/shard_map/ppermute | solution.py:47
  36.8 6.2 %collective-permute-start.15 = (bf16[64,512]{1,0:T(8,128)(2,1)S(1)}, bf16[64,512]{1,0:T(8,128)(2,1)S(1)}, u32[]{:S(2)}, u32[]{:S(2)}) collective-permute-start(bf16[64,512]{1,0:T(8,128)(2,1)S(1)} %get-tuple-element.82), channel_id=1, source_target_pairs={{0,12},{4,8},{8,4},{12,0},{1,13},{5,9},{9,5},{13,1},{2,14},{6,10},... | collective-permute-start | bytes 196616 | tf_op jit(solution)/shard_map/ppermute | solution.py:47
  38.0 5.8 %collective-permute-start.16 = (bf16[64,512]{1,0:T(8,128)(2,1)S(1)}, bf16[64,512]{1,0:T(8,128)(2,1)S(1)}, u32[]{:S(2)}, u32[]{:S(2)}) collective-permute-start(bf16[64,512]{1,0:T(8,128)(2,1)S(1)} %get-tuple-element.79.refs_0_), channel_id=1, source_target_pairs={{0,1},{1,0},{2,3},{3,2},{4,5},{5,4},{6,7},{7,6},{8,9},{9,8},{10,11... | collective-permute-start | bytes 196616 | tf_op jit(solution)/shard_map/ppermute | solution.py:47
  38.4 5.4 %collective-permute-start.17 = (bf16[64,512]{1,0:T(8,128)(2,1)S(1)}, bf16[64,512]{1,0:T(8,128)(2,1)S(1)}, u32[]{:S(2)}, u32[]{:S(2)}) collective-permute-start(bf16[64,512]{1,0:T(8,128)(2,1)S(1)} %collective-permute-done.13.refs_1_), channel_id=1, source_target_pairs={{0,1},{1,0},{2,3},{3,2},{4,5},{5,4},{6,7},{7,6},{8,9},{9,8},{10,11... | collective-permute-start | bytes 196616 | tf_op jit(solution)/shard_map/ppermute | solution.py:47
  41.7 2.2 %collective-permute-start.18 = (bf16[64,512]{1,0:T(8,128)(2,1)S(1)}, bf16[64,512]{1,0:T(8,128)(2,1)S(1)}, u32[]{:S(2)}, u32[]{:S(2)}) collective-permute-start(bf16[64,512]{1,0:T(8,128)(2,1)S(1)} %collective-permute-done.14.refs_2_), channel_id=1, source_target_pairs={{0,1},{1,0},{2,3},{3,2},{4,5},{5,4},{6,7},{7,6},{8,9},{9,8},{10,11... | collective-permute-start | bytes 196616 | tf_op jit(solution)/shard_map/ppermute | solution.py:47
  42.9 1.3 %collective-permute-start.19 = (bf16[64,512]{1,0:T(8,128)(2,1)S(1)}, bf16[64,512]{1,0:T(8,128)(2,1)S(1)}, u32[]{:S(2)}, u32[]{:S(2)}) collective-permute-start(bf16[64,512]{1,0:T(8,128)(2,1)S(1)} %collective-permute-done.15.refs_3_), channel_id=1, source_target_pairs={{0,1},{1,0},{2,3},{3,2},{4,5},{5,4},{6,7},{7,6},{8,9},{9,8},{10,11... | collective-permute-start | bytes 196616 | tf_op jit(solution)/shard_map/ppermute | solution.py:47

commit v6 on v5

--- a/solution.py
+++ b/solution.py
@@ -92,7 +92,31 @@
     )(gate)
 
 
-def per_entry(rule, latents, fans, dtype, carried=()):
+def fetch(arrays):
+    count = len(arrays)
+
+    def body(*refs):
+        sems = refs[-1]
+        copies = [
+            pltpu.make_async_copy(refs[n], refs[count + n], sems.at[n]) for n in range(count)
+        ]
+        for copy in copies:
+            copy.start()
+        for copy in copies:
+            copy.wait()
+
+    return pl.pallas_call(
+        body,
+        in_specs=[pl.BlockSpec(memory_space=pltpu.HBM) for _ in arrays],
+        out_specs=[whole() for _ in arrays],
+        out_shape=[like(array.shape, array.dtype) for array in arrays],
+        scratch_shapes=[pltpu.SemaphoreType.DMA((count,))],
+        compiler_params=pltpu.CompilerParams(vmem_limit_bytes=2 * MEBI),
+        name="fetch",
+    )(*[pltpu.with_memory_space_constraint(array, pltpu.HBM) for array in arrays])
+
+
+def row_pieces(latents):
     pieces = []
     for n, latent in enumerate(latents):
         cuts = 2 if latent.shape[-2] % 32 == 0 else 1
@@ -100,42 +124,52 @@
         lead = [()]
         for size in latent.shape[:-2]:
             lead = [(*at, i) for at in lead for i in range(size)]
-        pieces.extend((n, at, c * rows) for at in lead for c in range(cuts))
-    wide = latents[0].shape[-1]
+        pieces.extend((n, (*at, pl.ds(c * rows, rows))) for at in lead for c in range(cuts))
+    return pieces
+
+
+def weights_of(latents, fans):
+    pieces = row_pieces(latents)
+    count = len(latents)
 
     def body(*refs):
-        count = len(latents) + len(carried)
-        sources = refs[:count]
-        targets = refs[count:-2]
-        held, sems = refs[-2:]
+        sems = refs[-1]
         copies = []
-        for n in range(len(latents), count):
-            sem = sems.at[len(pieces) + n - len(latents)]
-            copies.append(pltpu.make_async_copy(sources[n], targets[n], sem))
-            copies[-1].start()
-        for slot, (n, at, row) in enumerate(pieces):
-            source = sources[n].at[(*at, pl.ds(row, rows))]
-            copies.append(pltpu.make_async_copy(source, held.at[slot], sems.at[slot]))
-            copies[-1].start()
-        for slot, (n, at, row) in enumerate(pieces):
-            copies[len(carried) + slot].wait()
-            targets[n][(*at, pl.ds(row, rows))] = rule(held[slot], fans[n])
-        for copy in copies[: len(carried)]:
+        for slot, (n, at) in enumerate(pieces):
+            copy = pltpu.make_async_copy(refs[n].at[at], refs[count + n].at[at], sems.at[slot])
+            copy.start()
+            copies.append(copy)
+        for copy, (n, at) in zip(copies, pieces):
             copy.wait()
-
-    inputs = [*latents, *carried]
-    return pl.pallas_call(
-        body,
-        in_specs=[pl.BlockSpec(memory_space=pltpu.HBM) for _ in inputs],
-        out_specs=[whole() for _ in inputs],
-        out_shape=[like(latent.shape, dtype) for latent in latents]
-        + [like(array.shape, array.dtype) for array in carried],
-        scratch_shapes=[
-            pltpu.VMEM((len(pieces), rows, wide), jnp.float32),
-            pltpu.SemaphoreType.DMA((len(pieces) + len(carried),)),
-        ],
-        compiler_params=pltpu.CompilerParams(vmem_limit_bytes=8 * MEBI),
-    )(*[pltpu.with_memory_space_constraint(array, pltpu.HBM) for array in inputs])
+            refs[2 * count + n][at] = weight_of(refs[count + n][at], fans[n])
+
+    return pl.pallas_call(
+        body,
+        in_specs=[pl.BlockSpec(memory_space=pltpu.HBM) for _ in latents],
+        out_specs=[whole() for _ in range(2 * count)],
+        out_shape=[like(latent.shape, latent.dtype) for latent in latents]
+        + [like(latent.shape, jnp.bfloat16) for latent in latents],
+        scratch_shapes=[pltpu.SemaphoreType.DMA((len(pieces),))],
+        compiler_params=pltpu.CompilerParams(vmem_limit_bytes=4 * MEBI),
+        name="weights",
+    )(*[pltpu.with_memory_space_constraint(latent, pltpu.HBM) for latent in latents])
+
+
+def slopes_of(latents, fans):
+    pieces = row_pieces(latents)
+
+    def body(*refs):
+        for n, at in pieces:
+            refs[len(latents) + n][at] = slope_of(refs[n][at], fans[n])
+
+    return pl.pallas_call(
+        body,
+        in_specs=[whole() for _ in latents],
+        out_specs=[whole() for _ in latents],
+        out_shape=[like(latent.shape, latent.dtype) for latent in latents],
+        compiler_params=pltpu.CompilerParams(vmem_limit_bytes=4 * MEBI),
+        name="slopes",
+    )(*latents)
 
 
 def project(rep, mine, gu_weight):
@@ -364,23 +398,18 @@
         hidden, by_gate, by_up = [
             jnp.concatenate([triple[n][...] for triple in triples], axis=1) for n in range(3)
         ]
+        joined_inputs = [jnp.concatenate([ref[...] for ref in refs_of], axis=0) for refs_of in x_refs]
         at = pl.ds(there, part)
         hidden_grad = started_ref[...] + dot(dn_weight[0, :, at], theirs, 1, 1)
-        row_grads = jnp.concatenate(
-            [(hidden_grad * factor).astype(jnp.bfloat16) for factor in (by_gate, by_up)], axis=0
-        )
-        for which, place in enumerate((here, there)):
-            inputs = jnp.concatenate([ref[...] for ref in x_refs[which]], axis=0)
-            grad = dot(row_grads, inputs, 1, 0)
-            at = pl.ds(place, part)
-            for i in range(pair):
-                gu_new[i, which] = (
-                    gu_ref[0, i, :, at] - gu_slope[0, i, :, at] * grad[i * hid : (i + 1) * hid]
-                )
-                send(gu_new.at[i, which], gu_out.at[0, i, :, at])
-        at = pl.ds(there, part)
         dn_new[...] = dn_ref[0, :, at] - dn_slope[0, :, at] * dot(hidden, theirs, 1, 0)
         send(dn_new, dn_out.at[0, :, at])
+        for i, factor in enumerate((by_gate, by_up)):
+            row_grad = (hidden_grad * factor).astype(jnp.bfloat16)
+            for which, place in enumerate((here, there)):
+                at = pl.ds(place, part)
+                grad = dot(row_grad, joined_inputs[which], 1, 0)
+                gu_new[i, which] = gu_ref[0, i, :, at] - gu_slope[0, i, :, at] * grad
+                send(gu_new.at[i, which], gu_out.at[0, i, :, at])
         for copy in copies:
             copy.wait()
 
@@ -423,12 +452,10 @@
         crossed.append(shift(tokens, "outer", j))
     gate_fan = part_width * reps
     down_fan = down_latent.shape[1] * reps
-    gu_weight, blocks[0], ids, codes = per_entry(
-        weight_of, [gate_up_latent], [gate_fan], bf16, carried=(tokens, expert_ids.T, gate_codes.T)
-    )
-    blocks[-1], gu_weight, late_down = lax.optimization_barrier(
-        (blocks[-1], gu_weight, down_latent)
-    )
+    blocks[0], ids, codes = fetch([tokens, expert_ids.T, gate_codes.T])
+    fans = [gate_fan, down_fan]
+    late = (blocks[-1], blocks[0], gate_up_latent, down_latent)
+    blocks[-1], blocks[0], *latents = lax.optimization_barrier(late)
 
     def code_of(column):
         expert = ahead(inner, jnp.arange(depth, dtype=jnp.int32), depth) * width + column
@@ -451,7 +478,7 @@
     gate = upright(jnp.pad(gate, ((0, -depth % 8), (0, -gate.shape[1] % 128))))
     gate = gate[: width * tok_rows]
 
-    (dn_weight,) = per_entry(weight_of, [late_down], [down_fan], bf16)
+    *latents, gu_weight, dn_weight = weights_of(latents, fans)
     their_groups, factors, keeps, arrivals = [], [], [], []
     for group in tok_groups:
         theirs = other_rep(group)
@@ -464,10 +491,9 @@
         keeps.append(keep)
     messages = list(pack(keeps, arrivals, depth))
 
-    latents = [gate_up_latent, down_latent]
     messages[0], *latents = lax.optimization_barrier((messages[0], *latents))
     picked = over_inner(messages, back)
-    slopes = per_entry(slope_of, latents, [gate_fan, down_fan], f32)
+    slopes = slopes_of(latents, fans)
     picked[-1], *slopes = lax.optimization_barrier((picked[-1], *slopes))
     total, sent = mix(gate, picked, teacher)
     arrivals = [shift(sent, "outer", step) for step in range(1, width)]

time: 46.2 us -> 46 us (level)
  Pallas kernels: 10.4 us -> 8.5 us
  waiting for transfers between devices: 15.2 us -> 16.9 us
    pallas_call x3, Pallas kernels: 5.99 us -> 4.15 us  [the longest x1 2.34 us: weights_of(): pl.pallas_call(body, in_specs=[pl.BlockSpec(memory_space=pltpu.HBM) for _...]
    ppermute x20, waiting for transfers between devices: 15.2 us -> 16.9 us  [shift(): return lax.ppermute(x, axis, [(i, way(i, step, size)) for i in range(size)])]
  transfers between devices with their start and end apart: 20 -> 20, of which waited for: 9 -> 10; matrix products, arithmetic and copies ran while one was open for 2% -> 2% of each run, Pallas kernels for 18% -> 14%
where the time goes in v6:
time: 46 us; the launch traced here: 45.8 us
  starting transfers between devices  18.5 us (40%)
  waiting for transfers between devices  16.9 us (37%)
  Pallas kernels  8.5 us (18%)
  other arithmetic  0.99 us (2%)
  between operations  0.84 us (2%)
    ppermute x20, starting transfers between devices, shift(): return lax.ppermute(x, axis, [(i, way(i, step, size)) for i in range(size)])  18.5 us
    ppermute x20, waiting for transfers between devices, shift(): return lax.ppermute(x, axis, [(i, way(i, step, size)) for i in range(size)])  16.9 us
    pallas_call x1, Pallas kernels, weights_of(): pl.pallas_call(body, in_specs=[pl.BlockSpec(memory_space=pltpu.HBM) for _...  2.34 us
    pallas_call x1, Pallas kernels, backward(): pl.pallas_call(body, in_specs=[pl.BlockSpec(memory_space=pltpu.SMEM)] + [...  1.8 us
    pallas_call x1, Pallas kernels, slopes_of(): pl.pallas_call(body, in_specs=[whole() for _ in latents], out_specs=[whol...  0.99 us
    pallas_call x2, Pallas kernels, forward(): pl.pallas_call(body, in_specs=[pl.BlockSpec(memory_space=pltpu.SMEM)] + [...  0.94 us
  transfers between devices with their start and end apart: 20, of which 10 were waited for; matrix products, arithmetic and copies ran while one was open for 2% of the time, Pallas kernels for 14%

profile of v6, /device:TPU:0, one launch (start us, length us, event | category | flops | bytes accessed | tf_op | source)
XLA Modules:
  0.0 45.8 jit_solution(8146446431025651846)
XLA Ops:
  0.6 3.0 %collective-permute-start.5 = (bf16[32,512]{1,0:T(8,128)(2,1)}, bf16[32,512]{1,0:T(8,128)(2,1)S(1)}, u32[]{:S(2)}, u32[]{:S(2)}) collective-permute-start(bf16[32,512]{1,0:T(8,128)(2,1)} %refs_0_), channel_id=1, source_target_pairs={{0,2},{2,0},{1,3},{3,1},{4,6},{6,4},{5,7},{7,5},{8,10},{10,8},{9,1... | collective-permute-start | bytes 98312 | tf_op jit(solution)/shard_map/ppermute | solution.py:47
  3.7 3.6 %collective-permute-start.2 = (bf16[32,512]{1,0:T(8,128)(2,1)}, bf16[32,512]{1,0:T(8,128)(2,1)S(1)}, u32[]{:S(2)}, u32[]{:S(2)}) collective-permute-start(bf16[32,512]{1,0:T(8,128)(2,1)} %refs_0_), channel_id=1, source_target_pairs={{0,12},{4,8},{8,4},{12,0},{1,13},{5,9},{9,5},{13,1},{2,14},{6,10},... | collective-permute-start | bytes 98312 | tf_op jit(solution)/shard_map/ppermute | solution.py:47
  7.3 0.0 collective-permute-start.1
  7.3 0.8 %collective-permute-start = (bf16[32,512]{1,0:T(8,128)(2,1)}, bf16[32,512]{1,0:T(8,128)(2,1)S(1)}, u32[]{:S(2)}, u32[]{:S(2)}) collective-permute-start(bf16[32,512]{1,0:T(8,128)(2,1)} %refs_0_), channel_id=1, source_target_pairs={{0,4},{4,0},{8,12},{12,8},{1,5},{5,1},{9,13},{13,9},{2,6},{6,2},{1... | collective-permute-start | bytes 98312 | tf_op jit(solution)/shard_map/ppermute | solution.py:47
  8.1 0.8 %fetch.1 = (bf16[32,512]{1,0:T(8,128)(2,1)S(1)}, s32[8,32]{1,0:T(8,128)S(1)}, s32[8,32]{1,0:T(8,128)S(1)}) custom-call(bf16[32,512]{1,0:T(8,128)(2,1)} %refs_0_, s32[8,32]{1,0:T(8,128)} %bitcast.3, s32[8,32]{1,0:T(8,128)} %bitcast.4), custom_call_target="tpu_custom_call" | custom-call | tf_op jit(solution)/shard_map/fetch/pallas_call | solution.py:108
  8.9 0.1 select_reduce_fusion.1
  9.0 0.1 fusion.5
  9.1 0.9 %collective-permute-done.2 = bf16[32,512]{1,0:T(8,128)(2,1)S(1)} collective-permute-done((bf16[32,512]{1,0:T(8,128)(2,1)}, bf16[32,512]{1,0:T(8,128)(2,1)S(1)}, u32[]{:S(2)}, u32[]{:S(2)}) %collective-permute-start.2) | collective-permute-done | bytes 32800 | tf_op jit(solution)/shard_map/ppermute | solution.py:47
  9.9 2.4 %collective-permute-done.1 = bf16[32,512]{1,0:T(8,128)(2,1)S(1)} collective-permute-done((bf16[32,512]{1,0:T(8,128)(2,1)}, bf16[32,512]{1,0:T(8,128)(2,1)S(1)}, u32[]{:S(2)}, u32[]{:S(2)}) %collective-permute-start.1) | collective-permute-done | bytes 32800 | tf_op jit(solution)/shard_map/ppermute | solution.py:47
  12.3 0.0 collective-permute-done
  12.3 0.6 %collective-permute-start.3 = (bf16[104,512]{1,0:T(8,128)(2,1)S(1)}, bf16[104,512]{1,0:T(8,128)(2,1)S(1)}, u32[]{:S(2)}, u32[]{:S(2)}) collective-permute-start(bf16[104,512]{1,0:T(8,128)(2,1)S(1)} %pad_maximum_fusion.1), channel_id=1, source_target_pairs={{0,2},{2,0},{1,3},{3,1},{4,6},{6,4},{5,7},{7,5},{8,10},{10,8},{9,1... | collective-permute-start | bytes 319496 | tf_op jit(solution)/shard_map/ppermute | solution.py:47
  12.9 0.1 collective-permute-start.4
  13.0 2.3 %weights.1 = (f32[1,2,192,1024]{3,2,1,0:T(8,128)S(1)}, f32[1,192,1024]{2,1,0:T(8,128)S(1)}, bf16[1,2,192,1024]{3,2,1,0:T(8,128)(2,1)S(1)}, bf16[1,192,1024]{2,1,0:T(8,128)(2,1)S(1)}) custom-call(f32[1,2,192,1024]{3,2,1,0:T(8,128)} %refs_0_.1, f32[1,192,1024]{2,1,0:T(8,128)} %refs_1_.2), custom_call_target="tpu_custom_call" | custom-call | tf_op jit(solution)/shard_map/weights/pallas_call | solution.py:146
  15.4 0.3 project.2.started_ref
  15.6 1.5 %collective-permute-done.3 = bf16[104,512]{1,0:T(8,128)(2,1)S(1)} collective-permute-done((bf16[104,512]{1,0:T(8,128)(2,1)S(1)}, bf16[104,512]{1,0:T(8,128)(2,1)S(1)}, u32[]{:S(2)}, u32[]{:S(2)}) %collective-permute-start.3) | collective-permute-done | bytes 106528 | tf_op jit(solution)/shard_map/ppermute | solution.py:47
  17.1 0.0 collective-permute-done.5
  17.1 0.1 collective-permute-start.6
  17.2 0.3 project.3.started_ref
  17.5 0.0 collective-permute-done.4.theirs_ref.refs_9_
  17.5 0.5 %forward.2 = (f32[2,192,128]{2,1,0:T(8,128)S(1)}, bf16[192,128]{1,0:T(8,128)(2,1)S(1)}, bf16[128,512]{1,0:T(8,128)(2,1)S(1)}) custom-call(s32[1]{0:T(128)} %bitcast.rep_ref.refs_0_, f32[2,192,128]{2,1,0:T(8,128)S(1)} %project.2.started_ref, bf16[128,512]{1,0:T(8,128)(2,1)S(1)} %collective-permute-done.4.theirs_ref.refs_9_, ...), custom_call_target="tpu_custom_call" | custom-call | tf_op jit(solution)/shard_map/forward/pallas_call | solution.py:209
  18.0 0.6 %collective-permute-start.7 = (bf16[128,512]{1,0:T(8,128)(2,1)S(1)}, bf16[128,512]{1,0:T(8,128)(2,1)S(1)}, u32[]{:S(2)}, u32[]{:S(2)}) collective-permute-start(bf16[128,512]{1,0:T(8,128)(2,1)S(1)} %get-tuple-element.71), channel_id=1, source_target_pairs={{0,1},{1,0},{2,3},{3,2},{4,5},{5,4},{6,7},{7,6},{8,9},{9,8},{10,11... | collective-permute-start | bytes 393224 | tf_op jit(solution)/shard_map/ppermute | solution.py:47
  18.5 0.0 collective-permute-done.6.theirs_ref.refs_10_
  18.5 0.5 %forward.3 = (f32[2,192,128]{2,1,0:T(8,128)S(1)}, bf16[192,128]{1,0:T(8,128)(2,1)S(1)}, bf16[128,512]{1,0:T(8,128)(2,1)S(1)}) custom-call(s32[1]{0:T(128)} %bitcast.rep_ref.refs_0_, f32[2,192,128]{2,1,0:T(8,128)S(1)} %project.3.started_ref, bf16[128,512]{1,0:T(8,128)(2,1)S(1)} %collective-permute-done.6.theirs_ref.refs_10_, ...), custom_call_target="tpu_custom_call" | custom-call | tf_op jit(solution)/shard_map/forward/pallas_call | solution.py:209
  19.0 0.2 collective-permute-start.8
  19.2 0.1 slice_add_fusion
  19.3 0.2 keep_share.2
  19.5 0.2 keep_share.3
  19.7 0.0 collective-permute-done.7.refs_2_
  19.7 0.7 %collective-permute-done.8.refs_3_ = bf16[128,512]{1,0:T(8,128)(2,1)S(1)} collective-permute-done((bf16[128,512]{1,0:T(8,128)(2,1)S(1)}, bf16[128,512]{1,0:T(8,128)(2,1)S(1)}, u32[]{:S(2)}, u32[]{:S(2)}) %collective-permute-start.8) | collective-permute-done | bytes 131104 | tf_op jit(solution)/shard_map/ppermute | solution.py:47
  20.4 0.0 copy-start
  20.5 0.1 collective-permute-start.9
  20.6 2.1 %collective-permute-start.10 = (bf16[64,512]{1,0:T(8,128)(2,1)S(1)}, bf16[64,512]{1,0:T(8,128)(2,1)S(1)}, u32[]{:S(2)}, u32[]{:S(2)}) collective-permute-start(bf16[64,512]{1,0:T(8,128)(2,1)S(1)} %get-tuple-element.78), channel_id=1, source_target_pairs={{0,8},{4,12},{8,0},{12,4},{1,9},{5,13},{9,1},{13,5},{2,10},{6,14},... | collective-permute-start | bytes 196616 | tf_op jit(solution)/shard_map/ppermute | solution.py:47
  22.6 2.3 %collective-permute-start.11 = (bf16[64,512]{1,0:T(8,128)(2,1)S(1)}, bf16[64,512]{1,0:T(8,128)(2,1)S(1)}, u32[]{:S(2)}, u32[]{:S(2)}) collective-permute-start(bf16[64,512]{1,0:T(8,128)(2,1)S(1)} %get-tuple-element.79), channel_id=1, source_target_pairs={{0,12},{4,8},{8,4},{12,0},{1,13},{5,9},{9,5},{13,1},{2,14},{6,10},... | collective-permute-start | bytes 196616 | tf_op jit(solution)/shard_map/ppermute | solution.py:47
  24.9 0.1 maximum_multiply_fusion
  25.0 0.1 upright.1
  25.1 1.0 %slopes.1 = (f32[1,2,192,1024]{3,2,1,0:T(8,128)S(1)}, f32[1,192,1024]{2,1,0:T(8,128)S(1)}) custom-call(f32[1,2,192,1024]{3,2,1,0:T(8,128)S(1)} %get-tuple-element.80.refs_0_.refs_20_, f32[1,192,1024]{2,1,0:T(8,128)S(1)} %get-tuple-element.81.refs_1_.refs_8_.refs_21_), custom_call_target="tpu_custom_call" | custom-call | tf_op jit(solution)/shard_map/slopes/pallas_call | solution.py:165
  26.1 2.8 %collective-permute-done.11.refs_5_ = bf16[64,512]{1,0:T(8,128)(2,1)S(1)} collective-permute-done((bf16[64,512]{1,0:T(8,128)(2,1)S(1)}, bf16[64,512]{1,0:T(8,128)(2,1)S(1)}, u32[]{:S(2)}, u32[]{:S(2)}) %collective-permute-start.11) | collective-permute-done | bytes 65568 | tf_op jit(solution)/shard_map/ppermute | solution.py:47
  29.0 0.0 collective-permute-done.9.refs_3_
  29.0 0.0 collective-permute-done.10.refs_4_
  29.0 0.0 copy-done
  29.0 0.1 mix.1
  29.1 0.6 %collective-permute-start.12 = (bf16[64,512]{1,0:T(8,128)(2,1)S(1)}, bf16[64,512]{1,0:T(8,128)(2,1)S(1)}, u32[]{:S(2)}, u32[]{:S(2)}) collective-permute-start(bf16[64,512]{1,0:T(8,128)(2,1)S(1)} %get-tuple-element.86), channel_id=1, source_target_pairs={{0,2},{2,0},{1,3},{3,1},{4,6},{6,4},{5,7},{7,5},{8,10},{10,8},{9,1... | collective-permute-start | bytes 196616 | tf_op jit(solution)/shard_map/ppermute | solution.py:47
  29.7 3.7 %collective-permute-done.12.refs_3_ = bf16[64,512]{1,0:T(8,128)(2,1)S(1)} collective-permute-done((bf16[64,512]{1,0:T(8,128)(2,1)S(1)}, bf16[64,512]{1,0:T(8,128)(2,1)S(1)}, u32[]{:S(2)}, u32[]{:S(2)}) %collective-permute-start.12) | collective-permute-done | bytes 65568 | tf_op jit(solution)/shard_map/ppermute | solution.py:47
  33.4 0.1 upstream.1
  33.5 1.7 %collective-permute-start.13 = (bf16[64,512]{1,0:T(8,128)(2,1)S(1)}, bf16[64,512]{1,0:T(8,128)(2,1)S(1)}, u32[]{:S(2)}, u32[]{:S(2)}) collective-permute-start(bf16[64,512]{1,0:T(8,128)(2,1)S(1)} %get-tuple-element.88), channel_id=1, source_target_pairs={{0,4},{4,0},{8,12},{12,8},{1,5},{5,1},{9,13},{13,9},{2,6},{6,2},{1... | collective-permute-start | bytes 196616 | tf_op jit(solution)/shard_map/ppermute | solution.py:47
  35.2 1.5 %collective-permute-start.14 = (bf16[64,512]{1,0:T(8,128)(2,1)S(1)}, bf16[64,512]{1,0:T(8,128)(2,1)S(1)}, u32[]{:S(2)}, u32[]{:S(2)}) collective-permute-start(bf16[64,512]{1,0:T(8,128)(2,1)S(1)} %get-tuple-element.89), channel_id=1, source_target_pairs={{0,8},{4,12},{8,0},{12,4},{1,9},{5,13},{9,1},{13,5},{2,10},{6,14},... | collective-permute-start | bytes 196616 | tf_op jit(solution)/shard_map/ppermute | solution.py:47
  36.7 1.3 %collective-permute-start.15 = (bf16[64,512]{1,0:T(8,128)(2,1)S(1)}, bf16[64,512]{1,0:T(8,128)(2,1)S(1)}, u32[]{:S(2)}, u32[]{:S(2)}) collective-permute-start(bf16[64,512]{1,0:T(8,128)(2,1)S(1)} %get-tuple-element.90), channel_id=1, source_target_pairs={{0,12},{4,8},{8,4},{12,0},{1,13},{5,9},{9,5},{13,1},{2,14},{6,10},... | collective-permute-start | bytes 196616 | tf_op jit(solution)/shard_map/ppermute | solution.py:47
  38.0 0.0 collective-permute-start.16
  38.0 0.4 collective-permute-done.13.refs_1_
  38.4 0.1 collective-permute-start.17
  38.5 2.5 %collective-permute-done.14.refs_2_ = bf16[64,512]{1,0:T(8,128)(2,1)S(1)} collective-permute-done((bf16[64,512]{1,0:T(8,128)(2,1)S(1)}, bf16[64,512]{1,0:T(8,128)(2,1)S(1)}, u32[]{:S(2)}, u32[]{:S(2)}) %collective-permute-start.14) | collective-permute-done | bytes 65568 | tf_op jit(solution)/shard_map/ppermute | solution.py:47
  41.0 0.0 collective-permute-start.18
  41.0 1.8 %collective-permute-done.15.refs_3_ = bf16[64,512]{1,0:T(8,128)(2,1)S(1)} collective-permute-done((bf16[64,512]{1,0:T(8,128)(2,1)S(1)}, bf16[64,512]{1,0:T(8,128)(2,1)S(1)}, u32[]{:S(2)}, u32[]{:S(2)}) %collective-permute-start.15) | collective-permute-done | bytes 65568 | tf_op jit(solution)/shard_map/ppermute | solution.py:47
  42.8 0.0 collective-permute-start.19
  42.8 0.6 %add_convert_fusion = bf16[32,512]{1,0:T(8,128)(2,1)} fusion(f32[64,512]{1,0:T(8,128)S(1)} %get-tuple-element.85.refs_2_, bf16[64,512]{1,0:T(8,128)(2,1)S(1)} %collective-permute-done.12.refs_3_), kind=kLoop, calls=%fused_computation.2 | loop fusion | flops 49152 | bytes 131072 | tf_op jit(solution)/shard_map/convert_element_type | solution.py:506
  43.4 0.3 begin.1
  43.7 0.0 collective-permute-done.16.refs_3_
  43.7 0.0 collective-permute-done.17.refs_4_
  43.7 0.0 collective-permute-done.18.refs_5_
  43.8 0.3 collective-permute-done.19.refs_6_
  44.0 1.8 %backward.1 = (f32[1,2,192,1024]{3,2,1,0:T(8,128)}, f32[1,192,1024]{2,1,0:T(8,128)}) custom-call(s32[1]{0:T(128)} %bitcast.rep_ref.refs_0_, f32[192,256]{1,0:T(8,128)S(1)} %get-tuple-element.92.refs_1_, f32[192,512]{1,0:T(8,128)S(1)} %get-tuple-element.93.refs_2_, bf16[64,512]{1,0:T(8,128)(2,1)S(1)} %collective-permute-done.16.refs_3_, ...), custom_call_target="tpu_custom_call" | custom-call | tf_op jit(solution)/shard_map/backward/pallas_call | solution.py:416
  (14 shorter events, 0.1 us)
Async XLA Ops:
  0.6 16.5 %collective-permute-start.5 = (bf16[32,512]{1,0:T(8,128)(2,1)}, bf16[32,512]{1,0:T(8,128)(2,1)S(1)}, u32[]{:S(2)}, u32[]{:S(2)}) collective-permute-start(bf16[32,512]{1,0:T(8,128)(2,1)} %refs_0_), channel_id=1, source_target_pairs={{0,2},{2,0},{1,3},{3,1},{4,6},{6,4},{5,7},{7,5},{8,10},{10,8},{9,1... | collective-permute-start | bytes 98312 | tf_op jit(solution)/shard_map/ppermute | solution.py:47
  3.7 6.3 %collective-permute-start.2 = (bf16[32,512]{1,0:T(8,128)(2,1)}, bf16[32,512]{1,0:T(8,128)(2,1)S(1)}, u32[]{:S(2)}, u32[]{:S(2)}) collective-permute-start(bf16[32,512]{1,0:T(8,128)(2,1)} %refs_0_), channel_id=1, source_target_pairs={{0,12},{4,8},{8,4},{12,0},{1,13},{5,9},{9,5},{13,1},{2,14},{6,10},... | collective-permute-start | bytes 98312 | tf_op jit(solution)/shard_map/ppermute | solution.py:47
  7.3 5.0 %collective-permute-start.1 = (bf16[32,512]{1,0:T(8,128)(2,1)}, bf16[32,512]{1,0:T(8,128)(2,1)S(1)}, u32[]{:S(2)}, u32[]{:S(2)}) collective-permute-start(bf16[32,512]{1,0:T(8,128)(2,1)} %refs_0_), channel_id=1, source_target_pairs={{0,8},{4,12},{8,0},{12,4},{1,9},{5,13},{9,1},{13,5},{2,10},{6,14},... | collective-permute-start | bytes 98312 | tf_op jit(solution)/shard_map/ppermute | solution.py:47
  7.3 5.0 %collective-permute-start = (bf16[32,512]{1,0:T(8,128)(2,1)}, bf16[32,512]{1,0:T(8,128)(2,1)S(1)}, u32[]{:S(2)}, u32[]{:S(2)}) collective-permute-start(bf16[32,512]{1,0:T(8,128)(2,1)} %refs_0_), channel_id=1, source_target_pairs={{0,4},{4,0},{8,12},{12,8},{1,5},{5,1},{9,13},{13,9},{2,6},{6,2},{1... | collective-permute-start | bytes 98312 | tf_op jit(solution)/shard_map/ppermute | solution.py:47
  12.3 4.8 %collective-permute-start.3 = (bf16[104,512]{1,0:T(8,128)(2,1)S(1)}, bf16[104,512]{1,0:T(8,128)(2,1)S(1)}, u32[]{:S(2)}, u32[]{:S(2)}) collective-permute-start(bf16[104,512]{1,0:T(8,128)(2,1)S(1)} %pad_maximum_fusion.1), channel_id=1, source_target_pairs={{0,2},{2,0},{1,3},{3,1},{4,6},{6,4},{5,7},{7,5},{8,10},{10,8},{9,1... | collective-permute-start | bytes 319496 | tf_op jit(solution)/shard_map/ppermute | solution.py:47
  12.9 4.6 %collective-permute-start.4 = (bf16[128,512]{1,0:T(8,128)(2,1)S(1)}, bf16[128,512]{1,0:T(8,128)(2,1)S(1)}, u32[]{:S(2)}, u32[]{:S(2)}) collective-permute-start(bf16[128,512]{1,0:T(8,128)(2,1)S(1)} %constant_dynamic-update-slice_fusion.mine_ref.refs_7_), channel_id=1, source_target_pairs={{0,1},{1,0},{2,3},{3,2},{4,5},{5,4},{6,7},{7,6},{8,9},{9,8},{10,11... | collective-permute-start | bytes 393224 | tf_op jit(solution)/shard_map/ppermute | solution.py:47
  17.1 1.4 %collective-permute-start.6 = (bf16[128,512]{1,0:T(8,128)(2,1)S(1)}, bf16[128,512]{1,0:T(8,128)(2,1)S(1)}, u32[]{:S(2)}, u32[]{:S(2)}) collective-permute-start(bf16[128,512]{1,0:T(8,128)(2,1)S(1)} %pad_maximum_fusion.mine_ref.refs_8_), channel_id=1, source_target_pairs={{0,1},{1,0},{2,3},{3,2},{4,5},{5,4},{6,7},{7,6},{8,9},{9,8},{10,11... | collective-permute-start | bytes 393224 | tf_op jit(solution)/shard_map/ppermute | solution.py:47
  18.0 1.8 %collective-permute-start.7 = (bf16[128,512]{1,0:T(8,128)(2,1)S(1)}, bf16[128,512]{1,0:T(8,128)(2,1)S(1)}, u32[]{:S(2)}, u32[]{:S(2)}) collective-permute-start(bf16[128,512]{1,0:T(8,128)(2,1)S(1)} %get-tuple-element.71), channel_id=1, source_target_pairs={{0,1},{1,0},{2,3},{3,2},{4,5},{5,4},{6,7},{7,6},{8,9},{9,8},{10,11... | collective-permute-start | bytes 393224 | tf_op jit(solution)/shard_map/ppermute | solution.py:47
  19.0 1.4 %collective-permute-start.8 = (bf16[128,512]{1,0:T(8,128)(2,1)S(1)}, bf16[128,512]{1,0:T(8,128)(2,1)S(1)}, u32[]{:S(2)}, u32[]{:S(2)}) collective-permute-start(bf16[128,512]{1,0:T(8,128)(2,1)S(1)} %get-tuple-element.72), channel_id=1, source_target_pairs={{0,1},{1,0},{2,3},{3,2},{4,5},{5,4},{6,7},{7,6},{8,9},{9,8},{10,11... | collective-permute-start | bytes 393224 | tf_op jit(solution)/shard_map/ppermute | solution.py:47
  20.4 8.5 %copy-start = (bf16[32,512]{1,0:T(8,128)(2,1)S(1)}, bf16[32,512]{1,0:T(8,128)(2,1)}, u32[]{:S(2)}) copy-start(bf16[32,512]{1,0:T(8,128)(2,1)} %refs_1_.4) | copy-start | bytes 98308
  20.5 8.5 %collective-permute-start.9 = (bf16[64,512]{1,0:T(8,128)(2,1)S(1)}, bf16[64,512]{1,0:T(8,128)(2,1)S(1)}, u32[]{:S(2)}, u32[]{:S(2)}) collective-permute-start(bf16[64,512]{1,0:T(8,128)(2,1)S(1)} %get-tuple-element.77), channel_id=1, source_target_pairs={{0,4},{4,0},{8,12},{12,8},{1,5},{5,1},{9,13},{13,9},{2,6},{6,2},{1... | collective-permute-start | bytes 196616 | tf_op jit(solution)/shard_map/ppermute | solution.py:47
  20.6 8.4 %collective-permute-start.10 = (bf16[64,512]{1,0:T(8,128)(2,1)S(1)}, bf16[64,512]{1,0:T(8,128)(2,1)S(1)}, u32[]{:S(2)}, u32[]{:S(2)}) collective-permute-start(bf16[64,512]{1,0:T(8,128)(2,1)S(1)} %get-tuple-element.78), channel_id=1, source_target_pairs={{0,8},{4,12},{8,0},{12,4},{1,9},{5,13},{9,1},{13,5},{2,10},{6,14},... | collective-permute-start | bytes 196616 | tf_op jit(solution)/shard_map/ppermute | solution.py:47
  22.6 6.3 %collective-permute-start.11 = (bf16[64,512]{1,0:T(8,128)(2,1)S(1)}, bf16[64,512]{1,0:T(8,128)(2,1)S(1)}, u32[]{:S(2)}, u32[]{:S(2)}) collective-permute-start(bf16[64,512]{1,0:T(8,128)(2,1)S(1)} %get-tuple-element.79), channel_id=1, source_target_pairs={{0,12},{4,8},{8,4},{12,0},{1,13},{5,9},{9,5},{13,1},{2,14},{6,10},... | collective-permute-start | bytes 196616 | tf_op jit(solution)/shard_map/ppermute | solution.py:47
  29.1 4.3 %collective-permute-start.12 = (bf16[64,512]{1,0:T(8,128)(2,1)S(1)}, bf16[64,512]{1,0:T(8,128)(2,1)S(1)}, u32[]{:S(2)}, u32[]{:S(2)}) collective-permute-start(bf16[64,512]{1,0:T(8,128)(2,1)S(1)} %get-tuple-element.86), channel_id=1, source_target_pairs={{0,2},{2,0},{1,3},{3,1},{4,6},{6,4},{5,7},{7,5},{8,10},{10,8},{9,1... | collective-permute-start | bytes 196616 | tf_op jit(solution)/shard_map/ppermute | solution.py:47
  33.5 4.9 %collective-permute-start.13 = (bf16[64,512]{1,0:T(8,128)(2,1)S(1)}, bf16[64,512]{1,0:T(8,128)(2,1)S(1)}, u32[]{:S(2)}, u32[]{:S(2)}) collective-permute-start(bf16[64,512]{1,0:T(8,128)(2,1)S(1)} %get-tuple-element.88), channel_id=1, source_target_pairs={{0,4},{4,0},{8,12},{12,8},{1,5},{5,1},{9,13},{13,9},{2,6},{6,2},{1... | collective-permute-start | bytes 196616 | tf_op jit(solution)/shard_map/ppermute | solution.py:47
  35.2 5.8 %collective-permute-start.14 = (bf16[64,512]{1,0:T(8,128)(2,1)S(1)}, bf16[64,512]{1,0:T(8,128)(2,1)S(1)}, u32[]{:S(2)}, u32[]{:S(2)}) collective-permute-start(bf16[64,512]{1,0:T(8,128)(2,1)S(1)} %get-tuple-element.89), channel_id=1, source_target_pairs={{0,8},{4,12},{8,0},{12,4},{1,9},{5,13},{9,1},{13,5},{2,10},{6,14},... | collective-permute-start | bytes 196616 | tf_op jit(solution)/shard_map/ppermute | solution.py:47
  36.7 6.1 %collective-permute-start.15 = (bf16[64,512]{1,0:T(8,128)(2,1)S(1)}, bf16[64,512]{1,0:T(8,128)(2,1)S(1)}, u32[]{:S(2)}, u32[]{:S(2)}) collective-permute-start(bf16[64,512]{1,0:T(8,128)(2,1)S(1)} %get-tuple-element.90), channel_id=1, source_target_pairs={{0,12},{4,8},{8,4},{12,0},{1,13},{5,9},{9,5},{13,1},{2,14},{6,10},... | collective-permute-start | bytes 196616 | tf_op jit(solution)/shard_map/ppermute | solution.py:47
  38.0 5.7 %collective-permute-start.16 = (bf16[64,512]{1,0:T(8,128)(2,1)S(1)}, bf16[64,512]{1,0:T(8,128)(2,1)S(1)}, u32[]{:S(2)}, u32[]{:S(2)}) collective-permute-start(bf16[64,512]{1,0:T(8,128)(2,1)S(1)} %get-tuple-element.87.refs_0_), channel_id=1, source_target_pairs={{0,1},{1,0},{2,3},{3,2},{4,5},{5,4},{6,7},{7,6},{8,9},{9,8},{10,11... | collective-permute-start | bytes 196616 | tf_op jit(solution)/shard_map/ppermute | solution.py:47
  38.4 5.3 %collective-permute-start.17 = (bf16[64,512]{1,0:T(8,128)(2,1)S(1)}, bf16[64,512]{1,0:T(8,128)(2,1)S(1)}, u32[]{:S(2)}, u32[]{:S(2)}) collective-permute-start(bf16[64,512]{1,0:T(8,128)(2,1)S(1)} %collective-permute-done.13.refs_1_), channel_id=1, source_target_pairs={{0,1},{1,0},{2,3},{3,2},{4,5},{5,4},{6,7},{7,6},{8,9},{9,8},{10,11... | collective-permute-start | bytes 196616 | tf_op jit(solution)/shard_map/ppermute | solution.py:47
  41.0 2.7 %collective-permute-start.18 = (bf16[64,512]{1,0:T(8,128)(2,1)S(1)}, bf16[64,512]{1,0:T(8,128)(2,1)S(1)}, u32[]{:S(2)}, u32[]{:S(2)}) collective-permute-start(bf16[64,512]{1,0:T(8,128)(2,1)S(1)} %collective-permute-done.14.refs_2_), channel_id=1, source_target_pairs={{0,1},{1,0},{2,3},{3,2},{4,5},{5,4},{6,7},{7,6},{8,9},{9,8},{10,11... | collective-permute-start | bytes 196616 | tf_op jit(solution)/shard_map/ppermute | solution.py:47
  42.8 1.3 %collective-permute-start.19 = (bf16[64,512]{1,0:T(8,128)(2,1)S(1)}, bf16[64,512]{1,0:T(8,128)(2,1)S(1)}, u32[]{:S(2)}, u32[]{:S(2)}) collective-permute-start(bf16[64,512]{1,0:T(8,128)(2,1)S(1)} %collective-permute-done.15.refs_3_), channel_id=1, source_target_pairs={{0,1},{1,0},{2,3},{3,2},{4,5},{5,4},{6,7},{7,6},{8,9},{9,8},{10,11... | collective-permute-start | bytes 196616 | tf_op jit(solution)/shard_map/ppermute | solution.py:47

commit v7 on v6

--- a/solution.py
+++ b/solution.py
@@ -135,13 +135,13 @@
     def body(*refs):
         sems = refs[-1]
         copies = []
-        for slot, (n, at) in enumerate(pieces):
-            copy = pltpu.make_async_copy(refs[n].at[at], refs[count + n].at[at], sems.at[slot])
-            copy.start()
-            copies.append(copy)
-        for copy, (n, at) in zip(copies, pieces):
-            copy.wait()
-            refs[2 * count + n][at] = weight_of(refs[count + n][at], fans[n])
+        for n in range(count):
+            copies.append(pltpu.make_async_copy(refs[n], refs[count + n], sems.at[n]))
+            copies[n].start()
+        for n in range(count):
+            copies[n].wait()
+            for at in [at for m, at in pieces if m == n]:
+                refs[2 * count + n][at] = weight_of(refs[count + n][at], fans[n])
 
     return pl.pallas_call(
         body,
@@ -149,7 +149,7 @@
         out_specs=[whole() for _ in range(2 * count)],
         out_shape=[like(latent.shape, latent.dtype) for latent in latents]
         + [like(latent.shape, jnp.bfloat16) for latent in latents],
-        scratch_shapes=[pltpu.SemaphoreType.DMA((len(pieces),))],
+        scratch_shapes=[pltpu.SemaphoreType.DMA((count,))],
         compiler_params=pltpu.CompilerParams(vmem_limit_bytes=4 * MEBI),
         name="weights",
     )(*[pltpu.with_memory_space_constraint(latent, pltpu.HBM) for latent in latents])
@@ -367,7 +367,7 @@
 
 def backward(rep, begun, grads, rows_of, factors, weights, slopes, latents):
     gate_up, down = latents
-    _, pair, hid, _ = gate_up.shape
+    _, pair, hid, wide = gate_up.shape
     width = len(factors)
     depth = len(grads)
     part = grads[0].shape[1]
@@ -408,8 +408,8 @@
             for which, place in enumerate((here, there)):
                 at = pl.ds(place, part)
                 grad = dot(row_grad, joined_inputs[which], 1, 0)
-                gu_new[i, which] = gu_ref[0, i, :, at] - gu_slope[0, i, :, at] * grad
-                send(gu_new.at[i, which], gu_out.at[0, i, :, at])
+                gu_new[i, :, at] = gu_ref[0, i, :, at] - gu_slope[0, i, :, at] * grad
+            send(gu_new.at[i], gu_out.at[0, i])
         for copy in copies:
             copy.wait()
 
@@ -419,7 +419,7 @@
         out_specs=[pl.BlockSpec(memory_space=pl.ANY), pl.BlockSpec(memory_space=pl.ANY)],
         out_shape=[like(gate_up.shape, jnp.float32), like(down.shape, jnp.float32)],
         scratch_shapes=[
-            pltpu.VMEM((pair, 2, hid, part), jnp.float32),
+            pltpu.VMEM((pair, hid, wide), jnp.float32),
             pltpu.VMEM((hid, part), jnp.float32),
             pltpu.SemaphoreType.DMA((2 * pair + 2,)),
         ],

time: 46 us -> 46.1 us (level)
  no operation moved by 1% of the time
where the time goes in v7:
time: 46.1 us; the launch traced here: 45.9 us
  starting transfers between devices  18.5 us (40%)
  waiting for transfers between devices  16.9 us (37%)
  Pallas kernels  8.5 us (18%)
  other arithmetic  0.99 us (2%)
  between operations  0.84 us (2%)
    ppermute x20, starting transfers between devices, shift(): return lax.ppermute(x, axis, [(i, way(i, step, size)) for i in range(size)])  18.5 us
    ppermute x20, waiting for transfers between devices, shift(): return lax.ppermute(x, axis, [(i, way(i, step, size)) for i in range(size)])  16.9 us
    pallas_call x1, Pallas kernels, weights_of(): pl.pallas_call(body, in_specs=[pl.BlockSpec(memory_space=pltpu.HBM) for _...  2.34 us
    pallas_call x1, Pallas kernels, backward(): pl.pallas_call(body, in_specs=[pl.BlockSpec(memory_space=pltpu.SMEM)] + [...  1.81 us
    pallas_call x1, Pallas kernels, slopes_of(): pl.pallas_call(body, in_specs=[whole() for _ in latents], out_specs=[whol...  0.99 us
    pallas_call x2, Pallas kernels, forward(): pl.pallas_call(body, in_specs=[pl.BlockSpec(memory_space=pltpu.SMEM)] + [...  0.94 us
  transfers between devices with their start and end apart: 20, of which 10 were waited for; matrix products, arithmetic and copies ran while one was open for 2% of the time, Pallas kernels for 14%

profile of v7, /device:TPU:0, one launch (start us, length us, event | category | flops | bytes accessed | tf_op | source)
XLA Modules:
  0.0 45.9 jit_solution(3022962368216501337)
XLA Ops:
  0.6 3.0 %collective-permute-start.5 = (bf16[32,512]{1,0:T(8,128)(2,1)}, bf16[32,512]{1,0:T(8,128)(2,1)S(1)}, u32[]{:S(2)}, u32[]{:S(2)}) collective-permute-start(bf16[32,512]{1,0:T(8,128)(2,1)} %refs_0_), channel_id=1, source_target_pairs={{0,2},{2,0},{1,3},{3,1},{4,6},{6,4},{5,7},{7,5},{8,10},{10,8},{9,1... | collective-permute-start | bytes 98312 | tf_op jit(solution)/shard_map/ppermute | solution.py:47
  3.7 3.6 %collective-permute-start.2 = (bf16[32,512]{1,0:T(8,128)(2,1)}, bf16[32,512]{1,0:T(8,128)(2,1)S(1)}, u32[]{:S(2)}, u32[]{:S(2)}) collective-permute-start(bf16[32,512]{1,0:T(8,128)(2,1)} %refs_0_), channel_id=1, source_target_pairs={{0,12},{4,8},{8,4},{12,0},{1,13},{5,9},{9,5},{13,1},{2,14},{6,10},... | collective-permute-start | bytes 98312 | tf_op jit(solution)/shard_map/ppermute | solution.py:47
  7.3 0.0 collective-permute-start.1
  7.3 0.8 %collective-permute-start = (bf16[32,512]{1,0:T(8,128)(2,1)}, bf16[32,512]{1,0:T(8,128)(2,1)S(1)}, u32[]{:S(2)}, u32[]{:S(2)}) collective-permute-start(bf16[32,512]{1,0:T(8,128)(2,1)} %refs_0_), channel_id=1, source_target_pairs={{0,4},{4,0},{8,12},{12,8},{1,5},{5,1},{9,13},{13,9},{2,6},{6,2},{1... | collective-permute-start | bytes 98312 | tf_op jit(solution)/shard_map/ppermute | solution.py:47
  8.1 0.8 %fetch.1 = (bf16[32,512]{1,0:T(8,128)(2,1)S(1)}, s32[8,32]{1,0:T(8,128)S(1)}, s32[8,32]{1,0:T(8,128)S(1)}) custom-call(bf16[32,512]{1,0:T(8,128)(2,1)} %refs_0_, s32[8,32]{1,0:T(8,128)} %bitcast.3, s32[8,32]{1,0:T(8,128)} %bitcast.4), custom_call_target="tpu_custom_call" | custom-call | tf_op jit(solution)/shard_map/fetch/pallas_call | solution.py:108
  8.9 0.1 select_reduce_fusion.1
  9.0 0.1 fusion.5
  9.1 0.9 %collective-permute-done.2 = bf16[32,512]{1,0:T(8,128)(2,1)S(1)} collective-permute-done((bf16[32,512]{1,0:T(8,128)(2,1)}, bf16[32,512]{1,0:T(8,128)(2,1)S(1)}, u32[]{:S(2)}, u32[]{:S(2)}) %collective-permute-start.2) | collective-permute-done | bytes 32800 | tf_op jit(solution)/shard_map/ppermute | solution.py:47
  9.9 2.4 %collective-permute-done.1 = bf16[32,512]{1,0:T(8,128)(2,1)S(1)} collective-permute-done((bf16[32,512]{1,0:T(8,128)(2,1)}, bf16[32,512]{1,0:T(8,128)(2,1)S(1)}, u32[]{:S(2)}, u32[]{:S(2)}) %collective-permute-start.1) | collective-permute-done | bytes 32800 | tf_op jit(solution)/shard_map/ppermute | solution.py:47
  12.3 0.0 collective-permute-done
  12.3 0.6 %collective-permute-start.3 = (bf16[104,512]{1,0:T(8,128)(2,1)S(1)}, bf16[104,512]{1,0:T(8,128)(2,1)S(1)}, u32[]{:S(2)}, u32[]{:S(2)}) collective-permute-start(bf16[104,512]{1,0:T(8,128)(2,1)S(1)} %pad_maximum_fusion.1), channel_id=1, source_target_pairs={{0,2},{2,0},{1,3},{3,1},{4,6},{6,4},{5,7},{7,5},{8,10},{10,8},{9,1... | collective-permute-start | bytes 319496 | tf_op jit(solution)/shard_map/ppermute | solution.py:47
  12.9 0.1 collective-permute-start.4
  13.0 2.3 %weights.1 = (f32[1,2,192,1024]{3,2,1,0:T(8,128)S(1)}, f32[1,192,1024]{2,1,0:T(8,128)S(1)}, bf16[1,2,192,1024]{3,2,1,0:T(8,128)(2,1)S(1)}, bf16[1,192,1024]{2,1,0:T(8,128)(2,1)S(1)}) custom-call(f32[1,2,192,1024]{3,2,1,0:T(8,128)} %refs_0_.1, f32[1,192,1024]{2,1,0:T(8,128)} %refs_1_.2), custom_call_target="tpu_custom_call" | custom-call | tf_op jit(solution)/shard_map/weights/pallas_call | solution.py:146
  15.3 0.3 project.2.started_ref
  15.6 1.5 %collective-permute-done.3 = bf16[104,512]{1,0:T(8,128)(2,1)S(1)} collective-permute-done((bf16[104,512]{1,0:T(8,128)(2,1)S(1)}, bf16[104,512]{1,0:T(8,128)(2,1)S(1)}, u32[]{:S(2)}, u32[]{:S(2)}) %collective-permute-start.3) | collective-permute-done | bytes 106528 | tf_op jit(solution)/shard_map/ppermute | solution.py:47
  17.1 0.0 collective-permute-done.5
  17.1 0.1 collective-permute-start.6
  17.2 0.3 project.3.started_ref
  17.5 0.0 collective-permute-done.4.theirs_ref.refs_9_
  17.5 0.5 %forward.2 = (f32[2,192,128]{2,1,0:T(8,128)S(1)}, bf16[192,128]{1,0:T(8,128)(2,1)S(1)}, bf16[128,512]{1,0:T(8,128)(2,1)S(1)}) custom-call(s32[1]{0:T(128)} %bitcast.rep_ref.refs_0_, f32[2,192,128]{2,1,0:T(8,128)S(1)} %project.2.started_ref, bf16[128,512]{1,0:T(8,128)(2,1)S(1)} %collective-permute-done.4.theirs_ref.refs_9_, ...), custom_call_target="tpu_custom_call" | custom-call | tf_op jit(solution)/shard_map/forward/pallas_call | solution.py:209
  18.0 0.6 %collective-permute-start.7 = (bf16[128,512]{1,0:T(8,128)(2,1)S(1)}, bf16[128,512]{1,0:T(8,128)(2,1)S(1)}, u32[]{:S(2)}, u32[]{:S(2)}) collective-permute-start(bf16[128,512]{1,0:T(8,128)(2,1)S(1)} %get-tuple-element.71), channel_id=1, source_target_pairs={{0,1},{1,0},{2,3},{3,2},{4,5},{5,4},{6,7},{7,6},{8,9},{9,8},{10,11... | collective-permute-start | bytes 393224 | tf_op jit(solution)/shard_map/ppermute | solution.py:47
  18.5 0.0 collective-permute-done.6.theirs_ref.refs_10_
  18.5 0.5 %forward.3 = (f32[2,192,128]{2,1,0:T(8,128)S(1)}, bf16[192,128]{1,0:T(8,128)(2,1)S(1)}, bf16[128,512]{1,0:T(8,128)(2,1)S(1)}) custom-call(s32[1]{0:T(128)} %bitcast.rep_ref.refs_0_, f32[2,192,128]{2,1,0:T(8,128)S(1)} %project.3.started_ref, bf16[128,512]{1,0:T(8,128)(2,1)S(1)} %collective-permute-done.6.theirs_ref.refs_10_, ...), custom_call_target="tpu_custom_call" | custom-call | tf_op jit(solution)/shard_map/forward/pallas_call | solution.py:209
  19.0 0.2 collective-permute-start.8
  19.2 0.1 slice_add_fusion
  19.3 0.2 keep_share.2
  19.5 0.2 keep_share.3
  19.7 0.0 collective-permute-done.7.refs_2_
  19.7 0.7 %collective-permute-done.8.refs_3_ = bf16[128,512]{1,0:T(8,128)(2,1)S(1)} collective-permute-done((bf16[128,512]{1,0:T(8,128)(2,1)S(1)}, bf16[128,512]{1,0:T(8,128)(2,1)S(1)}, u32[]{:S(2)}, u32[]{:S(2)}) %collective-permute-start.8) | collective-permute-done | bytes 131104 | tf_op jit(solution)/shard_map/ppermute | solution.py:47
  20.4 0.0 copy-start
  20.5 0.1 collective-permute-start.9
  20.6 2.1 %collective-permute-start.10 = (bf16[64,512]{1,0:T(8,128)(2,1)S(1)}, bf16[64,512]{1,0:T(8,128)(2,1)S(1)}, u32[]{:S(2)}, u32[]{:S(2)}) collective-permute-start(bf16[64,512]{1,0:T(8,128)(2,1)S(1)} %get-tuple-element.78), channel_id=1, source_target_pairs={{0,8},{4,12},{8,0},{12,4},{1,9},{5,13},{9,1},{13,5},{2,10},{6,14},... | collective-permute-start | bytes 196616 | tf_op jit(solution)/shard_map/ppermute | solution.py:47
  22.6 2.3 %collective-permute-start.11 = (bf16[64,512]{1,0:T(8,128)(2,1)S(1)}, bf16[64,512]{1,0:T(8,128)(2,1)S(1)}, u32[]{:S(2)}, u32[]{:S(2)}) collective-permute-start(bf16[64,512]{1,0:T(8,128)(2,1)S(1)} %get-tuple-element.79), channel_id=1, source_target_pairs={{0,12},{4,8},{8,4},{12,0},{1,13},{5,9},{9,5},{13,1},{2,14},{6,10},... | collective-permute-start | bytes 196616 | tf_op jit(solution)/shard_map/ppermute | solution.py:47
  24.9 0.1 maximum_multiply_fusion
  25.0 0.1 upright.1
  25.1 1.0 %slopes.1 = (f32[1,2,192,1024]{3,2,1,0:T(8,128)S(1)}, f32[1,192,1024]{2,1,0:T(8,128)S(1)}) custom-call(f32[1,2,192,1024]{3,2,1,0:T(8,128)S(1)} %get-tuple-element.80.refs_0_.refs_20_, f32[1,192,1024]{2,1,0:T(8,128)S(1)} %get-tuple-element.81.refs_1_.refs_8_.refs_21_), custom_call_target="tpu_custom_call" | custom-call | tf_op jit(solution)/shard_map/slopes/pallas_call | solution.py:165
  26.1 2.8 %collective-permute-done.11.refs_5_ = bf16[64,512]{1,0:T(8,128)(2,1)S(1)} collective-permute-done((bf16[64,512]{1,0:T(8,128)(2,1)S(1)}, bf16[64,512]{1,0:T(8,128)(2,1)S(1)}, u32[]{:S(2)}, u32[]{:S(2)}) %collective-permute-start.11) | collective-permute-done | bytes 65568 | tf_op jit(solution)/shard_map/ppermute | solution.py:47
  29.0 0.0 collective-permute-done.9.refs_3_
  29.0 0.0 collective-permute-done.10.refs_4_
  29.0 0.0 copy-done
  29.0 0.1 mix.1
  29.1 0.6 %collective-permute-start.12 = (bf16[64,512]{1,0:T(8,128)(2,1)S(1)}, bf16[64,512]{1,0:T(8,128)(2,1)S(1)}, u32[]{:S(2)}, u32[]{:S(2)}) collective-permute-start(bf16[64,512]{1,0:T(8,128)(2,1)S(1)} %get-tuple-element.86), channel_id=1, source_target_pairs={{0,2},{2,0},{1,3},{3,1},{4,6},{6,4},{5,7},{7,5},{8,10},{10,8},{9,1... | collective-permute-start | bytes 196616 | tf_op jit(solution)/shard_map/ppermute | solution.py:47
  29.7 3.7 %collective-permute-done.12.refs_3_ = bf16[64,512]{1,0:T(8,128)(2,1)S(1)} collective-permute-done((bf16[64,512]{1,0:T(8,128)(2,1)S(1)}, bf16[64,512]{1,0:T(8,128)(2,1)S(1)}, u32[]{:S(2)}, u32[]{:S(2)}) %collective-permute-start.12) | collective-permute-done | bytes 65568 | tf_op jit(solution)/shard_map/ppermute | solution.py:47
  33.4 0.1 upstream.1
  33.5 1.7 %collective-permute-start.13 = (bf16[64,512]{1,0:T(8,128)(2,1)S(1)}, bf16[64,512]{1,0:T(8,128)(2,1)S(1)}, u32[]{:S(2)}, u32[]{:S(2)}) collective-permute-start(bf16[64,512]{1,0:T(8,128)(2,1)S(1)} %get-tuple-element.88), channel_id=1, source_target_pairs={{0,4},{4,0},{8,12},{12,8},{1,5},{5,1},{9,13},{13,9},{2,6},{6,2},{1... | collective-permute-start | bytes 196616 | tf_op jit(solution)/shard_map/ppermute | solution.py:47
  35.2 1.5 %collective-permute-start.14 = (bf16[64,512]{1,0:T(8,128)(2,1)S(1)}, bf16[64,512]{1,0:T(8,128)(2,1)S(1)}, u32[]{:S(2)}, u32[]{:S(2)}) collective-permute-start(bf16[64,512]{1,0:T(8,128)(2,1)S(1)} %get-tuple-element.89), channel_id=1, source_target_pairs={{0,8},{4,12},{8,0},{12,4},{1,9},{5,13},{9,1},{13,5},{2,10},{6,14},... | collective-permute-start | bytes 196616 | tf_op jit(solution)/shard_map/ppermute | solution.py:47
  36.7 1.3 %collective-permute-start.15 = (bf16[64,512]{1,0:T(8,128)(2,1)S(1)}, bf16[64,512]{1,0:T(8,128)(2,1)S(1)}, u32[]{:S(2)}, u32[]{:S(2)}) collective-permute-start(bf16[64,512]{1,0:T(8,128)(2,1)S(1)} %get-tuple-element.90), channel_id=1, source_target_pairs={{0,12},{4,8},{8,4},{12,0},{1,13},{5,9},{9,5},{13,1},{2,14},{6,10},... | collective-permute-start | bytes 196616 | tf_op jit(solution)/shard_map/ppermute | solution.py:47
  38.0 0.0 collective-permute-start.16
  38.0 0.4 collective-permute-done.13.refs_1_
  38.4 0.1 collective-permute-start.17
  38.5 2.5 %collective-permute-done.14.refs_2_ = bf16[64,512]{1,0:T(8,128)(2,1)S(1)} collective-permute-done((bf16[64,512]{1,0:T(8,128)(2,1)S(1)}, bf16[64,512]{1,0:T(8,128)(2,1)S(1)}, u32[]{:S(2)}, u32[]{:S(2)}) %collective-permute-start.14) | collective-permute-done | bytes 65568 | tf_op jit(solution)/shard_map/ppermute | solution.py:47
  41.0 0.0 collective-permute-start.18
  41.0 1.8 %collective-permute-done.15.refs_3_ = bf16[64,512]{1,0:T(8,128)(2,1)S(1)} collective-permute-done((bf16[64,512]{1,0:T(8,128)(2,1)S(1)}, bf16[64,512]{1,0:T(8,128)(2,1)S(1)}, u32[]{:S(2)}, u32[]{:S(2)}) %collective-permute-start.15) | collective-permute-done | bytes 65568 | tf_op jit(solution)/shard_map/ppermute | solution.py:47
  42.8 0.0 collective-permute-start.19
  42.8 0.6 %add_convert_fusion = bf16[32,512]{1,0:T(8,128)(2,1)} fusion(f32[64,512]{1,0:T(8,128)S(1)} %get-tuple-element.85.refs_2_, bf16[64,512]{1,0:T(8,128)(2,1)S(1)} %collective-permute-done.12.refs_3_), kind=kLoop, calls=%fused_computation.2 | loop fusion | flops 49152 | bytes 131072 | tf_op jit(solution)/shard_map/convert_element_type | solution.py:506
  43.4 0.3 begin.1
  43.7 0.0 collective-permute-done.16.refs_3_
  43.7 0.0 collective-permute-done.17.refs_4_
  43.7 0.0 collective-permute-done.18.refs_5_
  43.8 0.3 collective-permute-done.19.refs_6_
  44.0 1.8 %backward.1 = (f32[1,2,192,1024]{3,2,1,0:T(8,128)}, f32[1,192,1024]{2,1,0:T(8,128)}) custom-call(s32[1]{0:T(128)} %bitcast.rep_ref.refs_0_, f32[192,256]{1,0:T(8,128)S(1)} %get-tuple-element.92.refs_1_, f32[192,512]{1,0:T(8,128)S(1)} %get-tuple-element.93.refs_2_, bf16[64,512]{1,0:T(8,128)(2,1)S(1)} %collective-permute-done.16.refs_3_, ...), custom_call_target="tpu_custom_call" | custom-call | tf_op jit(solution)/shard_map/backward/pallas_call | solution.py:416
  (14 shorter events, 0.1 us)
Async XLA Ops:
  0.6 16.5 %collective-permute-start.5 = (bf16[32,512]{1,0:T(8,128)(2,1)}, bf16[32,512]{1,0:T(8,128)(2,1)S(1)}, u32[]{:S(2)}, u32[]{:S(2)}) collective-permute-start(bf16[32,512]{1,0:T(8,128)(2,1)} %refs_0_), channel_id=1, source_target_pairs={{0,2},{2,0},{1,3},{3,1},{4,6},{6,4},{5,7},{7,5},{8,10},{10,8},{9,1... | collective-permute-start | bytes 98312 | tf_op jit(solution)/shard_map/ppermute | solution.py:47
  3.7 6.3 %collective-permute-start.2 = (bf16[32,512]{1,0:T(8,128)(2,1)}, bf16[32,512]{1,0:T(8,128)(2,1)S(1)}, u32[]{:S(2)}, u32[]{:S(2)}) collective-permute-start(bf16[32,512]{1,0:T(8,128)(2,1)} %refs_0_), channel_id=1, source_target_pairs={{0,12},{4,8},{8,4},{12,0},{1,13},{5,9},{9,5},{13,1},{2,14},{6,10},... | collective-permute-start | bytes 98312 | tf_op jit(solution)/shard_map/ppermute | solution.py:47
  7.3 5.0 %collective-permute-start.1 = (bf16[32,512]{1,0:T(8,128)(2,1)}, bf16[32,512]{1,0:T(8,128)(2,1)S(1)}, u32[]{:S(2)}, u32[]{:S(2)}) collective-permute-start(bf16[32,512]{1,0:T(8,128)(2,1)} %refs_0_), channel_id=1, source_target_pairs={{0,8},{4,12},{8,0},{12,4},{1,9},{5,13},{9,1},{13,5},{2,10},{6,14},... | collective-permute-start | bytes 98312 | tf_op jit(solution)/shard_map/ppermute | solution.py:47
  7.3 5.0 %collective-permute-start = (bf16[32,512]{1,0:T(8,128)(2,1)}, bf16[32,512]{1,0:T(8,128)(2,1)S(1)}, u32[]{:S(2)}, u32[]{:S(2)}) collective-permute-start(bf16[32,512]{1,0:T(8,128)(2,1)} %refs_0_), channel_id=1, source_target_pairs={{0,4},{4,0},{8,12},{12,8},{1,5},{5,1},{9,13},{13,9},{2,6},{6,2},{1... | collective-permute-start | bytes 98312 | tf_op jit(solution)/shard_map/ppermute | solution.py:47
  12.3 4.8 %collective-permute-start.3 = (bf16[104,512]{1,0:T(8,128)(2,1)S(1)}, bf16[104,512]{1,0:T(8,128)(2,1)S(1)}, u32[]{:S(2)}, u32[]{:S(2)}) collective-permute-start(bf16[104,512]{1,0:T(8,128)(2,1)S(1)} %pad_maximum_fusion.1), channel_id=1, source_target_pairs={{0,2},{2,0},{1,3},{3,1},{4,6},{6,4},{5,7},{7,5},{8,10},{10,8},{9,1... | collective-permute-start | bytes 319496 | tf_op jit(solution)/shard_map/ppermute | solution.py:47
  12.9 4.6 %collective-permute-start.4 = (bf16[128,512]{1,0:T(8,128)(2,1)S(1)}, bf16[128,512]{1,0:T(8,128)(2,1)S(1)}, u32[]{:S(2)}, u32[]{:S(2)}) collective-permute-start(bf16[128,512]{1,0:T(8,128)(2,1)S(1)} %constant_dynamic-update-slice_fusion.mine_ref.refs_7_), channel_id=1, source_target_pairs={{0,1},{1,0},{2,3},{3,2},{4,5},{5,4},{6,7},{7,6},{8,9},{9,8},{10,11... | collective-permute-start | bytes 393224 | tf_op jit(solution)/shard_map/ppermute | solution.py:47
  17.1 1.4 %collective-permute-start.6 = (bf16[128,512]{1,0:T(8,128)(2,1)S(1)}, bf16[128,512]{1,0:T(8,128)(2,1)S(1)}, u32[]{:S(2)}, u32[]{:S(2)}) collective-permute-start(bf16[128,512]{1,0:T(8,128)(2,1)S(1)} %pad_maximum_fusion.mine_ref.refs_8_), channel_id=1, source_target_pairs={{0,1},{1,0},{2,3},{3,2},{4,5},{5,4},{6,7},{7,6},{8,9},{9,8},{10,11... | collective-permute-start | bytes 393224 | tf_op jit(solution)/shard_map/ppermute | solution.py:47
  18.0 1.8 %collective-permute-start.7 = (bf16[128,512]{1,0:T(8,128)(2,1)S(1)}, bf16[128,512]{1,0:T(8,128)(2,1)S(1)}, u32[]{:S(2)}, u32[]{:S(2)}) collective-permute-start(bf16[128,512]{1,0:T(8,128)(2,1)S(1)} %get-tuple-element.71), channel_id=1, source_target_pairs={{0,1},{1,0},{2,3},{3,2},{4,5},{5,4},{6,7},{7,6},{8,9},{9,8},{10,11... | collective-permute-start | bytes 393224 | tf_op jit(solution)/shard_map/ppermute | solution.py:47
  19.0 1.4 %collective-permute-start.8 = (bf16[128,512]{1,0:T(8,128)(2,1)S(1)}, bf16[128,512]{1,0:T(8,128)(2,1)S(1)}, u32[]{:S(2)}, u32[]{:S(2)}) collective-permute-start(bf16[128,512]{1,0:T(8,128)(2,1)S(1)} %get-tuple-element.72), channel_id=1, source_target_pairs={{0,1},{1,0},{2,3},{3,2},{4,5},{5,4},{6,7},{7,6},{8,9},{9,8},{10,11... | collective-permute-start | bytes 393224 | tf_op jit(solution)/shard_map/ppermute | solution.py:47
  20.4 8.5 %copy-start = (bf16[32,512]{1,0:T(8,128)(2,1)S(1)}, bf16[32,512]{1,0:T(8,128)(2,1)}, u32[]{:S(2)}) copy-start(bf16[32,512]{1,0:T(8,128)(2,1)} %refs_1_.4) | copy-start | bytes 98308
  20.5 8.5 %collective-permute-start.9 = (bf16[64,512]{1,0:T(8,128)(2,1)S(1)}, bf16[64,512]{1,0:T(8,128)(2,1)S(1)}, u32[]{:S(2)}, u32[]{:S(2)}) collective-permute-start(bf16[64,512]{1,0:T(8,128)(2,1)S(1)} %get-tuple-element.77), channel_id=1, source_target_pairs={{0,4},{4,0},{8,12},{12,8},{1,5},{5,1},{9,13},{13,9},{2,6},{6,2},{1... | collective-permute-start | bytes 196616 | tf_op jit(solution)/shard_map/ppermute | solution.py:47
  20.6 8.4 %collective-permute-start.10 = (bf16[64,512]{1,0:T(8,128)(2,1)S(1)}, bf16[64,512]{1,0:T(8,128)(2,1)S(1)}, u32[]{:S(2)}, u32[]{:S(2)}) collective-permute-start(bf16[64,512]{1,0:T(8,128)(2,1)S(1)} %get-tuple-element.78), channel_id=1, source_target_pairs={{0,8},{4,12},{8,0},{12,4},{1,9},{5,13},{9,1},{13,5},{2,10},{6,14},... | collective-permute-start | bytes 196616 | tf_op jit(solution)/shard_map/ppermute | solution.py:47
  22.6 6.3 %collective-permute-start.11 = (bf16[64,512]{1,0:T(8,128)(2,1)S(1)}, bf16[64,512]{1,0:T(8,128)(2,1)S(1)}, u32[]{:S(2)}, u32[]{:S(2)}) collective-permute-start(bf16[64,512]{1,0:T(8,128)(2,1)S(1)} %get-tuple-element.79), channel_id=1, source_target_pairs={{0,12},{4,8},{8,4},{12,0},{1,13},{5,9},{9,5},{13,1},{2,14},{6,10},... | collective-permute-start | bytes 196616 | tf_op jit(solution)/shard_map/ppermute | solution.py:47
  29.1 4.3 %collective-permute-start.12 = (bf16[64,512]{1,0:T(8,128)(2,1)S(1)}, bf16[64,512]{1,0:T(8,128)(2,1)S(1)}, u32[]{:S(2)}, u32[]{:S(2)}) collective-permute-start(bf16[64,512]{1,0:T(8,128)(2,1)S(1)} %get-tuple-element.86), channel_id=1, source_target_pairs={{0,2},{2,0},{1,3},{3,1},{4,6},{6,4},{5,7},{7,5},{8,10},{10,8},{9,1... | collective-permute-start | bytes 196616 | tf_op jit(solution)/shard_map/ppermute | solution.py:47
  33.5 4.9 %collective-permute-start.13 = (bf16[64,512]{1,0:T(8,128)(2,1)S(1)}, bf16[64,512]{1,0:T(8,128)(2,1)S(1)}, u32[]{:S(2)}, u32[]{:S(2)}) collective-permute-start(bf16[64,512]{1,0:T(8,128)(2,1)S(1)} %get-tuple-element.88), channel_id=1, source_target_pairs={{0,4},{4,0},{8,12},{12,8},{1,5},{5,1},{9,13},{13,9},{2,6},{6,2},{1... | collective-permute-start | bytes 196616 | tf_op jit(solution)/shard_map/ppermute | solution.py:47
  35.2 5.8 %collective-permute-start.14 = (bf16[64,512]{1,0:T(8,128)(2,1)S(1)}, bf16[64,512]{1,0:T(8,128)(2,1)S(1)}, u32[]{:S(2)}, u32[]{:S(2)}) collective-permute-start(bf16[64,512]{1,0:T(8,128)(2,1)S(1)} %get-tuple-element.89), channel_id=1, source_target_pairs={{0,8},{4,12},{8,0},{12,4},{1,9},{5,13},{9,1},{13,5},{2,10},{6,14},... | collective-permute-start | bytes 196616 | tf_op jit(solution)/shard_map/ppermute | solution.py:47
  36.7 6.1 %collective-permute-start.15 = (bf16[64,512]{1,0:T(8,128)(2,1)S(1)}, bf16[64,512]{1,0:T(8,128)(2,1)S(1)}, u32[]{:S(2)}, u32[]{:S(2)}) collective-permute-start(bf16[64,512]{1,0:T(8,128)(2,1)S(1)} %get-tuple-element.90), channel_id=1, source_target_pairs={{0,12},{4,8},{8,4},{12,0},{1,13},{5,9},{9,5},{13,1},{2,14},{6,10},... | collective-permute-start | bytes 196616 | tf_op jit(solution)/shard_map/ppermute | solution.py:47
  38.0 5.7 %collective-permute-start.16 = (bf16[64,512]{1,0:T(8,128)(2,1)S(1)}, bf16[64,512]{1,0:T(8,128)(2,1)S(1)}, u32[]{:S(2)}, u32[]{:S(2)}) collective-permute-start(bf16[64,512]{1,0:T(8,128)(2,1)S(1)} %get-tuple-element.87.refs_0_), channel_id=1, source_target_pairs={{0,1},{1,0},{2,3},{3,2},{4,5},{5,4},{6,7},{7,6},{8,9},{9,8},{10,11... | collective-permute-start | bytes 196616 | tf_op jit(solution)/shard_map/ppermute | solution.py:47
  38.4 5.3 %collective-permute-start.17 = (bf16[64,512]{1,0:T(8,128)(2,1)S(1)}, bf16[64,512]{1,0:T(8,128)(2,1)S(1)}, u32[]{:S(2)}, u32[]{:S(2)}) collective-permute-start(bf16[64,512]{1,0:T(8,128)(2,1)S(1)} %collective-permute-done.13.refs_1_), channel_id=1, source_target_pairs={{0,1},{1,0},{2,3},{3,2},{4,5},{5,4},{6,7},{7,6},{8,9},{9,8},{10,11... | collective-permute-start | bytes 196616 | tf_op jit(solution)/shard_map/ppermute | solution.py:47
  41.0 2.7 %collective-permute-start.18 = (bf16[64,512]{1,0:T(8,128)(2,1)S(1)}, bf16[64,512]{1,0:T(8,128)(2,1)S(1)}, u32[]{:S(2)}, u32[]{:S(2)}) collective-permute-start(bf16[64,512]{1,0:T(8,128)(2,1)S(1)} %collective-permute-done.14.refs_2_), channel_id=1, source_target_pairs={{0,1},{1,0},{2,3},{3,2},{4,5},{5,4},{6,7},{7,6},{8,9},{9,8},{10,11... | collective-permute-start | bytes 196616 | tf_op jit(solution)/shard_map/ppermute | solution.py:47
  42.8 1.3 %collective-permute-start.19 = (bf16[64,512]{1,0:T(8,128)(2,1)S(1)}, bf16[64,512]{1,0:T(8,128)(2,1)S(1)}, u32[]{:S(2)}, u32[]{:S(2)}) collective-permute-start(bf16[64,512]{1,0:T(8,128)(2,1)S(1)} %collective-permute-done.15.refs_3_), channel_id=1, source_target_pairs={{0,1},{1,0},{2,3},{3,2},{4,5},{5,4},{6,7},{7,6},{8,9},{9,8},{10,11... | collective-permute-start | bytes 196616 | tf_op jit(solution)/shard_map/ppermute | solution.py:47

commit v8 on v6

--- a/solution.py
+++ b/solution.py
@@ -119,7 +119,7 @@
 def row_pieces(latents):
     pieces = []
     for n, latent in enumerate(latents):
-        cuts = 2 if latent.shape[-2] % 32 == 0 else 1
+        cuts = 1
         rows = latent.shape[-2] // cuts
         lead = [()]
         for size in latent.shape[:-2]:
@@ -367,7 +367,7 @@
 
 def backward(rep, begun, grads, rows_of, factors, weights, slopes, latents):
     gate_up, down = latents
-    _, pair, hid, _ = gate_up.shape
+    _, pair, hid, wide = gate_up.shape
     width = len(factors)
     depth = len(grads)
     part = grads[0].shape[1]
@@ -408,8 +408,8 @@
             for which, place in enumerate((here, there)):
                 at = pl.ds(place, part)
                 grad = dot(row_grad, joined_inputs[which], 1, 0)
-                gu_new[i, which] = gu_ref[0, i, :, at] - gu_slope[0, i, :, at] * grad
-                send(gu_new.at[i, which], gu_out.at[0, i, :, at])
+                gu_new[i, :, at] = gu_ref[0, i, :, at] - gu_slope[0, i, :, at] * grad
+            send(gu_new.at[i], gu_out.at[0, i])
         for copy in copies:
             copy.wait()
 
@@ -419,7 +419,7 @@
         out_specs=[pl.BlockSpec(memory_space=pl.ANY), pl.BlockSpec(memory_space=pl.ANY)],
         out_shape=[like(gate_up.shape, jnp.float32), like(down.shape, jnp.float32)],
         scratch_shapes=[
-            pltpu.VMEM((pair, 2, hid, part), jnp.float32),
+            pltpu.VMEM((pair, hid, wide), jnp.float32),
             pltpu.VMEM((hid, part), jnp.float32),
             pltpu.SemaphoreType.DMA((2 * pair + 2,)),
         ],

time: 46 us -> 46.1 us (level)
  no operation moved by 1% of the time
where the time goes in v8:
time: 46.1 us; the launch traced here: 45.9 us
  starting transfers between devices  18.5 us (40%)
  waiting for transfers between devices  17.1 us (37%)
  Pallas kernels  8.34 us (18%)
  other arithmetic  0.99 us (2%)
  between operations  0.84 us (2%)
    ppermute x20, starting transfers between devices, shift(): return lax.ppermute(x, axis, [(i, way(i, step, size)) for i in range(size)])  18.5 us
    ppermute x20, waiting for transfers between devices, shift(): return lax.ppermute(x, axis, [(i, way(i, step, size)) for i in range(size)])  17.1 us
    pallas_call x1, Pallas kernels, weights_of(): pl.pallas_call(body, in_specs=[pl.BlockSpec(memory_space=pltpu.HBM) for _...  2.17 us
    pallas_call x1, Pallas kernels, backward(): pl.pallas_call(body, in_specs=[pl.BlockSpec(memory_space=pltpu.SMEM)] + [...  1.81 us
    pallas_call x1, Pallas kernels, slopes_of(): pl.pallas_call(body, in_specs=[whole() for _ in latents], out_specs=[whol...  0.99 us
    pallas_call x2, Pallas kernels, forward(): pl.pallas_call(body, in_specs=[pl.BlockSpec(memory_space=pltpu.SMEM)] + [...  0.94 us
  transfers between devices with their start and end apart: 20, of which 10 were waited for; matrix products, arithmetic and copies ran while one was open for 2% of the time, Pallas kernels for 14%

profile of v8, /device:TPU:0, one launch (start us, length us, event | category | flops | bytes accessed | tf_op | source)
XLA Modules:
  0.0 45.9 jit_solution(627005259083587488)
XLA Ops:
  0.6 3.0 %collective-permute-start.5 = (bf16[32,512]{1,0:T(8,128)(2,1)}, bf16[32,512]{1,0:T(8,128)(2,1)S(1)}, u32[]{:S(2)}, u32[]{:S(2)}) collective-permute-start(bf16[32,512]{1,0:T(8,128)(2,1)} %refs_0_), channel_id=1, source_target_pairs={{0,2},{2,0},{1,3},{3,1},{4,6},{6,4},{5,7},{7,5},{8,10},{10,8},{9,1... | collective-permute-start | bytes 98312 | tf_op jit(solution)/shard_map/ppermute | solution.py:47
  3.7 3.6 %collective-permute-start.2 = (bf16[32,512]{1,0:T(8,128)(2,1)}, bf16[32,512]{1,0:T(8,128)(2,1)S(1)}, u32[]{:S(2)}, u32[]{:S(2)}) collective-permute-start(bf16[32,512]{1,0:T(8,128)(2,1)} %refs_0_), channel_id=1, source_target_pairs={{0,12},{4,8},{8,4},{12,0},{1,13},{5,9},{9,5},{13,1},{2,14},{6,10},... | collective-permute-start | bytes 98312 | tf_op jit(solution)/shard_map/ppermute | solution.py:47
  7.3 0.0 collective-permute-start.1
  7.3 0.8 %collective-permute-start = (bf16[32,512]{1,0:T(8,128)(2,1)}, bf16[32,512]{1,0:T(8,128)(2,1)S(1)}, u32[]{:S(2)}, u32[]{:S(2)}) collective-permute-start(bf16[32,512]{1,0:T(8,128)(2,1)} %refs_0_), channel_id=1, source_target_pairs={{0,4},{4,0},{8,12},{12,8},{1,5},{5,1},{9,13},{13,9},{2,6},{6,2},{1... | collective-permute-start | bytes 98312 | tf_op jit(solution)/shard_map/ppermute | solution.py:47
  8.1 0.8 %fetch.1 = (bf16[32,512]{1,0:T(8,128)(2,1)S(1)}, s32[8,32]{1,0:T(8,128)S(1)}, s32[8,32]{1,0:T(8,128)S(1)}) custom-call(bf16[32,512]{1,0:T(8,128)(2,1)} %refs_0_, s32[8,32]{1,0:T(8,128)} %bitcast.3, s32[8,32]{1,0:T(8,128)} %bitcast.4), custom_call_target="tpu_custom_call" | custom-call | tf_op jit(solution)/shard_map/fetch/pallas_call | solution.py:108
  8.9 0.1 select_reduce_fusion.1
  9.0 0.1 fusion.5
  9.1 0.9 %collective-permute-done.2 = bf16[32,512]{1,0:T(8,128)(2,1)S(1)} collective-permute-done((bf16[32,512]{1,0:T(8,128)(2,1)}, bf16[32,512]{1,0:T(8,128)(2,1)S(1)}, u32[]{:S(2)}, u32[]{:S(2)}) %collective-permute-start.2) | collective-permute-done | bytes 32800 | tf_op jit(solution)/shard_map/ppermute | solution.py:47
  9.9 2.4 %collective-permute-done.1 = bf16[32,512]{1,0:T(8,128)(2,1)S(1)} collective-permute-done((bf16[32,512]{1,0:T(8,128)(2,1)}, bf16[32,512]{1,0:T(8,128)(2,1)S(1)}, u32[]{:S(2)}, u32[]{:S(2)}) %collective-permute-start.1) | collective-permute-done | bytes 32800 | tf_op jit(solution)/shard_map/ppermute | solution.py:47
  12.3 0.0 collective-permute-done
  12.3 0.6 %collective-permute-start.3 = (bf16[104,512]{1,0:T(8,128)(2,1)S(1)}, bf16[104,512]{1,0:T(8,128)(2,1)S(1)}, u32[]{:S(2)}, u32[]{:S(2)}) collective-permute-start(bf16[104,512]{1,0:T(8,128)(2,1)S(1)} %pad_maximum_fusion.1), channel_id=1, source_target_pairs={{0,2},{2,0},{1,3},{3,1},{4,6},{6,4},{5,7},{7,5},{8,10},{10,8},{9,1... | collective-permute-start | bytes 319496 | tf_op jit(solution)/shard_map/ppermute | solution.py:47
  12.9 0.1 collective-permute-start.4
  13.0 2.2 %weights.1 = (f32[1,2,192,1024]{3,2,1,0:T(8,128)S(1)}, f32[1,192,1024]{2,1,0:T(8,128)S(1)}, bf16[1,2,192,1024]{3,2,1,0:T(8,128)(2,1)S(1)}, bf16[1,192,1024]{2,1,0:T(8,128)(2,1)S(1)}) custom-call(f32[1,2,192,1024]{3,2,1,0:T(8,128)} %refs_0_.1, f32[1,192,1024]{2,1,0:T(8,128)} %refs_1_.2), custom_call_target="tpu_custom_call" | custom-call | tf_op jit(solution)/shard_map/weights/pallas_call | solution.py:146
  15.2 0.3 project.2.started_ref
  15.4 1.6 %collective-permute-done.3 = bf16[104,512]{1,0:T(8,128)(2,1)S(1)} collective-permute-done((bf16[104,512]{1,0:T(8,128)(2,1)S(1)}, bf16[104,512]{1,0:T(8,128)(2,1)S(1)}, u32[]{:S(2)}, u32[]{:S(2)}) %collective-permute-start.3) | collective-permute-done | bytes 106528 | tf_op jit(solution)/shard_map/ppermute | solution.py:47
  17.1 0.0 collective-permute-done.5
  17.1 0.1 collective-permute-start.6
  17.2 0.3 project.3.started_ref
  17.5 0.0 collective-permute-done.4.theirs_ref.refs_9_
  17.5 0.5 %forward.2 = (f32[2,192,128]{2,1,0:T(8,128)S(1)}, bf16[192,128]{1,0:T(8,128)(2,1)S(1)}, bf16[128,512]{1,0:T(8,128)(2,1)S(1)}) custom-call(s32[1]{0:T(128)} %bitcast.rep_ref.refs_0_, f32[2,192,128]{2,1,0:T(8,128)S(1)} %project.2.started_ref, bf16[128,512]{1,0:T(8,128)(2,1)S(1)} %collective-permute-done.4.theirs_ref.refs_9_, ...), custom_call_target="tpu_custom_call" | custom-call | tf_op jit(solution)/shard_map/forward/pallas_call | solution.py:209
  18.0 0.6 %collective-permute-start.7 = (bf16[128,512]{1,0:T(8,128)(2,1)S(1)}, bf16[128,512]{1,0:T(8,128)(2,1)S(1)}, u32[]{:S(2)}, u32[]{:S(2)}) collective-permute-start(bf16[128,512]{1,0:T(8,128)(2,1)S(1)} %get-tuple-element.71), channel_id=1, source_target_pairs={{0,1},{1,0},{2,3},{3,2},{4,5},{5,4},{6,7},{7,6},{8,9},{9,8},{10,11... | collective-permute-start | bytes 393224 | tf_op jit(solution)/shard_map/ppermute | solution.py:47
  18.5 0.0 collective-permute-done.6.theirs_ref.refs_10_
  18.5 0.5 %forward.3 = (f32[2,192,128]{2,1,0:T(8,128)S(1)}, bf16[192,128]{1,0:T(8,128)(2,1)S(1)}, bf16[128,512]{1,0:T(8,128)(2,1)S(1)}) custom-call(s32[1]{0:T(128)} %bitcast.rep_ref.refs_0_, f32[2,192,128]{2,1,0:T(8,128)S(1)} %project.3.started_ref, bf16[128,512]{1,0:T(8,128)(2,1)S(1)} %collective-permute-done.6.theirs_ref.refs_10_, ...), custom_call_target="tpu_custom_call" | custom-call | tf_op jit(solution)/shard_map/forward/pallas_call | solution.py:209
  19.0 0.2 collective-permute-start.8
  19.2 0.1 slice_add_fusion
  19.3 0.2 keep_share.2
  19.5 0.2 keep_share.3
  19.7 0.0 collective-permute-done.7.refs_2_
  19.7 0.7 %collective-permute-done.8.refs_3_ = bf16[128,512]{1,0:T(8,128)(2,1)S(1)} collective-permute-done((bf16[128,512]{1,0:T(8,128)(2,1)S(1)}, bf16[128,512]{1,0:T(8,128)(2,1)S(1)}, u32[]{:S(2)}, u32[]{:S(2)}) %collective-permute-start.8) | collective-permute-done | bytes 131104 | tf_op jit(solution)/shard_map/ppermute | solution.py:47
  20.4 0.0 copy-start
  20.5 0.1 collective-permute-start.9
  20.6 2.1 %collective-permute-start.10 = (bf16[64,512]{1,0:T(8,128)(2,1)S(1)}, bf16[64,512]{1,0:T(8,128)(2,1)S(1)}, u32[]{:S(2)}, u32[]{:S(2)}) collective-permute-start(bf16[64,512]{1,0:T(8,128)(2,1)S(1)} %get-tuple-element.78), channel_id=1, source_target_pairs={{0,8},{4,12},{8,0},{12,4},{1,9},{5,13},{9,1},{13,5},{2,10},{6,14},... | collective-permute-start | bytes 196616 | tf_op jit(solution)/shard_map/ppermute | solution.py:47
  22.6 2.3 %collective-permute-start.11 = (bf16[64,512]{1,0:T(8,128)(2,1)S(1)}, bf16[64,512]{1,0:T(8,128)(2,1)S(1)}, u32[]{:S(2)}, u32[]{:S(2)}) collective-permute-start(bf16[64,512]{1,0:T(8,128)(2,1)S(1)} %get-tuple-element.79), channel_id=1, source_target_pairs={{0,12},{4,8},{8,4},{12,0},{1,13},{5,9},{9,5},{13,1},{2,14},{6,10},... | collective-permute-start | bytes 196616 | tf_op jit(solution)/shard_map/ppermute | solution.py:47
  24.9 0.1 maximum_multiply_fusion
  25.0 0.1 upright.1
  25.1 1.0 %slopes.1 = (f32[1,2,192,1024]{3,2,1,0:T(8,128)S(1)}, f32[1,192,1024]{2,1,0:T(8,128)S(1)}) custom-call(f32[1,2,192,1024]{3,2,1,0:T(8,128)S(1)} %get-tuple-element.80.refs_0_.refs_20_, f32[1,192,1024]{2,1,0:T(8,128)S(1)} %get-tuple-element.81.refs_1_.refs_8_.refs_21_), custom_call_target="tpu_custom_call" | custom-call | tf_op jit(solution)/shard_map/slopes/pallas_call | solution.py:165
  26.1 2.8 %collective-permute-done.11.refs_5_ = bf16[64,512]{1,0:T(8,128)(2,1)S(1)} collective-permute-done((bf16[64,512]{1,0:T(8,128)(2,1)S(1)}, bf16[64,512]{1,0:T(8,128)(2,1)S(1)}, u32[]{:S(2)}, u32[]{:S(2)}) %collective-permute-start.11) | collective-permute-done | bytes 65568 | tf_op jit(solution)/shard_map/ppermute | solution.py:47
  29.0 0.0 collective-permute-done.9.refs_3_
  29.0 0.0 collective-permute-done.10.refs_4_
  29.0 0.0 copy-done
  29.0 0.1 mix.1
  29.1 0.6 %collective-permute-start.12 = (bf16[64,512]{1,0:T(8,128)(2,1)S(1)}, bf16[64,512]{1,0:T(8,128)(2,1)S(1)}, u32[]{:S(2)}, u32[]{:S(2)}) collective-permute-start(bf16[64,512]{1,0:T(8,128)(2,1)S(1)} %get-tuple-element.86), channel_id=1, source_target_pairs={{0,2},{2,0},{1,3},{3,1},{4,6},{6,4},{5,7},{7,5},{8,10},{10,8},{9,1... | collective-permute-start | bytes 196616 | tf_op jit(solution)/shard_map/ppermute | solution.py:47
  29.7 3.7 %collective-permute-done.12.refs_3_ = bf16[64,512]{1,0:T(8,128)(2,1)S(1)} collective-permute-done((bf16[64,512]{1,0:T(8,128)(2,1)S(1)}, bf16[64,512]{1,0:T(8,128)(2,1)S(1)}, u32[]{:S(2)}, u32[]{:S(2)}) %collective-permute-start.12) | collective-permute-done | bytes 65568 | tf_op jit(solution)/shard_map/ppermute | solution.py:47
  33.4 0.1 upstream.1
  33.5 1.7 %collective-permute-start.13 = (bf16[64,512]{1,0:T(8,128)(2,1)S(1)}, bf16[64,512]{1,0:T(8,128)(2,1)S(1)}, u32[]{:S(2)}, u32[]{:S(2)}) collective-permute-start(bf16[64,512]{1,0:T(8,128)(2,1)S(1)} %get-tuple-element.88), channel_id=1, source_target_pairs={{0,4},{4,0},{8,12},{12,8},{1,5},{5,1},{9,13},{13,9},{2,6},{6,2},{1... | collective-permute-start | bytes 196616 | tf_op jit(solution)/shard_map/ppermute | solution.py:47
  35.2 1.5 %collective-permute-start.14 = (bf16[64,512]{1,0:T(8,128)(2,1)S(1)}, bf16[64,512]{1,0:T(8,128)(2,1)S(1)}, u32[]{:S(2)}, u32[]{:S(2)}) collective-permute-start(bf16[64,512]{1,0:T(8,128)(2,1)S(1)} %get-tuple-element.89), channel_id=1, source_target_pairs={{0,8},{4,12},{8,0},{12,4},{1,9},{5,13},{9,1},{13,5},{2,10},{6,14},... | collective-permute-start | bytes 196616 | tf_op jit(solution)/shard_map/ppermute | solution.py:47
  36.7 1.3 %collective-permute-start.15 = (bf16[64,512]{1,0:T(8,128)(2,1)S(1)}, bf16[64,512]{1,0:T(8,128)(2,1)S(1)}, u32[]{:S(2)}, u32[]{:S(2)}) collective-permute-start(bf16[64,512]{1,0:T(8,128)(2,1)S(1)} %get-tuple-element.90), channel_id=1, source_target_pairs={{0,12},{4,8},{8,4},{12,0},{1,13},{5,9},{9,5},{13,1},{2,14},{6,10},... | collective-permute-start | bytes 196616 | tf_op jit(solution)/shard_map/ppermute | solution.py:47
  38.0 0.0 collective-permute-start.16
  38.0 0.4 collective-permute-done.13.refs_1_
  38.4 0.1 collective-permute-start.17
  38.5 2.5 %collective-permute-done.14.refs_2_ = bf16[64,512]{1,0:T(8,128)(2,1)S(1)} collective-permute-done((bf16[64,512]{1,0:T(8,128)(2,1)S(1)}, bf16[64,512]{1,0:T(8,128)(2,1)S(1)}, u32[]{:S(2)}, u32[]{:S(2)}) %collective-permute-start.14) | collective-permute-done | bytes 65568 | tf_op jit(solution)/shard_map/ppermute | solution.py:47
  41.0 0.0 collective-permute-start.18
  41.0 1.8 %collective-permute-done.15.refs_3_ = bf16[64,512]{1,0:T(8,128)(2,1)S(1)} collective-permute-done((bf16[64,512]{1,0:T(8,128)(2,1)S(1)}, bf16[64,512]{1,0:T(8,128)(2,1)S(1)}, u32[]{:S(2)}, u32[]{:S(2)}) %collective-permute-start.15) | collective-permute-done | bytes 65568 | tf_op jit(solution)/shard_map/ppermute | solution.py:47
  42.8 0.0 collective-permute-start.19
  42.8 0.6 %add_convert_fusion = bf16[32,512]{1,0:T(8,128)(2,1)} fusion(f32[64,512]{1,0:T(8,128)S(1)} %get-tuple-element.85.refs_2_, bf16[64,512]{1,0:T(8,128)(2,1)S(1)} %collective-permute-done.12.refs_3_), kind=kLoop, calls=%fused_computation.2 | loop fusion | flops 49152 | bytes 131072 | tf_op jit(solution)/shard_map/convert_element_type | solution.py:506
  43.4 0.3 begin.1
  43.7 0.0 collective-permute-done.16.refs_3_
  43.7 0.0 collective-permute-done.17.refs_4_
  43.7 0.0 collective-permute-done.18.refs_5_
  43.8 0.3 collective-permute-done.19.refs_6_
  44.0 1.8 %backward.1 = (f32[1,2,192,1024]{3,2,1,0:T(8,128)}, f32[1,192,1024]{2,1,0:T(8,128)}) custom-call(s32[1]{0:T(128)} %bitcast.rep_ref.refs_0_, f32[192,256]{1,0:T(8,128)S(1)} %get-tuple-element.92.refs_1_, f32[192,512]{1,0:T(8,128)S(1)} %get-tuple-element.93.refs_2_, bf16[64,512]{1,0:T(8,128)(2,1)S(1)} %collective-permute-done.16.refs_3_, ...), custom_call_target="tpu_custom_call" | custom-call | tf_op jit(solution)/shard_map/backward/pallas_call | solution.py:416
  (14 shorter events, 0.1 us)
Async XLA Ops:
  0.6 16.5 %collective-permute-start.5 = (bf16[32,512]{1,0:T(8,128)(2,1)}, bf16[32,512]{1,0:T(8,128)(2,1)S(1)}, u32[]{:S(2)}, u32[]{:S(2)}) collective-permute-start(bf16[32,512]{1,0:T(8,128)(2,1)} %refs_0_), channel_id=1, source_target_pairs={{0,2},{2,0},{1,3},{3,1},{4,6},{6,4},{5,7},{7,5},{8,10},{10,8},{9,1... | collective-permute-start | bytes 98312 | tf_op jit(solution)/shard_map/ppermute | solution.py:47
  3.7 6.3 %collective-permute-start.2 = (bf16[32,512]{1,0:T(8,128)(2,1)}, bf16[32,512]{1,0:T(8,128)(2,1)S(1)}, u32[]{:S(2)}, u32[]{:S(2)}) collective-permute-start(bf16[32,512]{1,0:T(8,128)(2,1)} %refs_0_), channel_id=1, source_target_pairs={{0,12},{4,8},{8,4},{12,0},{1,13},{5,9},{9,5},{13,1},{2,14},{6,10},... | collective-permute-start | bytes 98312 | tf_op jit(solution)/shard_map/ppermute | solution.py:47
  7.3 5.0 %collective-permute-start.1 = (bf16[32,512]{1,0:T(8,128)(2,1)}, bf16[32,512]{1,0:T(8,128)(2,1)S(1)}, u32[]{:S(2)}, u32[]{:S(2)}) collective-permute-start(bf16[32,512]{1,0:T(8,128)(2,1)} %refs_0_), channel_id=1, source_target_pairs={{0,8},{4,12},{8,0},{12,4},{1,9},{5,13},{9,1},{13,5},{2,10},{6,14},... | collective-permute-start | bytes 98312 | tf_op jit(solution)/shard_map/ppermute | solution.py:47
  7.3 5.0 %collective-permute-start = (bf16[32,512]{1,0:T(8,128)(2,1)}, bf16[32,512]{1,0:T(8,128)(2,1)S(1)}, u32[]{:S(2)}, u32[]{:S(2)}) collective-permute-start(bf16[32,512]{1,0:T(8,128)(2,1)} %refs_0_), channel_id=1, source_target_pairs={{0,4},{4,0},{8,12},{12,8},{1,5},{5,1},{9,13},{13,9},{2,6},{6,2},{1... | collective-permute-start | bytes 98312 | tf_op jit(solution)/shard_map/ppermute | solution.py:47
  12.3 4.8 %collective-permute-start.3 = (bf16[104,512]{1,0:T(8,128)(2,1)S(1)}, bf16[104,512]{1,0:T(8,128)(2,1)S(1)}, u32[]{:S(2)}, u32[]{:S(2)}) collective-permute-start(bf16[104,512]{1,0:T(8,128)(2,1)S(1)} %pad_maximum_fusion.1), channel_id=1, source_target_pairs={{0,2},{2,0},{1,3},{3,1},{4,6},{6,4},{5,7},{7,5},{8,10},{10,8},{9,1... | collective-permute-start | bytes 319496 | tf_op jit(solution)/shard_map/ppermute | solution.py:47
  12.9 4.6 %collective-permute-start.4 = (bf16[128,512]{1,0:T(8,128)(2,1)S(1)}, bf16[128,512]{1,0:T(8,128)(2,1)S(1)}, u32[]{:S(2)}, u32[]{:S(2)}) collective-permute-start(bf16[128,512]{1,0:T(8,128)(2,1)S(1)} %constant_dynamic-update-slice_fusion.mine_ref.refs_7_), channel_id=1, source_target_pairs={{0,1},{1,0},{2,3},{3,2},{4,5},{5,4},{6,7},{7,6},{8,9},{9,8},{10,11... | collective-permute-start | bytes 393224 | tf_op jit(solution)/shard_map/ppermute | solution.py:47
  17.1 1.4 %collective-permute-start.6 = (bf16[128,512]{1,0:T(8,128)(2,1)S(1)}, bf16[128,512]{1,0:T(8,128)(2,1)S(1)}, u32[]{:S(2)}, u32[]{:S(2)}) collective-permute-start(bf16[128,512]{1,0:T(8,128)(2,1)S(1)} %pad_maximum_fusion.mine_ref.refs_8_), channel_id=1, source_target_pairs={{0,1},{1,0},{2,3},{3,2},{4,5},{5,4},{6,7},{7,6},{8,9},{9,8},{10,11... | collective-permute-start | bytes 393224 | tf_op jit(solution)/shard_map/ppermute | solution.py:47
  18.0 1.8 %collective-permute-start.7 = (bf16[128,512]{1,0:T(8,128)(2,1)S(1)}, bf16[128,512]{1,0:T(8,128)(2,1)S(1)}, u32[]{:S(2)}, u32[]{:S(2)}) collective-permute-start(bf16[128,512]{1,0:T(8,128)(2,1)S(1)} %get-tuple-element.71), channel_id=1, source_target_pairs={{0,1},{1,0},{2,3},{3,2},{4,5},{5,4},{6,7},{7,6},{8,9},{9,8},{10,11... | collective-permute-start | bytes 393224 | tf_op jit(solution)/shard_map/ppermute | solution.py:47
  19.0 1.4 %collective-permute-start.8 = (bf16[128,512]{1,0:T(8,128)(2,1)S(1)}, bf16[128,512]{1,0:T(8,128)(2,1)S(1)}, u32[]{:S(2)}, u32[]{:S(2)}) collective-permute-start(bf16[128,512]{1,0:T(8,128)(2,1)S(1)} %get-tuple-element.72), channel_id=1, source_target_pairs={{0,1},{1,0},{2,3},{3,2},{4,5},{5,4},{6,7},{7,6},{8,9},{9,8},{10,11... | collective-permute-start | bytes 393224 | tf_op jit(solution)/shard_map/ppermute | solution.py:47
  20.4 8.5 %copy-start = (bf16[32,512]{1,0:T(8,128)(2,1)S(1)}, bf16[32,512]{1,0:T(8,128)(2,1)}, u32[]{:S(2)}) copy-start(bf16[32,512]{1,0:T(8,128)(2,1)} %refs_1_.4) | copy-start | bytes 98308
  20.5 8.5 %collective-permute-start.9 = (bf16[64,512]{1,0:T(8,128)(2,1)S(1)}, bf16[64,512]{1,0:T(8,128)(2,1)S(1)}, u32[]{:S(2)}, u32[]{:S(2)}) collective-permute-start(bf16[64,512]{1,0:T(8,128)(2,1)S(1)} %get-tuple-element.77), channel_id=1, source_target_pairs={{0,4},{4,0},{8,12},{12,8},{1,5},{5,1},{9,13},{13,9},{2,6},{6,2},{1... | collective-permute-start | bytes 196616 | tf_op jit(solution)/shard_map/ppermute | solution.py:47
  20.6 8.4 %collective-permute-start.10 = (bf16[64,512]{1,0:T(8,128)(2,1)S(1)}, bf16[64,512]{1,0:T(8,128)(2,1)S(1)}, u32[]{:S(2)}, u32[]{:S(2)}) collective-permute-start(bf16[64,512]{1,0:T(8,128)(2,1)S(1)} %get-tuple-element.78), channel_id=1, source_target_pairs={{0,8},{4,12},{8,0},{12,4},{1,9},{5,13},{9,1},{13,5},{2,10},{6,14},... | collective-permute-start | bytes 196616 | tf_op jit(solution)/shard_map/ppermute | solution.py:47
  22.6 6.3 %collective-permute-start.11 = (bf16[64,512]{1,0:T(8,128)(2,1)S(1)}, bf16[64,512]{1,0:T(8,128)(2,1)S(1)}, u32[]{:S(2)}, u32[]{:S(2)}) collective-permute-start(bf16[64,512]{1,0:T(8,128)(2,1)S(1)} %get-tuple-element.79), channel_id=1, source_target_pairs={{0,12},{4,8},{8,4},{12,0},{1,13},{5,9},{9,5},{13,1},{2,14},{6,10},... | collective-permute-start | bytes 196616 | tf_op jit(solution)/shard_map/ppermute | solution.py:47
  29.1 4.3 %collective-permute-start.12 = (bf16[64,512]{1,0:T(8,128)(2,1)S(1)}, bf16[64,512]{1,0:T(8,128)(2,1)S(1)}, u32[]{:S(2)}, u32[]{:S(2)}) collective-permute-start(bf16[64,512]{1,0:T(8,128)(2,1)S(1)} %get-tuple-element.86), channel_id=1, source_target_pairs={{0,2},{2,0},{1,3},{3,1},{4,6},{6,4},{5,7},{7,5},{8,10},{10,8},{9,1... | collective-permute-start | bytes 196616 | tf_op jit(solution)/shard_map/ppermute | solution.py:47
  33.5 4.9 %collective-permute-start.13 = (bf16[64,512]{1,0:T(8,128)(2,1)S(1)}, bf16[64,512]{1,0:T(8,128)(2,1)S(1)}, u32[]{:S(2)}, u32[]{:S(2)}) collective-permute-start(bf16[64,512]{1,0:T(8,128)(2,1)S(1)} %get-tuple-element.88), channel_id=1, source_target_pairs={{0,4},{4,0},{8,12},{12,8},{1,5},{5,1},{9,13},{13,9},{2,6},{6,2},{1... | collective-permute-start | bytes 196616 | tf_op jit(solution)/shard_map/ppermute | solution.py:47
  35.2 5.8 %collective-permute-start.14 = (bf16[64,512]{1,0:T(8,128)(2,1)S(1)}, bf16[64,512]{1,0:T(8,128)(2,1)S(1)}, u32[]{:S(2)}, u32[]{:S(2)}) collective-permute-start(bf16[64,512]{1,0:T(8,128)(2,1)S(1)} %get-tuple-element.89), channel_id=1, source_target_pairs={{0,8},{4,12},{8,0},{12,4},{1,9},{5,13},{9,1},{13,5},{2,10},{6,14},... | collective-permute-start | bytes 196616 | tf_op jit(solution)/shard_map/ppermute | solution.py:47
  36.7 6.1 %collective-permute-start.15 = (bf16[64,512]{1,0:T(8,128)(2,1)S(1)}, bf16[64,512]{1,0:T(8,128)(2,1)S(1)}, u32[]{:S(2)}, u32[]{:S(2)}) collective-permute-start(bf16[64,512]{1,0:T(8,128)(2,1)S(1)} %get-tuple-element.90), channel_id=1, source_target_pairs={{0,12},{4,8},{8,4},{12,0},{1,13},{5,9},{9,5},{13,1},{2,14},{6,10},... | collective-permute-start | bytes 196616 | tf_op jit(solution)/shard_map/ppermute | solution.py:47
  38.0 5.7 %collective-permute-start.16 = (bf16[64,512]{1,0:T(8,128)(2,1)S(1)}, bf16[64,512]{1,0:T(8,128)(2,1)S(1)}, u32[]{:S(2)}, u32[]{:S(2)}) collective-permute-start(bf16[64,512]{1,0:T(8,128)(2,1)S(1)} %get-tuple-element.87.refs_0_), channel_id=1, source_target_pairs={{0,1},{1,0},{2,3},{3,2},{4,5},{5,4},{6,7},{7,6},{8,9},{9,8},{10,11... | collective-permute-start | bytes 196616 | tf_op jit(solution)/shard_map/ppermute | solution.py:47
  38.4 5.3 %collective-permute-start.17 = (bf16[64,512]{1,0:T(8,128)(2,1)S(1)}, bf16[64,512]{1,0:T(8,128)(2,1)S(1)}, u32[]{:S(2)}, u32[]{:S(2)}) collective-permute-start(bf16[64,512]{1,0:T(8,128)(2,1)S(1)} %collective-permute-done.13.refs_1_), channel_id=1, source_target_pairs={{0,1},{1,0},{2,3},{3,2},{4,5},{5,4},{6,7},{7,6},{8,9},{9,8},{10,11... | collective-permute-start | bytes 196616 | tf_op jit(solution)/shard_map/ppermute | solution.py:47
  41.0 2.7 %collective-permute-start.18 = (bf16[64,512]{1,0:T(8,128)(2,1)S(1)}, bf16[64,512]{1,0:T(8,128)(2,1)S(1)}, u32[]{:S(2)}, u32[]{:S(2)}) collective-permute-start(bf16[64,512]{1,0:T(8,128)(2,1)S(1)} %collective-permute-done.14.refs_2_), channel_id=1, source_target_pairs={{0,1},{1,0},{2,3},{3,2},{4,5},{5,4},{6,7},{7,6},{8,9},{9,8},{10,11... | collective-permute-start | bytes 196616 | tf_op jit(solution)/shard_map/ppermute | solution.py:47
  42.8 1.3 %collective-permute-start.19 = (bf16[64,512]{1,0:T(8,128)(2,1)S(1)}, bf16[64,512]{1,0:T(8,128)(2,1)S(1)}, u32[]{:S(2)}, u32[]{:S(2)}) collective-permute-start(bf16[64,512]{1,0:T(8,128)(2,1)S(1)} %collective-permute-done.15.refs_3_), channel_id=1, source_target_pairs={{0,1},{1,0},{2,3},{3,2},{4,5},{5,4},{6,7},{7,6},{8,9},{9,8},{10,11... | collective-permute-start | bytes 196616 | tf_op jit(solution)/shard_map/ppermute | solution.py:47
